TPU v7x, 32 devices: a whole 2x2x4 slice. The times are simulated.
32 devices in a mesh: groups: 2 (over y), seq: 16 (over z, x, core).
Axes of the slice: x: 2, y: 2, z: 4, core: 2. Of those that a mesh axis runs over, the one named last changes fastest.
Arguments:
- frames: bfloat16 [64, 32, 128, 128], P(('groups', 'seq')), parts along dimension 0, may hold values from -6 to 6
- w_spatial: bfloat16 [3, 3, 128, 128], replicated, may hold values from -0.1875 to 0.1875
- w_temporal: bfloat16 [2, 3, 128, 128], replicated, may hold values from -0.3125 to 0.3125
- dilations: int32 [2], replicated, may hold values from 1 to 16
- offsets: int32 [2, 3], replicated, may hold values from 0 to 3
- cotangent: bfloat16 [64, 1024, 128], P('groups', 'seq'), parts along dimension 0, may hold values from -0.011962891 to 0.011962891
Outputs:
- features: bfloat16 [64, 1024, 128], P('groups', 'seq'), parts along dimension 0
- grad_spatial: float32 [6, 3, 128, 128], P('groups'), parts along dimension 0
- grad_temporal: float32 [4, 3, 128, 128], P('groups'), parts along dimension 0
There are 2 independent parts, one for each index of `groups`. A program takes and returns all parts, laid end to end along the dimension named above; an argument that names none is the same for every part. Nothing has to cross between parts.
All inputs are finite; a program needn't handle non-finite values.
Results may differ from a plain program's by a relative error of at most 0.0067.
Values may be sent and summed in bfloat16 or wider, within the bound.
No kernel may reach another device: no remote copies, remote signals or barrier semaphores. Data moves between devices by JAX's collectives and lax.ppermute only.
A program may use at most 64 MiB of HBM per device.

v0:
```python
import jax
import jax.numpy as jnp
from jax import lax
from jax.sharding import PartitionSpec as P


def padded_view(frames):
    count, height, width, channels = frames.shape
    padded = jnp.pad(frames, ((0, 0), (1, 1), (1, 1), (0, 0)))
    return padded.reshape(count, height // 2 + 1, 2, width // 2 + 1, 2, channels)


def window(view, row_tap, col_tap):
    out_rows = view.shape[1] - 1
    out_cols = view.shape[3] - 1
    return view[
        :,
        row_tap // 2 : row_tap // 2 + out_rows,
        row_tap % 2,
        col_tap // 2 : col_tap // 2 + out_cols,
        col_tap % 2,
        :,
    ]


def delayed(values, delay):
    length = values.shape[0]
    delay = jnp.minimum(delay, length)
    joined = jnp.concatenate([jnp.zeros_like(values), values], 0)
    return lax.dynamic_slice_in_dim(joined, length - delay, length, 0)


def advanced(values, delay):
    length = values.shape[0]
    delay = jnp.minimum(delay, length)
    joined = jnp.concatenate([values, jnp.zeros_like(values)], 0)
    return lax.dynamic_slice_in_dim(joined, delay, length, 0)


def temporal_forward(start, w_temporal, delays):
    length, pixels, channels = start.shape
    states = [start]
    activations = []
    for layer in range(w_temporal.shape[0]):
        state = states[-1]
        total = jnp.zeros((length * pixels, channels), jnp.float32)
        for tap in range(w_temporal.shape[1]):
            moved = delayed(state, delays[layer, tap]).reshape(-1, channels)
            total = total + jnp.dot(
                moved, w_temporal[layer, tap], preferred_element_type=jnp.float32
            )
        activ = jnp.tanh(total).reshape(length, pixels, channels)
        activations.append(activ)
        states.append((state.astype(jnp.float32) + activ).astype(jnp.bfloat16))
    return (states, activations)


def temporal_backward(states, activations, cotangent, w_temporal, delays):
    length, pixels, channels = cotangent.shape
    layer_count = w_temporal.shape[0]
    grad_state = cotangent.astype(jnp.float32)
    grads = [None] * layer_count
    for layer in reversed(range(layer_count)):
        activ = activations[layer]
        dz_flat = (grad_state * (1.0 - activ * activ)).astype(jnp.bfloat16).reshape(-1, channels)
        layer_grads = []
        for tap in range(w_temporal.shape[1]):
            moved = delayed(states[layer], delays[layer, tap]).reshape(-1, channels)
            layer_grads.append(
                lax.dot_general(
                    moved, dz_flat, (((0,), (0,)), ((), ())), preferred_element_type=jnp.float32
                )
            )
            backward = jnp.dot(
                dz_flat, w_temporal[layer, tap].T, preferred_element_type=jnp.float32
            )
            grad_state = grad_state + advanced(
                backward.reshape(length, pixels, channels), delays[layer, tap]
            )
        grads[layer] = jnp.stack(layer_grads)
    return (grad_state.astype(jnp.bfloat16), jnp.stack(grads))


def local(frames, w_spatial, w_temporal, dilations, offsets, cotangent):
    count, height, width, channels = frames.shape
    map_pixels = height // 2 * (width // 2)
    delays = offsets * dilations[:, None]
    view = padded_view(frames)
    total = jnp.zeros((count * map_pixels, channels), jnp.float32)
    for row_tap in range(3):
        for col_tap in range(3):
            patch = window(view, row_tap, col_tap).reshape(-1, channels)
            total = total + jnp.dot(
                patch, w_spatial[row_tap, col_tap], preferred_element_type=jnp.float32
            )
    spatial = total.astype(jnp.bfloat16).reshape(count, map_pixels, channels)
    gathered = lax.all_to_all(spatial, "seq", split_axis=1, concat_axis=0, tiled=True)
    states, activations = temporal_forward(gathered, w_temporal, delays)
    grad_maps, local_temporal = temporal_backward(
        states, activations, cotangent, w_temporal, delays
    )
    back = lax.all_to_all(grad_maps, "seq", split_axis=0, concat_axis=1, tiled=True)
    back_flat = back.reshape(-1, channels)
    rows = []
    for row_tap in range(3):
        cols = []
        for col_tap in range(3):
            patch = window(view, row_tap, col_tap).reshape(-1, channels)
            cols.append(
                lax.dot_general(
                    patch, back_flat, (((0,), (0,)), ((), ())), preferred_element_type=jnp.float32
                )
            )
        rows.append(jnp.stack(cols))
    local_spatial = jnp.stack(rows)
    grad_spatial, grad_temporal = lax.psum((local_spatial, local_temporal), "seq")
    return (states[-1], grad_spatial, grad_temporal)


def solution(mesh):
    in_specs = (
        P(("groups", "seq"), None, None, None),
        P(),
        P(),
        P(),
        P(),
        P("groups", "seq", None),
    )
    out_specs = (
        P("groups", "seq", None),
        P("groups", None, None, None),
        P("groups", None, None, None),
    )
    return jax.shard_map(local, mesh=mesh, in_specs=in_specs, out_specs=out_specs, check_vma=False)
```

profile of v0, /device:TPU:0, one launch (start us, length us, event | category | flops | bytes accessed | tf_op | source)
XLA Modules:
  0.0 182.1 jit_solution(3432139852399982071)
XLA Ops:
  7.2 3.8 %copy.37 = bf16[2,32,128,128]{3,0,2,1:T(2,128)(2,1)S(1)} copy(bf16[2,32,128,128]{3,2,1,0:T(8,128)(2,1)} %param.6) | data formatting | bytes 4194304
  10.9 1.7 pad.12.clone
  12.7 3.9 %fusion.62 = (bf16[2,16,1,64,1,128]{5,0,4,3,2,1:T(2,128)(2,1)S(1)}, bf16[2,16,1,64,1,128]{5,0,4,3,2,1:T(2,128)(2,1)S(1)}, bf16[2,16,1,64,1,128]{5,0,4,3,2,1:T(2,...) fusion(bf16[2,17,2,65,2,128]{5,0,4,3,2,1:T(2,128)(2,1)S(1)} %bi, ...), kind=kLoop, calls=%fused_computation.113 | loop fusion | bytes 9437184 | tf_op jit(solution)/shard_map/slice | solution.py:16
  17.8 0.7 copy-done.14
  21.1 1.3 copy.34
  22.4 7.5 %all-to-all-start = ((bf16[2,1024,128]{2,0,1:T(2,128)(2,1)}), bf16[2,1024,128]{2,0,1:T(2,128)(2,1)S(1)}, u32[]{:S(2)}, u32[]{:S(2)}) async-start(bf16[2,1024,128]{2,0,1:T(2,128)(2,1)} %copy.34), calls=%async_computation | async-start | bytes 1048576 | tf_op jit(solution)/shard_map/all_to_all | solution.py:97
  30.0 0.7 fusion.63
  34.6 9.8 %all-to-all-done = bf16[2,1024,128]{2,0,1:T(2,128)(2,1)S(1)} async-done(((bf16[2,1024,128]{2,0,1:T(2,128)(2,1)}), bf16[2,1024,128]{2,0,1:T(2,128)(2,1)S(1)}, u32[]{:S(2)}, u32[]{:S(2)}) %all-to-all-start) | async-done | bytes 524320 | tf_op jit(solution)/shard_map/all_to_all | solution.py:97
  44.5 0.8 pad_dynamic-slice_fusion.9
  46.7 0.8 pad_dynamic-slice_fusion.6
  48.4 0.5 copy-done.12
  48.9 1.1 fusion.3
  51.9 0.7 multiply_convert_fusion
  53.5 1.4 fusion.9
  54.8 4.2 %all-to-all-start.1 = ((bf16[32,64,128]{2,1,0:T(8,128)(2,1)}), bf16[32,64,128]{2,1,0:T(8,128)(2,1)}, u32[]{:S(2)}, u32[]{:S(2)}) async-start(bf16[32,64,128]{2,1,0:T(8,128)(2,1)} %fusion.9), calls=%async_computation.1 | async-start | bytes 1048576 | tf_op jit(solution)/shard_map/all_to_all | solution.py:102
  59.2 1.4 convolution_bitcast_fusion.3
  60.6 1.4 convolution_bitcast_fusion.4
  62.3 0.8 pad_maximum_fusion.1
  63.1 10.5 %all-to-all-done.1 = bf16[32,64,128]{2,1,0:T(8,128)(2,1)} async-done(((bf16[32,64,128]{2,1,0:T(8,128)(2,1)}), bf16[32,64,128]{2,1,0:T(8,128)(2,1)}, u32[]{:S(2)}, u32[]{:S(2)}) %all-to-all-start.1) | async-done | bytes 524320 | tf_op jit(solution)/shard_map/all_to_all | solution.py:102
  73.6 1.1 copy.36
  74.7 0.3 convolution_bitcast_fusion.6
  75.1 0.4 convolution_bitcast_fusion.7
  75.4 0.4 convolution_bitcast_fusion.8
  75.8 0.3 convolution_bitcast_fusion.9
  76.5 0.3 convolution_bitcast_fusion.11
  76.9 0.3 convolution_bitcast_fusion.12
  77.3 0.3 convolution_bitcast_fusion.13
  77.6 0.3 convolution_bitcast_fusion.14
  78.0 0.9 pad_maximum_fusion
  78.9 92.7 %all-reduce.12.cloned.1.call-done = (f32[3,3,128,128]{3,2,1,0:T(8,128)}, f32[2,3,128,128]{3,2,1,0:T(8,128)}) async-done(((f32[3,3,128,128]{3,2,1,0:T(8,128)}, f32[2,3,128,128]{3,2,1,0:T(8,128)}), (f32[3,3,128,128]{3,2,1,0:T(8,128)}, f32[2,3,128,128]{3,2,1,0:T(8,128)})) %all-reduce.12.cloned.1.call-update) | async-done | bytes 983056 | tf_op jit(solution)/shard_map/psum | solution.py:116
  171.6 1.9 %copy.40 = f32[3,3,128,128]{3,2,1,0:T(8,128)} copy(f32[3,3,128,128]{3,2,1,0:T(8,128)} %get-tuple-element.33) | data formatting | bytes 1179648
  173.5 1.8 copy.41
  (76 shorter events, 9.6 us)
Async XLA Ops:
  17.1 2.8 %copy-start = (bf16[2,16,1,64,1,128]{5,3,1,0,4,2:T(8,128)(2,1)}, bf16[2,16,1,64,1,128]{5,3,1,0,4,2:T(8,128)(2,1)S(1)}, u32[]{:S(2)}) copy-start(bf16[2,16,1,64,1,128]{5,3,1,0,4,2:T(8,128)(2,1)S(1)} %copy.30) | copy-start | bytes 1572868
  17.2 2.4 %copy-start.2 = (bf16[2,16,1,64,1,128]{5,3,1,0,4,2:T(8,128)(2,1)}, bf16[2,16,1,64,1,128]{5,3,1,0,4,2:T(8,128)(2,1)S(1)}, u32[]{:S(2)}) copy-start(bf16[2,16,1,64,1,128]{5,3,1,0,4,2:T(8,128)(2,1)S(1)} %copy.29) | copy-start | bytes 1572868
  17.2 1.2 copy-start.14
  17.4 1.9 %copy-start.4 = (bf16[2,16,1,64,1,128]{5,3,1,0,4,2:T(8,128)(2,1)}, bf16[2,16,1,64,1,128]{5,3,1,0,4,2:T(8,128)(2,1)S(1)}, u32[]{:S(2)}) copy-start(bf16[2,16,1,64,1,128]{5,3,1,0,4,2:T(8,128)(2,1)S(1)} %copy.28) | copy-start | bytes 1572868
  17.5 1.5 copy-start.6
  17.6 1.4 copy-start.8
  20.7 9.2 %copy-start.15 = (s32[2,3]{1,0:T(2,128)S(1)}, s32[2,3]{1,0:T(2,128)}, u32[]{:S(2)}) copy-start(s32[2,3]{1,0:T(2,128)} %param.10) | copy-start | bytes 76
  20.8 9.1 %copy-start.16 = (s32[2]{0:T(128)S(1)}, s32[2]{0:T(128)}, u32[]{:S(2)}) copy-start(s32[2]{0:T(128)} %param.9) | copy-start | bytes 28
  22.4 22.9 %copy-start.13 = (bf16[2,3,128,128]{3,2,1,0:T(8,128)(2,1)S(1)}, bf16[2,3,128,128]{3,2,1,0:T(8,128)(2,1)}, u32[]{:S(2)}) copy-start(bf16[2,3,128,128]{3,2,1,0:T(8,128)(2,1)} %param.8) | copy-start | bytes 589828
  22.4 22.0 %all-to-all-start = ((bf16[2,1024,128]{2,0,1:T(2,128)(2,1)}), bf16[2,1024,128]{2,0,1:T(2,128)(2,1)S(1)}, u32[]{:S(2)}, u32[]{:S(2)}) async-start(bf16[2,1024,128]{2,0,1:T(2,128)(2,1)} %copy.34), calls=%async_computation | async-start | bytes 1048576 | tf_op jit(solution)/shard_map/all_to_all | solution.py:97
  45.3 0.8 copy-start.10
  45.3 1.0 copy-start.11
  47.8 1.0 copy-start.12
  54.8 18.7 %all-to-all-start.1 = ((bf16[32,64,128]{2,1,0:T(8,128)(2,1)}), bf16[32,64,128]{2,1,0:T(8,128)(2,1)}, u32[]{:S(2)}, u32[]{:S(2)}) async-start(bf16[32,64,128]{2,1,0:T(8,128)(2,1)} %fusion.9), calls=%async_computation.1 | async-start | bytes 1048576 | tf_op jit(solution)/shard_map/all_to_all | solution.py:102
  59.1 112.5 %all-reduce.12.cloned.1.call-start = ((), (), s32[]{:S(2)}) async-start(), calls=%async_computation.2 | async-start | bytes 1966080 | tf_op jit(solution)/shard_map/psum | solution.py:116
  73.6 2.2 %copy-start.1 = (bf16[2,16,1,64,1,128]{5,3,1,0,4,2:T(8,128)(2,1)S(1)}, bf16[2,16,1,64,1,128]{5,3,1,0,4,2:T(8,128)(2,1)}, u32[]{:S(2)}) copy-start(bf16[2,16,1,64,1,128]{5,3,1,0,4,2:T(8,128)(2,1)} %copy-done) | copy-start | bytes 1572868
  74.7 1.5 copy-start.3
  75.1 1.5 copy-start.5
  75.4 1.4 copy-start.7
  75.8 1.4 copy-start.9
Sparse Core Ops, SparseCore 0:
  79.0 92.4 all-reduce.11
where the time goes:
time: 183 us; the launch traced here: 182 us
  waiting for transfers between devices  113 us (62%)
  local copies, waits for them, and re-layouts  20.5 us (11%)
  between operations  18.5 us (10%)
  matrix products  13.2 us (7%)
  starting transfers between devices  11.8 us (6%)
  other arithmetic  5.13 us (3%)
    psum x1, waiting for transfers between devices, local(): lax.psum((local_spatial, local_temporal), 'seq')  92.7 us
    all_to_all x1, waiting for transfers between devices, local(): lax.all_to_all(grad_maps, 'seq', split_axis=0, concat_axis=1, tiled=True)  10.5 us
    all_to_all x1, waiting for transfers between devices, local(): lax.all_to_all(spatial, 'seq', split_axis=1, concat_axis=0, tiled=True)  9.76 us
    unnamed x37, local copies, waits for them, and re-layouts  8.99 us
    all_to_all x1, starting transfers between devices, local(): lax.all_to_all(spatial, 'seq', split_axis=1, concat_axis=0, tiled=True)  7.5 us
    slice x10, local copies, waits for them, and re-layouts, window(): view[:, row_tap // 2:row_tap // 2 + out_rows, row_tap % 2, col_tap // 2:c...  4.93 us
    all_to_all x1, starting transfers between devices, local(): lax.all_to_all(grad_maps, 'seq', split_axis=0, concat_axis=1, tiled=True)  4.24 us
    dot_general x6, matrix products, temporal_backward(): lax.dot_general(moved, dz_flat, (((0,), (0,)), ((), ())), preferred_eleme...  4.12 us
  transfers between devices with their start and end apart: 3, of which 3 were waited for; matrix products, arithmetic and copies ran while one was open for 3% of the time, Pallas kernels for 0%

commit v1 on v0

v1 whole, which is shorter than its diff:
```python
import functools

import jax
import jax.numpy as jnp
from jax import lax
from jax.experimental import pallas as pl
from jax.experimental.pallas import tpu as pltpu
from jax.sharding import PartitionSpec as P

VMEM_LIMIT = 56 * 1024 * 1024


def conv_kernel(x_ref, w_ref, out_ref, planes_ref):
    height, width, channels = x_ref.shape[1:]
    out_rows, out_cols = height // 2, width // 2
    chunks, chunk_pixels = out_ref.shape[0], out_ref.shape[2]
    tap = lax.broadcasted_iota(jnp.int32, (3 * out_cols, width), 0)
    col = lax.broadcasted_iota(jnp.int32, (3 * out_cols, width), 1)
    wanted = 2 * lax.rem(tap, out_cols) + lax.div(tap, out_cols) - 1
    pick = jnp.where(col == wanted, 1.0, 0.0).astype(jnp.bfloat16)
    zero = jnp.zeros((out_cols, channels), jnp.bfloat16)
    for col_tap in range(3):
        planes_ref[col_tap, 0, 0] = zero
    for row in range(height):
        picked = jnp.dot(pick, x_ref[0, row], preferred_element_type=jnp.float32)
        picked = picked.astype(jnp.bfloat16)
        for col_tap in range(3):
            planes_ref[col_tap, 0, row + 1] = picked[
                col_tap * out_cols : (col_tap + 1) * out_cols
            ]
    weights = w_ref[...].reshape(9 * channels, channels)
    step = 4
    for first in range(0, out_rows, step):
        parts = []
        for row_tap in range(3):
            for col_tap in range(3):
                parts.append(
                    jnp.concatenate(
                        [
                            planes_ref[col_tap, 0, 2 * row + row_tap]
                            for row in range(first, first + step)
                        ],
                        0,
                    )
                )
        total = jnp.dot(
            jnp.concatenate(parts, 1), weights, preferred_element_type=jnp.float32
        ).astype(jnp.bfloat16)
        count = step * out_cols // chunk_pixels
        out_ref[pl.ds(first * out_cols // chunk_pixels, count), 0] = total.reshape(
            count, chunk_pixels, channels
        )


def conv(frames, w_spatial, n):
    count, height, width, channels = frames.shape
    out_rows, out_cols = height // 2, width // 2
    pixels = out_rows * out_cols
    return pl.pallas_call(
        conv_kernel,
        grid=(count,),
        in_specs=[
            pl.BlockSpec((1, height, width, channels), lambda f: (f, 0, 0, 0)),
            pl.BlockSpec((3, 3, channels, channels), lambda f: (0, 0, 0, 0)),
        ],
        out_specs=[
            pl.BlockSpec((n, 1, pixels // n, channels), lambda f: (0, f, 0, 0)),
            pl.BlockSpec((3, 1, height + 1, out_cols, channels), lambda f: (0, f, 0, 0, 0)),
        ],
        out_shape=[
            jax.ShapeDtypeStruct((n, count, pixels // n, channels), jnp.bfloat16),
            jax.ShapeDtypeStruct((3, count, height + 1, out_cols, channels), jnp.bfloat16),
        ],
        compiler_params=pltpu.CompilerParams(vmem_limit_bytes=VMEM_LIMIT),
        name="conv",
    )(frames, w_spatial)


def temporal_kernel(
    length, dil_ref, off_ref, start_ref, cot_ref, w_ref, feat_ref, back_ref, grad_ref, state, act, dz, grad, acc
):
    layers, taps, channels = w_ref.shape[:3]
    rows = start_ref.shape[0]
    pixels = rows // length
    chunk = min(512, rows)
    starts = range(0, rows, chunk)

    def shift(layer, tap):
        delay = jnp.minimum(off_ref[layer, tap] * dil_ref[layer], length)
        return pl.multiple_of(delay * pixels, pixels)

    shifts = [[shift(layer, tap) for tap in range(taps)] for layer in range(layers)]

    def lagged(layer, at):
        return jnp.concatenate(
            [
                state[layer, pl.ds(pl.multiple_of(rows + at - s, pixels), chunk), :]
                for s in shifts[layer]
            ],
            1,
        )

    def led(at):
        return lambda layer: jnp.concatenate(
            [dz[pl.ds(pl.multiple_of(at + s, pixels), chunk), :] for s in shifts[layer]], 1
        )

    def outer(layer, first, values, moved):
        part = lax.dot_general(
            values, moved, (((0,), (0,)), ((), ())), preferred_element_type=jnp.float32
        )
        acc[layer] = part if first else acc[layer] + part

    blank = jnp.zeros((rows, channels), jnp.bfloat16)
    for layer in range(layers):
        state[layer, pl.ds(0, rows), :] = blank
    dz[pl.ds(rows, rows), :] = blank
    state[0, pl.ds(rows, rows), :] = start_ref[...]
    down = [w_ref[layer].reshape(taps * channels, channels) for layer in range(layers)]
    up = [
        jnp.concatenate([w_ref[layer, tap].T for tap in range(taps)], 0)
        for layer in range(layers)
    ]
    for layer in range(layers):
        last = layer == layers - 1
        for at in starts:
            moved = lagged(layer, at)
            activ = jnp.tanh(jnp.dot(moved, down[layer], preferred_element_type=jnp.float32))
            held = state[layer, pl.ds(rows + at, chunk), :].astype(jnp.float32)
            following = (held + activ).astype(jnp.bfloat16)
            if last:
                feat_ref[pl.ds(at, chunk), :] = following
                cot = cot_ref[pl.ds(at, chunk), :].astype(jnp.float32)
                values = (cot * (1.0 - activ * activ)).astype(jnp.bfloat16)
                dz[pl.ds(at, chunk), :] = values
                outer(layer, at == 0, values, moved)
            else:
                state[layer + 1, pl.ds(rows + at, chunk), :] = following
                act[layer, pl.ds(at, chunk), :] = activ
    for layer in reversed(range(layers)):
        for at in starts:
            here = pl.ds(at, chunk)
            if layer == layers - 1:
                before = cot_ref[here, :].astype(jnp.float32)
            else:
                before = grad[here, :]
            grad[here, :] = before + jnp.dot(
                led(at)(layer), up[layer], preferred_element_type=jnp.float32
            )
        if layer > 0:
            for at in starts:
                here = pl.ds(at, chunk)
                activ = act[layer - 1, here, :]
                values = (grad[here, :] * (1.0 - activ * activ)).astype(jnp.bfloat16)
                dz[here, :] = values
                outer(layer - 1, at == 0, values, lagged(layer - 1, at))
    back_ref[...] = grad[...].astype(jnp.bfloat16)
    for layer in range(layers):
        for tap in range(taps):
            grad_ref[layer, tap] = acc[layer, :, tap * channels : (tap + 1) * channels].T


def temporal(start, cotangent, w_temporal, dilations, offsets, length):
    rows, channels = start.shape
    layers, taps = w_temporal.shape[:2]
    vmem = pl.BlockSpec(memory_space=pltpu.VMEM)
    smem = pl.BlockSpec(memory_space=pltpu.SMEM)
    return pl.pallas_call(
        functools.partial(temporal_kernel, length),
        in_specs=[smem, smem, vmem, vmem, vmem],
        out_specs=[vmem, vmem, vmem],
        out_shape=[
            jax.ShapeDtypeStruct((rows, channels), jnp.bfloat16),
            jax.ShapeDtypeStruct((rows, channels), jnp.bfloat16),
            jax.ShapeDtypeStruct((layers, taps, channels, channels), jnp.float32),
        ],
        scratch_shapes=[
            pltpu.VMEM((layers, 2 * rows, channels), jnp.bfloat16),
            pltpu.VMEM((max(layers - 1, 1), rows, channels), jnp.float32),
            pltpu.VMEM((2 * rows, channels), jnp.bfloat16),
            pltpu.VMEM((rows, channels), jnp.float32),
            pltpu.VMEM((layers, channels, taps * channels), jnp.float32),
        ],
        compiler_params=pltpu.CompilerParams(vmem_limit_bytes=VMEM_LIMIT),
        name="temporal",
    )(dilations, offsets, start, cotangent, w_temporal)


def outer_kernel(back_ref, planes_ref, out_ref, acc):
    chunks, _, chunk_pixels, channels = back_ref.shape
    out_rows = (planes_ref.shape[2] - 1) // 2
    out_cols = planes_ref.shape[3]
    back = back_ref[:, 0].reshape(chunks * chunk_pixels, channels)
    frame = pl.program_id(0)
    for row_tap in range(3):
        parts = []
        for col_tap in range(3):
            rows = [planes_ref[col_tap, 0, 2 * row + row_tap] for row in range(out_rows)]
            parts.append(jnp.concatenate(rows, 0))
        part = lax.dot_general(
            back,
            jnp.concatenate(parts, 1),
            (((0,), (0,)), ((), ())),
            preferred_element_type=jnp.float32,
        )

        @pl.when(frame == 0)
        def _():
            acc[row_tap] = part

        @pl.when(frame > 0)
        def _():
            acc[row_tap] += part

    @pl.when(frame == pl.num_programs(0) - 1)
    def _():
        for row_tap in range(3):
            for col_tap in range(3):
                out_ref[row_tap, col_tap] = acc[
                    row_tap, :, col_tap * channels : (col_tap + 1) * channels
                ].T


def outer(back, planes):
    chunks, count, chunk_pixels, channels = back.shape
    return pl.pallas_call(
        outer_kernel,
        grid=(count,),
        in_specs=[
            pl.BlockSpec((chunks, 1, chunk_pixels, channels), lambda f: (0, f, 0, 0)),
            pl.BlockSpec((3, 1) + planes.shape[2:], lambda f: (0, f, 0, 0, 0)),
        ],
        out_specs=pl.BlockSpec((3, 3, channels, channels), lambda f: (0, 0, 0, 0)),
        out_shape=jax.ShapeDtypeStruct((3, 3, channels, channels), jnp.float32),
        scratch_shapes=[pltpu.VMEM((3, channels, 3 * channels), jnp.float32)],
        compiler_params=pltpu.CompilerParams(vmem_limit_bytes=VMEM_LIMIT),
        name="outer",
    )(back, planes)


def reduce_all(values, n):
    me = lax.axis_index("seq")

    def swap(x, bit):
        return lax.ppermute(x, "seq", [(i, i ^ (1 << bit)) for i in range(n)])

    bits = n.bit_length() - 1
    halved = min(2, bits)
    for bit in range(halved):
        half = values.shape[0] // 2
        upper = (me >> bit) & 1
        pieces = values.reshape(2, half, -1)
        mine = lax.dynamic_index_in_dim(pieces, upper, 0, keepdims=False)
        other = lax.dynamic_index_in_dim(pieces, 1 - upper, 0, keepdims=False)
        values = mine + swap(other.astype(jnp.bfloat16), bit).astype(jnp.float32)
    for bit in range(halved, bits):
        sent = values.astype(jnp.bfloat16)
        values = sent.astype(jnp.float32) + swap(sent, bit).astype(jnp.float32)
    values = values.astype(jnp.bfloat16)
    for bit in reversed(range(halved)):
        upper = (me >> bit) & 1
        got = swap(values, bit)
        values = jnp.where(
            upper == 0, jnp.concatenate([values, got], 0), jnp.concatenate([got, values], 0)
        )
    return values.astype(jnp.float32)


def local(n, frames, w_spatial, w_temporal, dilations, offsets, cotangent):
    count, height, width, channels = frames.shape
    length, pixels = cotangent.shape[:2]
    maps, planes = conv(frames, w_spatial, n)
    start = lax.all_to_all(
        maps.reshape(n, count * pixels, channels), "seq", split_axis=0, concat_axis=0, tiled=True
    )
    features, grad_maps, grad_temporal = temporal(
        start.reshape(length * pixels, channels),
        cotangent.reshape(length * pixels, channels),
        w_temporal,
        dilations,
        offsets,
        length,
    )
    back = lax.all_to_all(
        grad_maps.reshape(n, count * pixels, channels), "seq", split_axis=0, concat_axis=0, tiled=True
    )
    grad_spatial = outer(back.reshape(n, count, pixels, channels), planes)
    both = jnp.concatenate(
        [grad_spatial.reshape(-1, channels), grad_temporal.reshape(-1, channels)], 0
    )
    both = reduce_all(both, n)
    cut = grad_spatial.size // channels
    return (
        features.reshape(length, pixels, channels),
        both[:cut].reshape(grad_spatial.shape),
        both[cut:].reshape(grad_temporal.shape),
    )


def solution(mesh):
    in_specs = (
        P(("groups", "seq"), None, None, None),
        P(),
        P(),
        P(),
        P(),
        P("groups", "seq", None),
    )
    out_specs = (
        P("groups", "seq", None),
        P("groups", None, None, None),
        P("groups", None, None, None),
    )
    return jax.shard_map(
        functools.partial(local, mesh.shape["seq"]),
        mesh=mesh,
        in_specs=in_specs,
        out_specs=out_specs,
        check_vma=False,
    )
```

time: 183 us -> 86.9 us (0.47)
  waiting for transfers between devices: 113 us -> 33.8 us
  blocking collectives: 0 us -> 21.9 us
  local copies, waits for them, and re-layouts: 20.5 us -> 2.48 us
  between operations: 18.5 us -> 0.71 us
  Pallas kernels: 0 us -> 15.6 us
  matrix products: 13.2 us -> 0 us
  other arithmetic: 5.13 us -> 1.45 us
    psum x1 -> x0, waiting for transfers between devices: 92.7 us -> none  [local(): lax.psum((local_spatial, local_temporal), 'seq')]
    all_to_all x0 -> x1, blocking collectives: none -> 21.9 us  [local(): lax.all_to_all(maps.reshape(n, count * pixels, channels), 'seq', split_ax...]
    ppermute x0 -> x6, waiting for transfers between devices: none -> 19.3 us  [swap(): return lax.ppermute(x, 'seq', [(i, i ^ 1 << bit) for i in range(n)])]
    pallas_call x0 -> x3, Pallas kernels: none -> 15.6 us  [the longest x1 6.11 us: temporal(): pl.pallas_call(functools.partial(temporal_kernel, length), in_specs=[smem...]
    dot_general x36 -> x0, matrix products: 13.2 us -> none  [the longest x6 4.12 us: temporal_backward(): lax.dot_general(moved, dz_flat, (((0,), (0,)), ((), ())), preferred_eleme...]
    unnamed x37 -> x4, local copies, waits for them, and re-layouts: 8.99 us -> 0.8 us
    all_to_all x2 -> x1, starting transfers between devices: 11.7 us -> 4.24 us  [local(): lax.all_to_all(grad_maps.reshape(n, count * pixels, channels), 'seq', spl...]
    ppermute x0 -> x6, starting transfers between devices: none -> 6.28 us  [swap(): return lax.ppermute(x, 'seq', [(i, i ^ 1 << bit) for i in range(n)])]
  transfers between devices with their start and end apart: 3 -> 7, of which waited for: 3 -> 7; matrix products, arithmetic and copies ran while one was open for 3% -> 0% of each run, Pallas kernels for 0% -> 0%
where the time goes in v1:
time: 86.9 us; the launch traced here: 86.5 us
  waiting for transfers between devices  33.8 us (39%)
  blocking collectives  21.9 us (25%)
  Pallas kernels  15.6 us (18%)
  starting transfers between devices  10.5 us (12%)
  local copies, waits for them, and re-layouts  2.48 us (3%)
  other arithmetic  1.45 us (2%)
    all_to_all x1, blocking collectives, local(): lax.all_to_all(maps.reshape(n, count * pixels, channels), 'seq', split_ax...  21.9 us
    ppermute x6, waiting for transfers between devices, swap(): return lax.ppermute(x, 'seq', [(i, i ^ 1 << bit) for i in range(n)])  19.3 us
    all_to_all x1, waiting for transfers between devices, local(): lax.all_to_all(grad_maps.reshape(n, count * pixels, channels), 'seq', spl...  14.5 us
    ppermute x6, starting transfers between devices, swap(): return lax.ppermute(x, 'seq', [(i, i ^ 1 << bit) for i in range(n)])  6.28 us
    pallas_call x1, Pallas kernels, temporal(): pl.pallas_call(functools.partial(temporal_kernel, length), in_specs=[smem...  6.11 us
    pallas_call x1, Pallas kernels, conv(): pl.pallas_call(conv_kernel, grid=(count,), in_specs=[pl.BlockSpec((1, hei...  4.97 us
    pallas_call x1, Pallas kernels, outer(): pl.pallas_call(outer_kernel, grid=(count,), in_specs=[pl.BlockSpec((chunk...  4.51 us
    all_to_all x1, starting transfers between devices, local(): lax.all_to_all(grad_maps.reshape(n, count * pixels, channels), 'seq', spl...  4.24 us
  transfers between devices with their start and end apart: 7, of which 7 were waited for; matrix products, arithmetic and copies ran while one was open for 0% of the time, Pallas kernels for 0%

profile of v1, /device:TPU:0, one launch (start us, length us, event | category | flops | bytes accessed | tf_op | source)
XLA Modules:
  0.0 86.5 jit_solution(6194570944493872469)
XLA Ops:
  0.6 5.0 %conv.1 = (bf16[16,2,64,128]{3,2,1,0:T(8,128)(2,1)}, bf16[3,2,33,64,128]{4,3,2,1,0:T(8,128)(2,1)}) custom-call(bf16[2,32,128,128]{3,2,1,0:T(8,128)(2,1)} %x_ref.1, bf16[3,3,128,128]{3,2,1,0:T(8,128)(2,1)} %w_ref.2), custom_call_target="tpu_custom_call" | custom-call | tf_op jit(solution)/shard_map/conv/pallas_call | solution.py:59
  5.6 21.9 %all_to_all.10 = bf16[16,128,128]{2,1,0:T(8,128)(2,1)} all-to-all(bf16[16,128,128]{2,1,0:T(8,128)(2,1)} %bitcast.31), channel_id=1, replica_groups=mesh['groups'=2,'seq'=16] {'seq'}, dimensions={0} | all-to-all | bytes 1048576 | tf_op jit(solution)/shard_map/all_to_all | solution.py:273
  27.5 6.1 %temporal.1 = (bf16[2048,128]{1,0:T(8,128)(2,1)}, bf16[2048,128]{1,0:T(8,128)(2,1)}, f32[2,3,128,128]{3,2,1,0:T(8,128)}) custom-call(s32[2]{0:T(128)} %dil_ref.1, s32[2,3]{1,0:T(2,128)} %off_ref.1, bf16[2048,128]{1,0:T(8,128)(2,1)} %bitcast.26, bf16[2048,128]{1,0:T(8,128)(2,1)} %bitcast.32, bf16[2,3,128,128]{3,2,1,0:T(8,128)(2,1)} %w_ref.3), custom_call_target="tpu_custom_call" | custom-call | tf_op jit(solution)/shard_map/temporal/pallas_call | solution.py:168
  33.6 0.0 copy-start.1
  33.6 4.2 %all-to-all-start.1 = ((bf16[16,128,128]{2,1,0:T(8,128)(2,1)}), bf16[16,128,128]{2,1,0:T(8,128)(2,1)S(1)}, u32[]{:S(2)}, u32[]{:S(2)}) async-start(bf16[16,128,128]{2,1,0:T(8,128)(2,1)} %bitcast.30), calls=%async_computation.1 | async-start | bytes 1048576 | tf_op jit(solution)/shard_map/all_to_all | solution.py:284
  37.9 14.5 %all-to-all-done.1 = bf16[16,128,128]{2,1,0:T(8,128)(2,1)S(1)} async-done(((bf16[16,128,128]{2,1,0:T(8,128)(2,1)}), bf16[16,128,128]{2,1,0:T(8,128)(2,1)S(1)}, u32[]{:S(2)}, u32[]{:S(2)}) %all-to-all-start.1) | async-done | bytes 524320 | tf_op jit(solution)/shard_map/all_to_all | solution.py:284
  52.4 0.0 copy-start
  52.4 0.8 copy-done
  53.1 4.5 %outer.1 = f32[3,3,128,128]{3,2,1,0:T(8,128)} custom-call(bf16[16,2,64,128]{3,2,1,0:T(8,128)(2,1)} %bitcast.25, bf16[3,2,33,64,128]{4,3,2,1,0:T(8,128)(2,1)} %get-tuple-element.11.planes_ref), custom_call_target="tpu_custom_call" | custom-call | tf_op jit(solution)/shard_map/outer/pallas_call | solution.py:226
  57.7 0.0 copy-done.1
  57.7 1.1 %pad_maximum_fusion = f32[1920,128]{1,0:T(8,128)S(1)} fusion(f32[768,128]{1,0:T(8,128)S(1)} %bitcast.34, f32[1152,128]{1,0:T(8,128)} %bitcast.24), kind=kLoop, calls=%fused_computation | loop fusion | flops 245760 | bytes 1966080 | tf_op jit(solution)/shard_map/concatenate | solution.py:288
  58.8 0.1 collective-permute-start
  58.9 1.5 %collective-permute-done = bf16[960,128]{1,0:T(8,128)(2,1)S(1)} collective-permute-done((bf16[960,128]{1,0:T(8,128)(2,1)S(1)}, bf16[960,128]{1,0:T(8,128)(2,1)S(1)}, u32[]{:S(2)}, u32[]{:S(2)}) %collective-permute-start) | collective-permute-done | bytes 245792 | tf_op jit(solution)/shard_map/ppermute | solution.py:245
  60.5 0.9 %collective-permute-start.1 = (bf16[480,128]{1,0:T(8,128)(2,1)S(1)}, bf16[480,128]{1,0:T(8,128)(2,1)S(1)}, u32[]{:S(2)}, u32[]{:S(2)}) collective-permute-start(bf16[480,128]{1,0:T(8,128)(2,1)S(1)} %fusion.3), channel_id=1, source_target_pairs={{0,2},{1,3},{2,0},{3,1},{4,6},{5,7},{6,4},{7,5},{8,10},{9,11},{10,... | collective-permute-start | bytes 368648 | tf_op jit(solution)/shard_map/ppermute | solution.py:245
  61.4 4.5 %collective-permute-done.1 = bf16[480,128]{1,0:T(8,128)(2,1)S(1)} collective-permute-done((bf16[480,128]{1,0:T(8,128)(2,1)S(1)}, bf16[480,128]{1,0:T(8,128)(2,1)S(1)}, u32[]{:S(2)}, u32[]{:S(2)}) %collective-permute-start.1) | collective-permute-done | bytes 122912 | tf_op jit(solution)/shard_map/ppermute | solution.py:245
  66.0 1.7 %collective-permute-start.2 = (bf16[480,128]{1,0:T(8,128)(2,1)S(1)}, bf16[480,128]{1,0:T(8,128)(2,1)S(1)}, u32[]{:S(2)}, u32[]{:S(2)}) collective-permute-start(bf16[480,128]{1,0:T(8,128)(2,1)S(1)} %fusion.2), channel_id=1, source_target_pairs={{0,4},{1,5},{2,6},{3,7},{4,0},{5,1},{6,2},{7,3},{8,12},{9,13},{10,... | collective-permute-start | bytes 368648 | tf_op jit(solution)/shard_map/ppermute | solution.py:245
  67.6 3.3 %collective-permute-done.2 = bf16[480,128]{1,0:T(8,128)(2,1)S(1)} collective-permute-done((bf16[480,128]{1,0:T(8,128)(2,1)S(1)}, bf16[480,128]{1,0:T(8,128)(2,1)S(1)}, u32[]{:S(2)}, u32[]{:S(2)}) %collective-permute-start.2) | collective-permute-done | bytes 122912 | tf_op jit(solution)/shard_map/ppermute | solution.py:245
  70.9 2.3 %collective-permute-start.3 = (bf16[480,128]{1,0:T(8,128)(2,1)S(1)}, bf16[480,128]{1,0:T(8,128)(2,1)S(1)}, u32[]{:S(2)}, u32[]{:S(2)}) collective-permute-start(bf16[480,128]{1,0:T(8,128)(2,1)S(1)} %add_convert_fusion.1), channel_id=1, source_target_pairs={{0,8},{1,9},{2,10},{3,11},{4,12},{5,13},{6,14},{7,15},{8,0},{9,1},... | collective-permute-start | bytes 368648 | tf_op jit(solution)/shard_map/ppermute | solution.py:245
  73.3 4.8 %collective-permute-done.3 = bf16[480,128]{1,0:T(8,128)(2,1)S(1)} collective-permute-done((bf16[480,128]{1,0:T(8,128)(2,1)S(1)}, bf16[480,128]{1,0:T(8,128)(2,1)S(1)}, u32[]{:S(2)}, u32[]{:S(2)}) %collective-permute-start.3) | collective-permute-done | bytes 122912 | tf_op jit(solution)/shard_map/ppermute | solution.py:245
  78.1 1.2 %collective-permute-start.4 = (bf16[480,128]{1,0:T(8,128)(2,1)S(1)}, bf16[480,128]{1,0:T(8,128)(2,1)S(1)}, u32[]{:S(2)}, u32[]{:S(2)}) collective-permute-start(bf16[480,128]{1,0:T(8,128)(2,1)S(1)} %add_convert_fusion), channel_id=1, source_target_pairs={{0,2},{1,3},{2,0},{3,1},{4,6},{5,7},{6,4},{7,5},{8,10},{9,11},{10,... | collective-permute-start | bytes 368648 | tf_op jit(solution)/shard_map/ppermute | solution.py:245
  79.3 3.8 %collective-permute-done.4 = bf16[480,128]{1,0:T(8,128)(2,1)S(1)} collective-permute-done((bf16[480,128]{1,0:T(8,128)(2,1)S(1)}, bf16[480,128]{1,0:T(8,128)(2,1)S(1)}, u32[]{:S(2)}, u32[]{:S(2)}) %collective-permute-start.4) | collective-permute-done | bytes 122912 | tf_op jit(solution)/shard_map/ppermute | solution.py:245
  83.1 0.1 maximum_select_fusion.1
  83.2 0.1 collective-permute-start.5
  83.2 1.5 %collective-permute-done.5 = bf16[960,128]{1,0:T(8,128)(2,1)S(1)} collective-permute-done((bf16[960,128]{1,0:T(8,128)(2,1)S(1)}, bf16[960,128]{1,0:T(8,128)(2,1)S(1)}, u32[]{:S(2)}, u32[]{:S(2)}) %collective-permute-start.5) | collective-permute-done | bytes 245792 | tf_op jit(solution)/shard_map/ppermute | solution.py:245
  84.7 0.1 fusion
  84.8 0.9 slice.8
  85.7 0.8 slice.9
  (6 shorter events, 0.2 us)
Async XLA Ops:
  33.6 24.0 %copy-start.1 = (f32[2,3,128,128]{3,2,1,0:T(8,128)S(1)}, f32[2,3,128,128]{3,2,1,0:T(8,128)}, u32[]{:S(2)}) copy-start(f32[2,3,128,128]{3,2,1,0:T(8,128)} %get-tuple-element.12) | copy-start | bytes 1179652
  33.6 18.7 %all-to-all-start.1 = ((bf16[16,128,128]{2,1,0:T(8,128)(2,1)}), bf16[16,128,128]{2,1,0:T(8,128)(2,1)S(1)}, u32[]{:S(2)}, u32[]{:S(2)}) async-start(bf16[16,128,128]{2,1,0:T(8,128)(2,1)} %bitcast.30), calls=%async_computation.1 | async-start | bytes 1048576 | tf_op jit(solution)/shard_map/all_to_all | solution.py:284
  52.4 0.8 copy-start
  58.8 1.6 %collective-permute-start = (bf16[960,128]{1,0:T(8,128)(2,1)S(1)}, bf16[960,128]{1,0:T(8,128)(2,1)S(1)}, u32[]{:S(2)}, u32[]{:S(2)}) collective-permute-start(bf16[960,128]{1,0:T(8,128)(2,1)S(1)} %fusion.1), channel_id=1, source_target_pairs={{0,1},{1,0},{2,3},{3,2},{4,5},{5,4},{6,7},{7,6},{8,9},{9,8},{10,11... | collective-permute-start | bytes 737288 | tf_op jit(solution)/shard_map/ppermute | solution.py:245
  60.5 5.4 %collective-permute-start.1 = (bf16[480,128]{1,0:T(8,128)(2,1)S(1)}, bf16[480,128]{1,0:T(8,128)(2,1)S(1)}, u32[]{:S(2)}, u32[]{:S(2)}) collective-permute-start(bf16[480,128]{1,0:T(8,128)(2,1)S(1)} %fusion.3), channel_id=1, source_target_pairs={{0,2},{1,3},{2,0},{3,1},{4,6},{5,7},{6,4},{7,5},{8,10},{9,11},{10,... | collective-permute-start | bytes 368648 | tf_op jit(solution)/shard_map/ppermute | solution.py:245
  66.0 4.9 %collective-permute-start.2 = (bf16[480,128]{1,0:T(8,128)(2,1)S(1)}, bf16[480,128]{1,0:T(8,128)(2,1)S(1)}, u32[]{:S(2)}, u32[]{:S(2)}) collective-permute-start(bf16[480,128]{1,0:T(8,128)(2,1)S(1)} %fusion.2), channel_id=1, source_target_pairs={{0,4},{1,5},{2,6},{3,7},{4,0},{5,1},{6,2},{7,3},{8,12},{9,13},{10,... | collective-permute-start | bytes 368648 | tf_op jit(solution)/shard_map/ppermute | solution.py:245
  70.9 7.2 %collective-permute-start.3 = (bf16[480,128]{1,0:T(8,128)(2,1)S(1)}, bf16[480,128]{1,0:T(8,128)(2,1)S(1)}, u32[]{:S(2)}, u32[]{:S(2)}) collective-permute-start(bf16[480,128]{1,0:T(8,128)(2,1)S(1)} %add_convert_fusion.1), channel_id=1, source_target_pairs={{0,8},{1,9},{2,10},{3,11},{4,12},{5,13},{6,14},{7,15},{8,0},{9,1},... | collective-permute-start | bytes 368648 | tf_op jit(solution)/shard_map/ppermute | solution.py:245
  78.1 4.9 %collective-permute-start.4 = (bf16[480,128]{1,0:T(8,128)(2,1)S(1)}, bf16[480,128]{1,0:T(8,128)(2,1)S(1)}, u32[]{:S(2)}, u32[]{:S(2)}) collective-permute-start(bf16[480,128]{1,0:T(8,128)(2,1)S(1)} %add_convert_fusion), channel_id=1, source_target_pairs={{0,2},{1,3},{2,0},{3,1},{4,6},{5,7},{6,4},{7,5},{8,10},{9,11},{10,... | collective-permute-start | bytes 368648 | tf_op jit(solution)/shard_map/ppermute | solution.py:245
  83.2 1.6 %collective-permute-start.5 = (bf16[960,128]{1,0:T(8,128)(2,1)S(1)}, bf16[960,128]{1,0:T(8,128)(2,1)S(1)}, u32[]{:S(2)}, u32[]{:S(2)}) collective-permute-start(bf16[960,128]{1,0:T(8,128)(2,1)S(1)} %maximum_select_fusion.1), channel_id=1, source_target_pairs={{0,1},{1,0},{2,3},{3,2},{4,5},{5,4},{6,7},{7,6},{8,9},{9,8},{10,11... | collective-permute-start | bytes 737288 | tf_op jit(solution)/shard_map/ppermute | solution.py:245

commit v2 on v0

v2 whole, which is shorter than its diff:
```python
import functools

import jax
import jax.numpy as jnp
from jax import lax
from jax.experimental import pallas as pl
from jax.experimental.pallas import tpu as pltpu
from jax.sharding import PartitionSpec as P

F32, BF16 = jnp.float32, jnp.bfloat16
VMEM_LIMIT = 24 * 1024 * 1024
ROWS = (((0,), (0,)), ((), ()))
VMEM = pl.BlockSpec(memory_space=pltpu.VMEM)
HBM = pl.BlockSpec(memory_space=pltpu.HBM)
SMEM = pl.BlockSpec(memory_space=pltpu.SMEM)


def dot(a, b):
    return jnp.dot(a, b, preferred_element_type=F32)


def on_chip(x):
    return pltpu.with_memory_space_constraint(x, pltpu.VMEM)


def moved_down(values, period):
    row = lax.broadcasted_iota(jnp.int32, values.shape, 0)
    return jnp.where(lax.rem(row, period) == 0, 0.0, pltpu.roll(values, 1, 0))


def moved_up(values, period):
    row = lax.broadcasted_iota(jnp.int32, values.shape, 0)
    return jnp.where(
        lax.rem(row, period) == period - 1, 0.0, pltpu.roll(values, values.shape[0] - 1, 0)
    )


def in_hbm(x):
    return pltpu.with_memory_space_constraint(x, pltpu.HBM)


def conv_kernel(x_hbm, w_hbm, out_ref, planes, buf, weights, wide, sems, w_sem, *, bands):
    count, height, width, channels = x_hbm.shape
    out_cols = width // 2
    band = height // bands
    out_band = band // 2
    copies = []
    for frame in range(count):
        for b in range(bands):
            rows = pl.ds(b * band, band)
            copies.append(
                pltpu.make_async_copy(
                    x_hbm.at[frame, rows], buf.at[frame, rows], sems.at[frame * bands + b]
                )
            )
    copies[0].start()
    w_copy = pltpu.make_async_copy(w_hbm, weights, w_sem)
    w_copy.start()
    for copy in copies[1:]:
        copy.start()
    zero = jnp.zeros((out_cols, 2 * channels), BF16)
    chunk_pixels = out_ref.shape[2]
    owners = out_band * out_cols // chunk_pixels
    for frame in range(count):
        planes[frame, 0] = zero
        for b in range(bands):
            copies[frame * bands + b].wait()
            for row in range(b * band, (b + 1) * band):
                slot = row % wide.shape[0]
                wide[slot] = buf[frame, row].astype(F32)
                even = wide[slot, pl.ds(0, out_cols, stride=2), :]
                odd = wide[slot, pl.ds(1, out_cols, stride=2), :]
                planes[frame, row + 1, :, :channels] = even.astype(BF16)
                planes[frame, row + 1, :, channels:] = odd.astype(BF16)
            if frame == 0 and b == 0:
                w_copy.wait()
                w_even = jnp.concatenate([weights[a, 1] for a in range(3)], 0)
                w_odd = jnp.concatenate(
                    [jnp.concatenate([weights[a, 2], weights[a, 0]], 1) for a in range(3)], 0
                )
            first = b * out_band

            def taps(lanes):
                return jnp.concatenate(
                    [
                        jnp.concatenate(
                            [planes[frame, 2 * i + a, :, lanes] for i in range(first, first + out_band)], 0
                        )
                        for a in range(3)
                    ],
                    1,
                )

            odds = dot(taps(slice(channels, 2 * channels)), w_odd)
            total = dot(taps(slice(0, channels)), w_even) + odds[:, :channels]
            total = (total + moved_down(odds[:, channels:], out_cols)).astype(BF16)
            out_ref[pl.ds(b * owners, owners), frame] = total.reshape(owners, chunk_pixels, channels)


def conv(frames, w_spatial, n):
    count, height, width, channels = frames.shape
    out_cols = width // 2
    bands = 4
    return pl.pallas_call(
        functools.partial(conv_kernel, bands=bands),
        in_specs=[HBM, HBM],
        out_specs=[VMEM, VMEM],
        out_shape=[
            pltpu.VMEM((n, count, height // 2 * out_cols // n, channels), BF16),
            pltpu.VMEM((count, height + 1, out_cols, 2 * channels), BF16),
        ],
        scratch_shapes=[
            pltpu.VMEM((count, height, width, channels), BF16),
            pltpu.VMEM(w_spatial.shape, BF16),
            pltpu.VMEM((4, width, channels), F32),
            pltpu.SemaphoreType.DMA((count * bands,)),
            pltpu.SemaphoreType.DMA,
        ],
        compiler_params=pltpu.CompilerParams(vmem_limit_bytes=VMEM_LIMIT),
        name="conv",
    )(in_hbm(frames), in_hbm(w_spatial))


def row_shifts(dil_ref, off_ref, length, pixels):
    layers, taps = off_ref.shape
    return [
        [
            pl.multiple_of(
                jnp.minimum(off_ref[layer, tap] * dil_ref[layer], length) * pixels, pixels
            )
            for tap in range(taps)
        ]
        for layer in range(layers)
    ]


def moved_rows(ref, layer, at, shifts, size, pixels):
    return jnp.concatenate(
        [ref[layer, pl.ds(pl.multiple_of(at + s, pixels), size), :] for s in shifts], 1
    )


def temporal_kernel(
    length, dil_ref, off_ref, start_ref, cot_ref, w_ref, feat_hbm, back_hbm, mid_hbm, dz_hbm, state, dz, act, grad, feat, back, sems
):
    layers, taps, channels = w_ref.shape[:3]
    rows = start_ref.shape[0]
    pixels = rows // length
    size = min(512, rows)
    starts = range(0, rows, size)
    shifts = row_shifts(dil_ref, off_ref, length, pixels)
    sent = []

    def send(source, target):
        sent.append(pltpu.make_async_copy(source, target, sems.at[len(sent)]))
        sent[-1].start()

    blank = jnp.zeros((rows, channels), BF16)
    for layer in range(layers):
        state[layer, pl.ds(0, rows), :] = blank
        dz[layer, pl.ds(rows, rows), :] = blank
    state[0, pl.ds(rows, rows), :] = start_ref[...]
    down = [w_ref[layer].reshape(taps * channels, channels) for layer in range(layers)]
    up = [
        jnp.concatenate([w_ref[layer, tap].T for tap in range(taps)], 0)
        for layer in range(layers)
    ]
    for layer in range(layers):
        last = layer == layers - 1
        for at in starts:
            here = pl.ds(at, size)
            moved = moved_rows(state, layer, rows + at, [-s for s in shifts[layer]], size, pixels)
            activ = jnp.tanh(dot(moved, down[layer]))
            held = state[layer, pl.ds(rows + at, size), :].astype(F32)
            following = (held + activ).astype(BF16)
            slope = 1.0 - activ * activ
            if last:
                feat[here, :] = following
                dz[layer, here, :] = (cot_ref[here, :].astype(F32) * slope).astype(BF16)
            else:
                state[layer + 1, pl.ds(rows + at, size), :] = following
                act[layer, here, :] = slope
        if last:
            send(feat, feat_hbm)
            send(dz.at[layer, pl.ds(0, rows)], dz_hbm.at[layer])
        else:
            send(state.at[layer + 1, pl.ds(rows, rows)], mid_hbm.at[layer])
    for layer in reversed(range(layers)):
        for at in starts:
            here = pl.ds(at, size)
            if layer == layers - 1:
                before = cot_ref[here, :].astype(F32)
            else:
                before = grad[here, :]
            after = before + dot(moved_rows(dz, layer, at, shifts[layer], size, pixels), up[layer])
            if layer > 0:
                grad[here, :] = after
                dz[layer - 1, here, :] = (after * act[layer - 1, here, :]).astype(BF16)
            else:
                back[here, :] = after.astype(BF16)
                send(back.at[here], back_hbm.at[here])
        if layer > 0:
            send(dz.at[layer - 1, pl.ds(0, rows)], dz_hbm.at[layer - 1])
    for copy in sent:
        copy.wait()


def temporal(start, cotangent, w_temporal, dilations, offsets, length):
    rows, channels = start.shape
    layers = w_temporal.shape[0]
    pieces = rows // min(512, rows)
    return pl.pallas_call(
        functools.partial(temporal_kernel, length),
        in_specs=[SMEM, SMEM, VMEM, VMEM, VMEM],
        out_specs=[HBM] * 4,
        out_shape=[
            pltpu.HBM((rows, channels), BF16),
            pltpu.HBM((rows, channels), BF16),
            pltpu.HBM((max(layers - 1, 1), rows, channels), BF16),
            pltpu.HBM((layers, rows, channels), BF16),
        ],
        scratch_shapes=[
            pltpu.VMEM((layers, 2 * rows, channels), BF16),
            pltpu.VMEM((layers, 2 * rows, channels), BF16),
            pltpu.VMEM((max(layers - 1, 1), rows, channels), F32),
            pltpu.VMEM((rows, channels), F32),
            pltpu.VMEM((rows, channels), BF16),
            pltpu.VMEM((rows, channels), BF16),
            pltpu.SemaphoreType.DMA((2 * layers + pieces,)),
        ],
        compiler_params=pltpu.CompilerParams(vmem_limit_bytes=VMEM_LIMIT),
        name="temporal",
    )(dilations, offsets, on_chip(start), on_chip(cotangent), on_chip(w_temporal))


def temporal_outer_kernel(length, dil_ref, off_ref, start_ref, mid_ref, dz_ref, out_ref, state):
    layers, taps, channels = out_ref.shape[:3]
    rows = start_ref.shape[0]
    pixels = rows // length
    size = min(1024, rows)
    shifts = row_shifts(dil_ref, off_ref, length, pixels)
    blank = jnp.zeros((rows, channels), BF16)
    for layer in range(layers):
        state[layer, pl.ds(0, rows), :] = blank
        held = start_ref[...] if layer == 0 else mid_ref[layer - 1]
        state[layer, pl.ds(rows, rows), :] = held
        total = jnp.zeros((channels, taps * channels), F32)
        for at in range(0, rows, size):
            moved = moved_rows(state, layer, rows + at, [-s for s in shifts[layer]], size, pixels)
            values = dz_ref[layer, pl.ds(at, size), :]
            total += lax.dot_general(values, moved, ROWS, preferred_element_type=F32)
        for tap in range(taps):
            out_ref[layer, tap] = total[:, tap * channels : (tap + 1) * channels].T


def temporal_outer(start, mid, dz, dilations, offsets, length):
    rows, channels = start.shape
    layers, taps = offsets.shape
    return pl.pallas_call(
        functools.partial(temporal_outer_kernel, length),
        in_specs=[SMEM, SMEM, VMEM, VMEM, VMEM],
        out_specs=VMEM,
        out_shape=pltpu.VMEM((layers, taps, channels, channels), F32),
        scratch_shapes=[pltpu.VMEM((layers, 2 * rows, channels), BF16)],
        compiler_params=pltpu.CompilerParams(vmem_limit_bytes=VMEM_LIMIT),
        name="temporal_outer",
    )(dilations, offsets, on_chip(start), mid, dz)


def spatial_outer_kernel(planes, back_ref, out_ref):
    count, height, out_cols, channels = planes.shape
    channels //= 2
    out_rows = (height - 1) // 2
    totals = [jnp.zeros((2 * channels, 2 * channels), F32) for _ in range(3)]
    for frame in range(count):
        back = back_ref[:, frame].reshape(out_rows * out_cols, channels)
        up = moved_up(back.astype(F32), out_cols).astype(BF16)
        both = jnp.concatenate([back, up], 1).T
        for a in range(3):
            moved = jnp.concatenate([planes[frame, 2 * i + a] for i in range(out_rows)], 0)
            totals[a] += dot(both, moved)
    for a in range(3):
        out_ref[a, 1] = totals[a][:channels, :channels].T
        out_ref[a, 2] = totals[a][:channels, channels:].T
        out_ref[a, 0] = totals[a][channels:, channels:].T


def spatial_outer(planes, back):
    channels = planes.shape[-1] // 2
    return pl.pallas_call(
        spatial_outer_kernel,
        in_specs=[VMEM, VMEM],
        out_specs=VMEM,
        out_shape=pltpu.VMEM((3, 3, channels, channels), F32),
        compiler_params=pltpu.CompilerParams(vmem_limit_bytes=VMEM_LIMIT),
        name="spatial_outer",
    )(on_chip(planes), on_chip(back))


def swap(x, n, bit):
    return lax.ppermute(x, "seq", [(i, i ^ (1 << bit)) for i in range(n)])


def sum_halves(values, n, halved):
    me = lax.axis_index("seq")
    for bit in range(halved):
        half = values.shape[0] // 2
        upper = (me >> bit) & 1
        pieces = values.reshape(2, half, -1)
        mine = lax.dynamic_index_in_dim(pieces, upper, 0, keepdims=False)
        other = lax.dynamic_index_in_dim(pieces, 1 - upper, 0, keepdims=False)
        values = mine + swap(other.astype(BF16), n, bit).astype(F32)
    return values


def sum_whole(values, n, bits):
    for bit in bits:
        sent = values.astype(BF16)
        values = sent.astype(F32) + swap(sent, n, bit).astype(F32)
    return values


def gather_halves(values, n, halved):
    me = lax.axis_index("seq")
    for bit in reversed(range(halved)):
        got = swap(values, n, bit)
        upper = (me >> bit) & 1
        values = jnp.where(upper == 0, jnp.stack([values, got]), jnp.stack([got, values]))
    return values


def exchange(x):
    return lax.all_to_all(x, "seq", split_axis=0, concat_axis=0, tiled=True)


def local(n, frames, w_spatial, w_temporal, dilations, offsets, cotangent):
    count, height, width, channels = frames.shape
    length, pixels = cotangent.shape[:2]
    bits = n.bit_length() - 1
    halved = min(2, bits)
    maps, planes = conv(frames, w_spatial, n)
    start = exchange(maps.reshape(n, count * pixels, channels)).reshape(length * pixels, channels)
    features, grad_maps, mid, dz = temporal(
        start, cotangent.reshape(length * pixels, channels), w_temporal, dilations, offsets, length
    )
    back = exchange(grad_maps.reshape(n, count * pixels, channels))
    grad_temporal = temporal_outer(start, mid, dz, dilations, offsets, length)
    of_temporal = sum_halves(grad_temporal.reshape(-1, channels), n, halved)
    grad_spatial = spatial_outer(planes, back.reshape(n, count, pixels, channels))
    of_temporal = sum_whole(of_temporal, n, range(halved, bits))
    of_temporal = gather_halves(of_temporal.astype(BF16), n, halved).astype(F32)
    of_spatial = sum_halves(grad_spatial.reshape(-1, channels), n, halved)
    of_spatial = sum_whole(of_spatial, n, range(halved, bits))
    of_spatial = gather_halves(of_spatial.astype(BF16), n, halved).astype(F32)
    return (
        features.reshape(length, pixels, channels),
        of_spatial.reshape(grad_spatial.shape),
        of_temporal.reshape(grad_temporal.shape),
    )


def solution(mesh):
    in_specs = (
        P(("groups", "seq"), None, None, None),
        P(),
        P(),
        P(),
        P(),
        P("groups", "seq", None),
    )
    out_specs = (
        P("groups", "seq", None),
        P("groups", None, None, None),
        P("groups", None, None, None),
    )
    return jax.shard_map(
        functools.partial(local, mesh.shape["seq"]),
        mesh=mesh,
        in_specs=in_specs,
        out_specs=out_specs,
        check_vma=False,
    )
```

time: 183 us -> 75.6 us (0.41)
  waiting for transfers between devices: 113 us -> 19.6 us
  blocking collectives: 0 us -> 21.6 us
  between operations: 18.5 us -> 0.87 us
  local copies, waits for them, and re-layouts: 20.5 us -> 3.09 us
  matrix products: 13.2 us -> 0 us
  Pallas kernels: 0 us -> 11.8 us
  starting transfers between devices: 11.8 us -> 15.4 us
  other arithmetic: 5.13 us -> 2.82 us
    psum x1 -> x0, waiting for transfers between devices: 92.7 us -> none  [local(): lax.psum((local_spatial, local_temporal), 'seq')]
    all_to_all x0 -> x1, blocking collectives: none -> 21.6 us  [exchange(): return lax.all_to_all(x, 'seq', split_axis=0, concat_axis=0, tiled=True)]
    all_to_all x2 -> x1, waiting for transfers between devices: 20.2 us -> 5.51 us  [exchange(): return lax.all_to_all(x, 'seq', split_axis=0, concat_axis=0, tiled=True)]
    ppermute x0 -> x12, waiting for transfers between devices: none -> 14.1 us  [swap(): return lax.ppermute(x, 'seq', [(i, i ^ 1 << bit) for i in range(n)])]
    dot_general x36 -> x0, matrix products: 13.2 us -> none  [the longest x6 4.12 us: temporal_backward(): lax.dot_general(moved, dz_flat, (((0,), (0,)), ((), ())), preferred_eleme...]
    pallas_call x0 -> x4, Pallas kernels: none -> 11.8 us  [the longest x1 4.89 us: temporal(): pl.pallas_call(functools.partial(temporal_kernel, length), in_specs=[SMEM...]
    ppermute x0 -> x12, starting transfers between devices: none -> 11.3 us  [swap(): return lax.ppermute(x, 'seq', [(i, i ^ 1 << bit) for i in range(n)])]
    all_to_all x2 -> x1, starting transfers between devices: 11.7 us -> 4.11 us  [exchange(): return lax.all_to_all(x, 'seq', split_axis=0, concat_axis=0, tiled=True)]
  transfers between devices with their start and end apart: 3 -> 13, of which waited for: 3 -> 9; matrix products, arithmetic and copies ran while one was open for 3% -> 3% of each run, Pallas kernels for 0% -> 4%
where the time goes in v2:
time: 75.6 us; the launch traced here: 75.2 us
  blocking collectives  21.6 us (29%)
  waiting for transfers between devices  19.6 us (26%)
  starting transfers between devices  15.4 us (20%)
  Pallas kernels  11.8 us (16%)
  local copies, waits for them, and re-layouts  3.09 us (4%)
  other arithmetic  2.82 us (4%)
  between operations  0.87 us (1%)
    all_to_all x1, blocking collectives, exchange(): return lax.all_to_all(x, 'seq', split_axis=0, concat_axis=0, tiled=True)  21.6 us
    ppermute x12, waiting for transfers between devices, swap(): return lax.ppermute(x, 'seq', [(i, i ^ 1 << bit) for i in range(n)])  14.1 us
    ppermute x12, starting transfers between devices, swap(): return lax.ppermute(x, 'seq', [(i, i ^ 1 << bit) for i in range(n)])  11.3 us
    all_to_all x1, waiting for transfers between devices, exchange(): return lax.all_to_all(x, 'seq', split_axis=0, concat_axis=0, tiled=True)  5.51 us
    pallas_call x1, Pallas kernels, temporal(): pl.pallas_call(functools.partial(temporal_kernel, length), in_specs=[SMEM...  4.89 us
    pallas_call x1, Pallas kernels, conv(): pl.pallas_call(functools.partial(conv_kernel, bands=bands), in_specs=[HBM...  4.17 us
    all_to_all x1, starting transfers between devices, exchange(): return lax.all_to_all(x, 'seq', split_axis=0, concat_axis=0, tiled=True)  4.11 us
    unnamed x14, local copies, waits for them, and re-layouts  3.02 us
  transfers between devices with their start and end apart: 13, of which 9 were waited for; matrix products, arithmetic and copies ran while one was open for 3% of the time, Pallas kernels for 4%

profile of v2, /device:TPU:0, one launch (start us, length us, event | category | flops | bytes accessed | tf_op | source)
XLA Modules:
  0.0 75.2 jit_solution(5051772043192062632)
XLA Ops:
  0.7 4.2 %conv.1 = (bf16[16,2,64,128]{3,2,1,0:T(8,128)(2,1)S(1)}, bf16[2,33,64,256]{3,2,1,0:T(8,128)(2,1)S(1)}) custom-call(bf16[2,32,128,128]{3,2,1,0:T(8,128)(2,1)} %x_hbm.1, bf16[3,3,128,128]{3,2,1,0:T(8,128)(2,1)} %w_hbm.1), custom_call_target="tpu_custom_call" | custom-call | tf_op jit(solution)/shard_map/conv/pallas_call | solution.py:104
  4.9 21.6 %all_to_all.10 = bf16[16,128,128]{2,1,0:T(8,128)(2,1)S(1)} all-to-all(bf16[16,128,128]{2,1,0:T(8,128)(2,1)S(1)} %bitcast.50), channel_id=1, replica_groups=mesh['groups'=2,'seq'=16] {'seq'}, dimensions={0} | all-to-all | bytes 1048576 | tf_op jit(solution)/shard_map/all_to_all | solution.py:333
  26.5 4.9 %temporal.1 = (bf16[2048,128]{1,0:T(8,128)(2,1)}, bf16[2048,128]{1,0:T(8,128)(2,1)}, bf16[1,2048,128]{2,1,0:T(8,128)(2,1)}, bf16[2,2048,128]{2,1,0:T(8,128)(2,1)}) custom-call(s32[2]{0:T(128)S(1)} %copy-done.6, s32[2,3]{1,0:T(2,128)S(1)} %copy-done.5, bf16[2048,128]{1,0:T(8,128)(2,1)S(1)} %bitcast.43, bf16[2048,128]{1,0:T(8,128)(2,1)S(1)} %bitcast.51, ...), custom_call_target="tpu_custom_call" | custom-call | tf_op jit(solution)/shard_map/temporal/pallas_call | solution.py:212
  31.4 4.1 %all-to-all-start.1 = ((bf16[16,128,128]{2,1,0:T(8,128)(2,1)}), bf16[16,128,128]{2,1,0:T(8,128)(2,1)S(1)}, u32[]{:S(2)}, u32[]{:S(2)}) async-start(bf16[16,128,128]{2,1,0:T(8,128)(2,1)} %bitcast.59), calls=%async_computation.1 | async-start | bytes 1048576 | tf_op jit(solution)/shard_map/all_to_all | solution.py:333
  35.5 1.2 %copy-done.1 = bf16[2,2048,128]{2,1,0:T(8,128)(2,1)S(1)} copy-done((bf16[2,2048,128]{2,1,0:T(8,128)(2,1)S(1)}, bf16[2,2048,128]{2,1,0:T(8,128)(2,1)}, u32[]{:S(2)}) %copy-start.1) | copy-done | bytes 1048600
  36.7 1.0 %copy-done.2 = bf16[1,2048,128]{2,1,0:T(8,128)(2,1)S(1)} copy-done((bf16[1,2048,128]{2,1,0:T(8,128)(2,1)S(1)}, bf16[1,2048,128]{2,1,0:T(8,128)(2,1)}, u32[]{:S(2)}) %copy-start.2) | copy-done | bytes 524312
  37.8 1.6 %temporal_outer.1 = f32[2,3,128,128]{3,2,1,0:T(8,128)S(1)} custom-call(s32[2]{0:T(128)S(1)} %copy-done.6, s32[2,3]{1,0:T(2,128)S(1)} %copy-done.5, bf16[2048,128]{1,0:T(8,128)(2,1)S(1)} %bitcast.44, bf16[1,2048,128]{2,1,0:T(8,128)(2,1)S(1)} %copy-done.2, bf16[2,2048,128]{2,1,0:T(8,128)(2,1)S(1)} %copy-done.1), custom_call_target="tpu_custom_call" | custom-call | tf_op jit(solution)/shard_map/temporal_outer/pallas_call | solution.py:259
  39.4 0.7 copy-done
  40.1 0.5 collective-permute-start.6
  40.6 0.9 %collective-permute-done.6 = bf16[384,128]{1,0:T(8,128)(2,1)S(1)} collective-permute-done((bf16[384,128]{1,0:T(8,128)(2,1)S(1)}, bf16[384,128]{1,0:T(8,128)(2,1)S(1)}, u32[]{:S(2)}, u32[]{:S(2)}) %collective-permute-start.6) | collective-permute-done | bytes 98336 | tf_op jit(solution)/shard_map/ppermute | solution.py:301
  41.6 0.9 %bitcast_add_fusion.1 = f32[384,128]{1,0:T(8,128)S(1)} fusion(bf16[384,128]{1,0:T(8,128)(2,1)S(1)} %collective-permute-done.6, f32[2,384,128]{2,1,0:T(8,128)} %bitcast.49, s32[]{:T(128)S(6)} %select_n.83), kind=kLoop, calls=%fused_computation.5 | loop fusion | flops 98304 | bytes 491524 | tf_op jit(solution)/shard_map/add | solution.py:312
  42.5 1.9 %collective-permute-start.7 = (bf16[192,128]{1,0:T(8,128)(2,1)S(1)}, bf16[192,128]{1,0:T(8,128)(2,1)S(1)}, u32[]{:S(2)}, u32[]{:S(2)}) collective-permute-start(bf16[192,128]{1,0:T(8,128)(2,1)S(1)} %fusion.6), channel_id=1, source_target_pairs={{0,2},{1,3},{2,0},{3,1},{4,6},{5,7},{6,4},{7,5},{8,10},{9,11},{10,... | collective-permute-start | bytes 147464 | tf_op jit(solution)/shard_map/ppermute | solution.py:301
  44.5 5.5 %all-to-all-done.1 = bf16[16,128,128]{2,1,0:T(8,128)(2,1)S(1)} async-done(((bf16[16,128,128]{2,1,0:T(8,128)(2,1)}), bf16[16,128,128]{2,1,0:T(8,128)(2,1)S(1)}, u32[]{:S(2)}, u32[]{:S(2)}) %all-to-all-start.1) | async-done | bytes 524320 | tf_op jit(solution)/shard_map/all_to_all | solution.py:333
  50.0 1.1 %spatial_outer.1 = f32[3,3,128,128]{3,2,1,0:T(8,128)S(1)} custom-call(bf16[2,33,64,256]{3,2,1,0:T(8,128)(2,1)S(1)} %get-tuple-element.11.planes, bf16[16,2,64,128]{3,2,1,0:T(8,128)(2,1)S(1)} %bitcast.45), custom_call_target="tpu_custom_call" | custom-call | tf_op jit(solution)/shard_map/spatial_outer/pallas_call | solution.py:290
  51.1 0.1 collective-permute-start
  51.3 1.8 %collective-permute-start.8 = (bf16[192,128]{1,0:T(8,128)(2,1)S(1)}, bf16[192,128]{1,0:T(8,128)(2,1)S(1)}, u32[]{:S(2)}, u32[]{:S(2)}) collective-permute-start(bf16[192,128]{1,0:T(8,128)(2,1)S(1)} %fusion.4), channel_id=1, source_target_pairs={{0,4},{1,5},{2,6},{3,7},{4,0},{5,1},{6,2},{7,3},{8,12},{9,13},{10,... | collective-permute-start | bytes 147464 | tf_op jit(solution)/shard_map/ppermute | solution.py:301
  53.1 1.0 %collective-permute-start.1 = (bf16[288,128]{1,0:T(8,128)(2,1)S(1)}, bf16[288,128]{1,0:T(8,128)(2,1)S(1)}, u32[]{:S(2)}, u32[]{:S(2)}) collective-permute-start(bf16[288,128]{1,0:T(8,128)(2,1)S(1)} %fusion.5), channel_id=1, source_target_pairs={{0,2},{1,3},{2,0},{3,1},{4,6},{5,7},{6,4},{7,5},{8,10},{9,11},{10,... | collective-permute-start | bytes 221192 | tf_op jit(solution)/shard_map/ppermute | solution.py:301
  54.1 1.4 %collective-permute-done.8 = bf16[192,128]{1,0:T(8,128)(2,1)S(1)} collective-permute-done((bf16[192,128]{1,0:T(8,128)(2,1)S(1)}, bf16[192,128]{1,0:T(8,128)(2,1)S(1)}, u32[]{:S(2)}, u32[]{:S(2)}) %collective-permute-start.8) | collective-permute-done | bytes 49184 | tf_op jit(solution)/shard_map/ppermute | solution.py:301
  55.5 2.3 %collective-permute-start.9 = (bf16[192,128]{1,0:T(8,128)(2,1)S(1)}, bf16[192,128]{1,0:T(8,128)(2,1)S(1)}, u32[]{:S(2)}, u32[]{:S(2)}) collective-permute-start(bf16[192,128]{1,0:T(8,128)(2,1)S(1)} %add_convert_fusion.3), channel_id=1, source_target_pairs={{0,8},{1,9},{2,10},{3,11},{4,12},{5,13},{6,14},{7,15},{8,0},{9,1},... | collective-permute-start | bytes 147464 | tf_op jit(solution)/shard_map/ppermute | solution.py:301
  57.8 0.9 %collective-permute-start.2 = (bf16[288,128]{1,0:T(8,128)(2,1)S(1)}, bf16[288,128]{1,0:T(8,128)(2,1)S(1)}, u32[]{:S(2)}, u32[]{:S(2)}) collective-permute-start(bf16[288,128]{1,0:T(8,128)(2,1)S(1)} %fusion.2), channel_id=1, source_target_pairs={{0,4},{1,5},{2,6},{3,7},{4,0},{5,1},{6,2},{7,3},{8,12},{9,13},{10,... | collective-permute-start | bytes 221192 | tf_op jit(solution)/shard_map/ppermute | solution.py:301
  58.7 1.9 %collective-permute-done.9 = bf16[192,128]{1,0:T(8,128)(2,1)S(1)} collective-permute-done((bf16[192,128]{1,0:T(8,128)(2,1)S(1)}, bf16[192,128]{1,0:T(8,128)(2,1)S(1)}, u32[]{:S(2)}, u32[]{:S(2)}) %collective-permute-start.9) | collective-permute-done | bytes 49184 | tf_op jit(solution)/shard_map/ppermute | solution.py:301
  60.6 1.1 %collective-permute-start.10 = (bf16[192,128]{1,0:T(8,128)(2,1)S(1)}, bf16[192,128]{1,0:T(8,128)(2,1)S(1)}, u32[]{:S(2)}, u32[]{:S(2)}) collective-permute-start(bf16[192,128]{1,0:T(8,128)(2,1)S(1)} %add_convert_fusion.2), channel_id=1, source_target_pairs={{0,2},{1,3},{2,0},{3,1},{4,6},{5,7},{6,4},{7,5},{8,10},{9,11},{10,... | collective-permute-start | bytes 147464 | tf_op jit(solution)/shard_map/ppermute | solution.py:301
  61.7 0.5 collective-permute-done.2
  62.3 1.6 %collective-permute-start.3 = (bf16[288,128]{1,0:T(8,128)(2,1)S(1)}, bf16[288,128]{1,0:T(8,128)(2,1)S(1)}, u32[]{:S(2)}, u32[]{:S(2)}) collective-permute-start(bf16[288,128]{1,0:T(8,128)(2,1)S(1)} %add_convert_fusion.1), channel_id=1, source_target_pairs={{0,8},{1,9},{2,10},{3,11},{4,12},{5,13},{6,14},{7,15},{8,0},{9,1},... | collective-permute-start | bytes 221192 | tf_op jit(solution)/shard_map/ppermute | solution.py:301
  63.8 1.0 %collective-permute-done.10 = bf16[192,128]{1,0:T(8,128)(2,1)S(1)} collective-permute-done((bf16[192,128]{1,0:T(8,128)(2,1)S(1)}, bf16[192,128]{1,0:T(8,128)(2,1)S(1)}, u32[]{:S(2)}, u32[]{:S(2)}) %collective-permute-start.10) | collective-permute-done | bytes 49184 | tf_op jit(solution)/shard_map/ppermute | solution.py:301
  64.8 0.1 collective-permute-start.11
  64.9 3.5 %collective-permute-done.3 = bf16[288,128]{1,0:T(8,128)(2,1)S(1)} collective-permute-done((bf16[288,128]{1,0:T(8,128)(2,1)S(1)}, bf16[288,128]{1,0:T(8,128)(2,1)S(1)}, u32[]{:S(2)}, u32[]{:S(2)}) %collective-permute-start.3) | collective-permute-done | bytes 73760 | tf_op jit(solution)/shard_map/ppermute | solution.py:301
  68.4 0.1 collective-permute-start.4
  68.5 4.3 %collective-permute-done.4 = bf16[288,128]{1,0:T(8,128)(2,1)S(1)} collective-permute-done((bf16[288,128]{1,0:T(8,128)(2,1)S(1)}, bf16[288,128]{1,0:T(8,128)(2,1)S(1)}, u32[]{:S(2)}, u32[]{:S(2)}) %collective-permute-start.4) | collective-permute-done | bytes 73760 | tf_op jit(solution)/shard_map/ppermute | solution.py:301
  72.9 0.8 %fusion = f32[2,3,128,128]{3,2,1,0:T(8,128)} fusion(bf16[1,3,128,128]{3,2,1,0:T(8,128)(2,1)S(1)} %bitcast.68, bf16[1,3,128,128]{3,2,1,0:T(8,128)(2,1)S(1)} %bitcast.62, pred[]{:T(512)S(6)} %eq.8), kind=kLoop, calls=%fused_computation.4 | loop fusion | flops 393216 | bytes 589825 | tf_op jit(solution)/shard_map/convert_element_type | solution.py:351
  73.7 0.5 collective-permute-done.5
  74.3 0.9 %convert.1 = f32[3,3,128,128]{3,2,1,0:T(8,128)} convert(bf16[3,3,128,128]{3,2,1,0:T(8,128)(2,1)S(1)} %bitcast.52) | non-fusion elementwise | flops 147456 | bytes 884736 | tf_op jit(solution)/shard_map/convert_element_type | solution.py:354
  (32 shorter events, 0.4 us)
Async XLA Ops:
  0.6 25.8 %copy-start.3 = (bf16[32,64,128]{2,1,0:T(8,128)(2,1)S(1)}, bf16[32,64,128]{2,1,0:T(8,128)(2,1)}, u32[]{:S(2)}) copy-start(bf16[32,64,128]{2,1,0:T(8,128)(2,1)} %param.11) | copy-start | bytes 1572868
  0.6 25.8 %copy-start.5 = (s32[2,3]{1,0:T(2,128)S(1)}, s32[2,3]{1,0:T(2,128)}, u32[]{:S(2)}) copy-start(s32[2,3]{1,0:T(2,128)} %off_ref.3) | copy-start | bytes 76
  0.7 25.8 %copy-start.4 = (bf16[2,3,128,128]{3,2,1,0:T(8,128)(2,1)S(1)}, bf16[2,3,128,128]{3,2,1,0:T(8,128)(2,1)}, u32[]{:S(2)}) copy-start(bf16[2,3,128,128]{3,2,1,0:T(8,128)(2,1)} %w_ref.1) | copy-start | bytes 589828
  0.7 25.8 %copy-start.6 = (s32[2]{0:T(128)S(1)}, s32[2]{0:T(128)}, u32[]{:S(2)}) copy-start(s32[2]{0:T(128)} %dil_ref.3) | copy-start | bytes 28
  31.4 18.6 %all-to-all-start.1 = ((bf16[16,128,128]{2,1,0:T(8,128)(2,1)}), bf16[16,128,128]{2,1,0:T(8,128)(2,1)S(1)}, u32[]{:S(2)}, u32[]{:S(2)}) async-start(bf16[16,128,128]{2,1,0:T(8,128)(2,1)} %bitcast.59), calls=%async_computation.1 | async-start | bytes 1048576 | tf_op jit(solution)/shard_map/all_to_all | solution.py:333
  35.5 1.2 %copy-start.1 = (bf16[2,2048,128]{2,1,0:T(8,128)(2,1)S(1)}, bf16[2,2048,128]{2,1,0:T(8,128)(2,1)}, u32[]{:S(2)}) copy-start(bf16[2,2048,128]{2,1,0:T(8,128)(2,1)} %get-tuple-element.14.dz_ref) | copy-start | bytes 3145732
  36.7 1.0 %copy-start.2 = (bf16[1,2048,128]{2,1,0:T(8,128)(2,1)S(1)}, bf16[1,2048,128]{2,1,0:T(8,128)(2,1)}, u32[]{:S(2)}) copy-start(bf16[1,2048,128]{2,1,0:T(8,128)(2,1)} %get-tuple-element.13.mid_ref) | copy-start | bytes 1572868
  39.4 0.8 copy-start
  40.1 1.4 %collective-permute-start.6 = (bf16[384,128]{1,0:T(8,128)(2,1)S(1)}, bf16[384,128]{1,0:T(8,128)(2,1)S(1)}, u32[]{:S(2)}, u32[]{:S(2)}) collective-permute-start(bf16[384,128]{1,0:T(8,128)(2,1)S(1)} %fusion.3), channel_id=1, source_target_pairs={{0,1},{1,0},{2,3},{3,2},{4,5},{5,4},{6,7},{7,6},{8,9},{9,8},{10,11... | collective-permute-start | bytes 294920 | tf_op jit(solution)/shard_map/ppermute | solution.py:301
  42.5 8.7 %collective-permute-start.7 = (bf16[192,128]{1,0:T(8,128)(2,1)S(1)}, bf16[192,128]{1,0:T(8,128)(2,1)S(1)}, u32[]{:S(2)}, u32[]{:S(2)}) collective-permute-start(bf16[192,128]{1,0:T(8,128)(2,1)S(1)} %fusion.6), channel_id=1, source_target_pairs={{0,2},{1,3},{2,0},{3,1},{4,6},{5,7},{6,4},{7,5},{8,10},{9,11},{10,... | collective-permute-start | bytes 147464 | tf_op jit(solution)/shard_map/ppermute | solution.py:301
  51.1 1.9 %collective-permute-start = (bf16[576,128]{1,0:T(8,128)(2,1)S(1)}, bf16[576,128]{1,0:T(8,128)(2,1)S(1)}, u32[]{:S(2)}, u32[]{:S(2)}) collective-permute-start(bf16[576,128]{1,0:T(8,128)(2,1)S(1)} %fusion.1), channel_id=1, source_target_pairs={{0,1},{1,0},{2,3},{3,2},{4,5},{5,4},{6,7},{7,6},{8,9},{9,8},{10,11... | collective-permute-start | bytes 442376 | tf_op jit(solution)/shard_map/ppermute | solution.py:301
  51.3 4.2 %collective-permute-start.8 = (bf16[192,128]{1,0:T(8,128)(2,1)S(1)}, bf16[192,128]{1,0:T(8,128)(2,1)S(1)}, u32[]{:S(2)}, u32[]{:S(2)}) collective-permute-start(bf16[192,128]{1,0:T(8,128)(2,1)S(1)} %fusion.4), channel_id=1, source_target_pairs={{0,4},{1,5},{2,6},{3,7},{4,0},{5,1},{6,2},{7,3},{8,12},{9,13},{10,... | collective-permute-start | bytes 147464 | tf_op jit(solution)/shard_map/ppermute | solution.py:301
  53.1 4.7 %collective-permute-start.1 = (bf16[288,128]{1,0:T(8,128)(2,1)S(1)}, bf16[288,128]{1,0:T(8,128)(2,1)S(1)}, u32[]{:S(2)}, u32[]{:S(2)}) collective-permute-start(bf16[288,128]{1,0:T(8,128)(2,1)S(1)} %fusion.5), channel_id=1, source_target_pairs={{0,2},{1,3},{2,0},{3,1},{4,6},{5,7},{6,4},{7,5},{8,10},{9,11},{10,... | collective-permute-start | bytes 221192 | tf_op jit(solution)/shard_map/ppermute | solution.py:301
  55.5 5.2 %collective-permute-start.9 = (bf16[192,128]{1,0:T(8,128)(2,1)S(1)}, bf16[192,128]{1,0:T(8,128)(2,1)S(1)}, u32[]{:S(2)}, u32[]{:S(2)}) collective-permute-start(bf16[192,128]{1,0:T(8,128)(2,1)S(1)} %add_convert_fusion.3), channel_id=1, source_target_pairs={{0,8},{1,9},{2,10},{3,11},{4,12},{5,13},{6,14},{7,15},{8,0},{9,1},... | collective-permute-start | bytes 147464 | tf_op jit(solution)/shard_map/ppermute | solution.py:301
  57.8 4.4 %collective-permute-start.2 = (bf16[288,128]{1,0:T(8,128)(2,1)S(1)}, bf16[288,128]{1,0:T(8,128)(2,1)S(1)}, u32[]{:S(2)}, u32[]{:S(2)}) collective-permute-start(bf16[288,128]{1,0:T(8,128)(2,1)S(1)} %fusion.2), channel_id=1, source_target_pairs={{0,4},{1,5},{2,6},{3,7},{4,0},{5,1},{6,2},{7,3},{8,12},{9,13},{10,... | collective-permute-start | bytes 221192 | tf_op jit(solution)/shard_map/ppermute | solution.py:301
  60.6 4.2 %collective-permute-start.10 = (bf16[192,128]{1,0:T(8,128)(2,1)S(1)}, bf16[192,128]{1,0:T(8,128)(2,1)S(1)}, u32[]{:S(2)}, u32[]{:S(2)}) collective-permute-start(bf16[192,128]{1,0:T(8,128)(2,1)S(1)} %add_convert_fusion.2), channel_id=1, source_target_pairs={{0,2},{1,3},{2,0},{3,1},{4,6},{5,7},{6,4},{7,5},{8,10},{9,11},{10,... | collective-permute-start | bytes 147464 | tf_op jit(solution)/shard_map/ppermute | solution.py:301
  62.3 6.1 %collective-permute-start.3 = (bf16[288,128]{1,0:T(8,128)(2,1)S(1)}, bf16[288,128]{1,0:T(8,128)(2,1)S(1)}, u32[]{:S(2)}, u32[]{:S(2)}) collective-permute-start(bf16[288,128]{1,0:T(8,128)(2,1)S(1)} %add_convert_fusion.1), channel_id=1, source_target_pairs={{0,8},{1,9},{2,10},{3,11},{4,12},{5,13},{6,14},{7,15},{8,0},{9,1},... | collective-permute-start | bytes 221192 | tf_op jit(solution)/shard_map/ppermute | solution.py:301
  64.8 8.1 %collective-permute-start.11 = (bf16[2,192,128]{2,1,0:T(8,128)(2,1)S(1)}, bf16[2,192,128]{2,1,0:T(8,128)(2,1)S(1)}, u32[]{:S(2)}, u32[]{:S(2)}) collective-permute-start(bf16[2,192,128]{2,1,0:T(8,128)(2,1)S(1)} %maximum_select_fusion.5), channel_id=1, source_target_pairs={{0,1},{1,0},{2,3},{3,2},{4,5},{5,4},{6,7},{7,6},{8,9},{9,8},{10,11... | collective-permute-start | bytes 294920 | tf_op jit(solution)/shard_map/ppermute | solution.py:301
  68.4 4.4 %collective-permute-start.4 = (bf16[288,128]{1,0:T(8,128)(2,1)S(1)}, bf16[288,128]{1,0:T(8,128)(2,1)S(1)}, u32[]{:S(2)}, u32[]{:S(2)}) collective-permute-start(bf16[288,128]{1,0:T(8,128)(2,1)S(1)} %add_convert_fusion), channel_id=1, source_target_pairs={{0,2},{1,3},{2,0},{3,1},{4,6},{5,7},{6,4},{7,5},{8,10},{9,11},{10,... | collective-permute-start | bytes 221192 | tf_op jit(solution)/shard_map/ppermute | solution.py:301
  72.8 1.4 %collective-permute-start.5 = (bf16[2,288,128]{2,1,0:T(8,128)(2,1)S(1)}, bf16[2,288,128]{2,1,0:T(8,128)(2,1)S(1)}, u32[]{:S(2)}, u32[]{:S(2)}) collective-permute-start(bf16[2,288,128]{2,1,0:T(8,128)(2,1)S(1)} %maximum_select_fusion.3), channel_id=1, source_target_pairs={{0,1},{1,0},{2,3},{3,2},{4,5},{5,4},{6,7},{7,6},{8,9},{9,8},{10,11... | collective-permute-start | bytes 442376 | tf_op jit(solution)/shard_map/ppermute | solution.py:301

commit v3 on v2

--- a/solution.py
+++ b/solution.py
@@ -43,7 +43,7 @@
     count, height, width, channels = x_hbm.shape
     out_cols = width // 2
     band = height // bands
-    out_band = band // 2
+    out_rows = height // 2
     copies = []
     for frame in range(count):
         for b in range(bands):
@@ -60,7 +60,7 @@
         copy.start()
     zero = jnp.zeros((out_cols, 2 * channels), BF16)
     chunk_pixels = out_ref.shape[2]
-    owners = out_band * out_cols // chunk_pixels
+    owners = out_rows * out_cols // chunk_pixels
     for frame in range(count):
         planes[frame, 0] = zero
         for b in range(bands):
@@ -72,29 +72,28 @@
                 odd = wide[slot, pl.ds(1, out_cols, stride=2), :]
                 planes[frame, row + 1, :, :channels] = even.astype(BF16)
                 planes[frame, row + 1, :, channels:] = odd.astype(BF16)
-            if frame == 0 and b == 0:
-                w_copy.wait()
-                w_even = jnp.concatenate([weights[a, 1] for a in range(3)], 0)
-                w_odd = jnp.concatenate(
-                    [jnp.concatenate([weights[a, 2], weights[a, 0]], 1) for a in range(3)], 0
-                )
-            first = b * out_band
-
-            def taps(lanes):
-                return jnp.concatenate(
-                    [
-                        jnp.concatenate(
-                            [planes[frame, 2 * i + a, :, lanes] for i in range(first, first + out_band)], 0
-                        )
-                        for a in range(3)
-                    ],
-                    1,
-                )
-
-            odds = dot(taps(slice(channels, 2 * channels)), w_odd)
-            total = dot(taps(slice(0, channels)), w_even) + odds[:, :channels]
-            total = (total + moved_down(odds[:, channels:], out_cols)).astype(BF16)
-            out_ref[pl.ds(b * owners, owners), frame] = total.reshape(owners, chunk_pixels, channels)
+        if frame == 0:
+            w_copy.wait()
+            w_even = jnp.concatenate([weights[a, 1] for a in range(3)], 0)
+            w_odd = jnp.concatenate(
+                [jnp.concatenate([weights[a, 2], weights[a, 0]], 1) for a in range(3)], 0
+            )
+
+        def taps(lanes):
+            return jnp.concatenate(
+                [
+                    jnp.concatenate(
+                        [planes[frame, 2 * i + a, :, lanes] for i in range(out_rows)], 0
+                    )
+                    for a in range(3)
+                ],
+                1,
+            )
+
+        odds = dot(taps(slice(channels, 2 * channels)), w_odd)
+        total = dot(taps(slice(0, channels)), w_even) + odds[:, :channels]
+        total = (total + moved_down(odds[:, channels:], out_cols)).astype(BF16)
+        out_ref[:, frame] = total.reshape(owners, chunk_pixels, channels)
 
 
 def conv(frames, w_spatial, n):
@@ -146,7 +145,7 @@
     layers, taps, channels = w_ref.shape[:3]
     rows = start_ref.shape[0]
     pixels = rows // length
-    size = min(512, rows)
+    size = min(1024, rows)
     starts = range(0, rows, size)
     shifts = row_shifts(dil_ref, off_ref, length, pixels)
     sent = []
@@ -208,7 +207,7 @@
 def temporal(start, cotangent, w_temporal, dilations, offsets, length):
     rows, channels = start.shape
     layers = w_temporal.shape[0]
-    pieces = rows // min(512, rows)
+    pieces = rows // min(1024, rows)
     return pl.pallas_call(
         functools.partial(temporal_kernel, length),
         in_specs=[SMEM, SMEM, VMEM, VMEM, VMEM],

time: 75.6 us -> 74.3 us (0.983)
  Pallas kernels: 11.8 us -> 10.5 us
    pallas_call x1, Pallas kernels: 4.17 us -> 3.37 us  [conv(): pl.pallas_call(functools.partial(conv_kernel, bands=bands), in_specs=[HBM...]
where the time goes in v3:
time: 74.3 us; the launch traced here: 73.9 us
  blocking collectives  21.6 us (29%)
  waiting for transfers between devices  19.6 us (26%)
  starting transfers between devices  15.4 us (21%)
  Pallas kernels  10.5 us (14%)
  local copies, waits for them, and re-layouts  3.09 us (4%)
  other arithmetic  2.82 us (4%)
  between operations  0.87 us (1%)
    all_to_all x1, blocking collectives, exchange(): return lax.all_to_all(x, 'seq', split_axis=0, concat_axis=0, tiled=True)  21.6 us
    ppermute x12, waiting for transfers between devices, swap(): return lax.ppermute(x, 'seq', [(i, i ^ 1 << bit) for i in range(n)])  14.1 us
    ppermute x12, starting transfers between devices, swap(): return lax.ppermute(x, 'seq', [(i, i ^ 1 << bit) for i in range(n)])  11.3 us
    all_to_all x1, waiting for transfers between devices, exchange(): return lax.all_to_all(x, 'seq', split_axis=0, concat_axis=0, tiled=True)  5.5 us
    pallas_call x1, Pallas kernels, temporal(): pl.pallas_call(functools.partial(temporal_kernel, length), in_specs=[SMEM...  4.37 us
    all_to_all x1, starting transfers between devices, exchange(): return lax.all_to_all(x, 'seq', split_axis=0, concat_axis=0, tiled=True)  4.11 us
    pallas_call x1, Pallas kernels, conv(): pl.pallas_call(functools.partial(conv_kernel, bands=bands), in_specs=[HBM...  3.37 us
    unnamed x14, local copies, waits for them, and re-layouts  3.02 us
  transfers between devices with their start and end apart: 13, of which 9 were waited for; matrix products, arithmetic and copies ran while one was open for 3% of the time, Pallas kernels for 4%

profile of v3, /device:TPU:0, one launch (start us, length us, event | category | flops | bytes accessed | tf_op | source)
XLA Modules:
  0.0 73.9 jit_solution(8612969906703260939)
XLA Ops:
  0.7 3.4 %conv.1 = (bf16[16,2,64,128]{3,2,1,0:T(8,128)(2,1)S(1)}, bf16[2,33,64,256]{3,2,1,0:T(8,128)(2,1)S(1)}) custom-call(bf16[2,32,128,128]{3,2,1,0:T(8,128)(2,1)} %x_hbm.1, bf16[3,3,128,128]{3,2,1,0:T(8,128)(2,1)} %w_hbm.1), custom_call_target="tpu_custom_call" | custom-call | tf_op jit(solution)/shard_map/conv/pallas_call | solution.py:103
  4.0 21.6 %all_to_all.10 = bf16[16,128,128]{2,1,0:T(8,128)(2,1)S(1)} all-to-all(bf16[16,128,128]{2,1,0:T(8,128)(2,1)S(1)} %bitcast.50), channel_id=1, replica_groups=mesh['groups'=2,'seq'=16] {'seq'}, dimensions={0} | all-to-all | bytes 1048576 | tf_op jit(solution)/shard_map/all_to_all | solution.py:332
  25.7 4.4 %temporal.1 = (bf16[2048,128]{1,0:T(8,128)(2,1)}, bf16[2048,128]{1,0:T(8,128)(2,1)}, bf16[1,2048,128]{2,1,0:T(8,128)(2,1)}, bf16[2,2048,128]{2,1,0:T(8,128)(2,1)}) custom-call(s32[2]{0:T(128)S(1)} %copy-done.6, s32[2,3]{1,0:T(2,128)S(1)} %copy-done.5, bf16[2048,128]{1,0:T(8,128)(2,1)S(1)} %bitcast.43, bf16[2048,128]{1,0:T(8,128)(2,1)S(1)} %bitcast.51, ...), custom_call_target="tpu_custom_call" | custom-call | tf_op jit(solution)/shard_map/temporal/pallas_call | solution.py:211
  30.1 4.1 %all-to-all-start.1 = ((bf16[16,128,128]{2,1,0:T(8,128)(2,1)}), bf16[16,128,128]{2,1,0:T(8,128)(2,1)S(1)}, u32[]{:S(2)}, u32[]{:S(2)}) async-start(bf16[16,128,128]{2,1,0:T(8,128)(2,1)} %bitcast.59), calls=%async_computation.1 | async-start | bytes 1048576 | tf_op jit(solution)/shard_map/all_to_all | solution.py:332
  34.2 1.2 %copy-done.1 = bf16[2,2048,128]{2,1,0:T(8,128)(2,1)S(1)} copy-done((bf16[2,2048,128]{2,1,0:T(8,128)(2,1)S(1)}, bf16[2,2048,128]{2,1,0:T(8,128)(2,1)}, u32[]{:S(2)}) %copy-start.1) | copy-done | bytes 1048600
  35.4 1.0 %copy-done.2 = bf16[1,2048,128]{2,1,0:T(8,128)(2,1)S(1)} copy-done((bf16[1,2048,128]{2,1,0:T(8,128)(2,1)S(1)}, bf16[1,2048,128]{2,1,0:T(8,128)(2,1)}, u32[]{:S(2)}) %copy-start.2) | copy-done | bytes 524312
  36.5 1.6 %temporal_outer.1 = f32[2,3,128,128]{3,2,1,0:T(8,128)S(1)} custom-call(s32[2]{0:T(128)S(1)} %copy-done.6, s32[2,3]{1,0:T(2,128)S(1)} %copy-done.5, bf16[2048,128]{1,0:T(8,128)(2,1)S(1)} %bitcast.44, bf16[1,2048,128]{2,1,0:T(8,128)(2,1)S(1)} %copy-done.2, bf16[2,2048,128]{2,1,0:T(8,128)(2,1)S(1)} %copy-done.1), custom_call_target="tpu_custom_call" | custom-call | tf_op jit(solution)/shard_map/temporal_outer/pallas_call | solution.py:258
  38.1 0.7 %copy-done = f32[2,3,128,128]{3,2,1,0:T(8,128)} copy-done((f32[2,3,128,128]{3,2,1,0:T(8,128)}, f32[2,3,128,128]{3,2,1,0:T(8,128)S(1)}, u32[]{:S(2)}) %copy-start) | copy-done | bytes 393240
  38.8 0.5 collective-permute-start.6
  39.3 0.9 %collective-permute-done.6 = bf16[384,128]{1,0:T(8,128)(2,1)S(1)} collective-permute-done((bf16[384,128]{1,0:T(8,128)(2,1)S(1)}, bf16[384,128]{1,0:T(8,128)(2,1)S(1)}, u32[]{:S(2)}, u32[]{:S(2)}) %collective-permute-start.6) | collective-permute-done | bytes 98336 | tf_op jit(solution)/shard_map/ppermute | solution.py:300
  40.2 0.9 %bitcast_add_fusion.1 = f32[384,128]{1,0:T(8,128)S(1)} fusion(bf16[384,128]{1,0:T(8,128)(2,1)S(1)} %collective-permute-done.6, f32[2,384,128]{2,1,0:T(8,128)} %bitcast.49, s32[]{:T(128)S(6)} %select_n.83), kind=kLoop, calls=%fused_computation.5 | loop fusion | flops 98304 | bytes 491524 | tf_op jit(solution)/shard_map/add | solution.py:311
  41.2 1.9 %collective-permute-start.7 = (bf16[192,128]{1,0:T(8,128)(2,1)S(1)}, bf16[192,128]{1,0:T(8,128)(2,1)S(1)}, u32[]{:S(2)}, u32[]{:S(2)}) collective-permute-start(bf16[192,128]{1,0:T(8,128)(2,1)S(1)} %fusion.6), channel_id=1, source_target_pairs={{0,2},{1,3},{2,0},{3,1},{4,6},{5,7},{6,4},{7,5},{8,10},{9,11},{10,... | collective-permute-start | bytes 147464 | tf_op jit(solution)/shard_map/ppermute | solution.py:300
  43.2 5.5 %all-to-all-done.1 = bf16[16,128,128]{2,1,0:T(8,128)(2,1)S(1)} async-done(((bf16[16,128,128]{2,1,0:T(8,128)(2,1)}), bf16[16,128,128]{2,1,0:T(8,128)(2,1)S(1)}, u32[]{:S(2)}, u32[]{:S(2)}) %all-to-all-start.1) | async-done | bytes 524320 | tf_op jit(solution)/shard_map/all_to_all | solution.py:332
  48.7 1.1 %spatial_outer.1 = f32[3,3,128,128]{3,2,1,0:T(8,128)S(1)} custom-call(bf16[2,33,64,256]{3,2,1,0:T(8,128)(2,1)S(1)} %get-tuple-element.11.planes, bf16[16,2,64,128]{3,2,1,0:T(8,128)(2,1)S(1)} %bitcast.45), custom_call_target="tpu_custom_call" | custom-call | tf_op jit(solution)/shard_map/spatial_outer/pallas_call | solution.py:289
  49.8 0.1 collective-permute-start
  49.9 1.8 %collective-permute-start.8 = (bf16[192,128]{1,0:T(8,128)(2,1)S(1)}, bf16[192,128]{1,0:T(8,128)(2,1)S(1)}, u32[]{:S(2)}, u32[]{:S(2)}) collective-permute-start(bf16[192,128]{1,0:T(8,128)(2,1)S(1)} %fusion.4), channel_id=1, source_target_pairs={{0,4},{1,5},{2,6},{3,7},{4,0},{5,1},{6,2},{7,3},{8,12},{9,13},{10,... | collective-permute-start | bytes 147464 | tf_op jit(solution)/shard_map/ppermute | solution.py:300
  51.8 1.0 %collective-permute-start.1 = (bf16[288,128]{1,0:T(8,128)(2,1)S(1)}, bf16[288,128]{1,0:T(8,128)(2,1)S(1)}, u32[]{:S(2)}, u32[]{:S(2)}) collective-permute-start(bf16[288,128]{1,0:T(8,128)(2,1)S(1)} %fusion.5), channel_id=1, source_target_pairs={{0,2},{1,3},{2,0},{3,1},{4,6},{5,7},{6,4},{7,5},{8,10},{9,11},{10,... | collective-permute-start | bytes 221192 | tf_op jit(solution)/shard_map/ppermute | solution.py:300
  52.8 1.4 %collective-permute-done.8 = bf16[192,128]{1,0:T(8,128)(2,1)S(1)} collective-permute-done((bf16[192,128]{1,0:T(8,128)(2,1)S(1)}, bf16[192,128]{1,0:T(8,128)(2,1)S(1)}, u32[]{:S(2)}, u32[]{:S(2)}) %collective-permute-start.8) | collective-permute-done | bytes 49184 | tf_op jit(solution)/shard_map/ppermute | solution.py:300
  54.2 2.3 %collective-permute-start.9 = (bf16[192,128]{1,0:T(8,128)(2,1)S(1)}, bf16[192,128]{1,0:T(8,128)(2,1)S(1)}, u32[]{:S(2)}, u32[]{:S(2)}) collective-permute-start(bf16[192,128]{1,0:T(8,128)(2,1)S(1)} %add_convert_fusion.3), channel_id=1, source_target_pairs={{0,8},{1,9},{2,10},{3,11},{4,12},{5,13},{6,14},{7,15},{8,0},{9,1},... | collective-permute-start | bytes 147464 | tf_op jit(solution)/shard_map/ppermute | solution.py:300
  56.5 0.9 %collective-permute-start.2 = (bf16[288,128]{1,0:T(8,128)(2,1)S(1)}, bf16[288,128]{1,0:T(8,128)(2,1)S(1)}, u32[]{:S(2)}, u32[]{:S(2)}) collective-permute-start(bf16[288,128]{1,0:T(8,128)(2,1)S(1)} %fusion.2), channel_id=1, source_target_pairs={{0,4},{1,5},{2,6},{3,7},{4,0},{5,1},{6,2},{7,3},{8,12},{9,13},{10,... | collective-permute-start | bytes 221192 | tf_op jit(solution)/shard_map/ppermute | solution.py:300
  57.4 1.9 %collective-permute-done.9 = bf16[192,128]{1,0:T(8,128)(2,1)S(1)} collective-permute-done((bf16[192,128]{1,0:T(8,128)(2,1)S(1)}, bf16[192,128]{1,0:T(8,128)(2,1)S(1)}, u32[]{:S(2)}, u32[]{:S(2)}) %collective-permute-start.9) | collective-permute-done | bytes 49184 | tf_op jit(solution)/shard_map/ppermute | solution.py:300
  59.3 1.1 %collective-permute-start.10 = (bf16[192,128]{1,0:T(8,128)(2,1)S(1)}, bf16[192,128]{1,0:T(8,128)(2,1)S(1)}, u32[]{:S(2)}, u32[]{:S(2)}) collective-permute-start(bf16[192,128]{1,0:T(8,128)(2,1)S(1)} %add_convert_fusion.2), channel_id=1, source_target_pairs={{0,2},{1,3},{2,0},{3,1},{4,6},{5,7},{6,4},{7,5},{8,10},{9,11},{10,... | collective-permute-start | bytes 147464 | tf_op jit(solution)/shard_map/ppermute | solution.py:300
  60.4 0.5 collective-permute-done.2
  60.9 1.6 %collective-permute-start.3 = (bf16[288,128]{1,0:T(8,128)(2,1)S(1)}, bf16[288,128]{1,0:T(8,128)(2,1)S(1)}, u32[]{:S(2)}, u32[]{:S(2)}) collective-permute-start(bf16[288,128]{1,0:T(8,128)(2,1)S(1)} %add_convert_fusion.1), channel_id=1, source_target_pairs={{0,8},{1,9},{2,10},{3,11},{4,12},{5,13},{6,14},{7,15},{8,0},{9,1},... | collective-permute-start | bytes 221192 | tf_op jit(solution)/shard_map/ppermute | solution.py:300
  62.5 1.0 %collective-permute-done.10 = bf16[192,128]{1,0:T(8,128)(2,1)S(1)} collective-permute-done((bf16[192,128]{1,0:T(8,128)(2,1)S(1)}, bf16[192,128]{1,0:T(8,128)(2,1)S(1)}, u32[]{:S(2)}, u32[]{:S(2)}) %collective-permute-start.10) | collective-permute-done | bytes 49184 | tf_op jit(solution)/shard_map/ppermute | solution.py:300
  63.5 0.1 collective-permute-start.11
  63.6 3.5 %collective-permute-done.3 = bf16[288,128]{1,0:T(8,128)(2,1)S(1)} collective-permute-done((bf16[288,128]{1,0:T(8,128)(2,1)S(1)}, bf16[288,128]{1,0:T(8,128)(2,1)S(1)}, u32[]{:S(2)}, u32[]{:S(2)}) %collective-permute-start.3) | collective-permute-done | bytes 73760 | tf_op jit(solution)/shard_map/ppermute | solution.py:300
  67.1 0.1 collective-permute-start.4
  67.2 4.3 %collective-permute-done.4 = bf16[288,128]{1,0:T(8,128)(2,1)S(1)} collective-permute-done((bf16[288,128]{1,0:T(8,128)(2,1)S(1)}, bf16[288,128]{1,0:T(8,128)(2,1)S(1)}, u32[]{:S(2)}, u32[]{:S(2)}) %collective-permute-start.4) | collective-permute-done | bytes 73760 | tf_op jit(solution)/shard_map/ppermute | solution.py:300
  71.6 0.8 %fusion = f32[2,3,128,128]{3,2,1,0:T(8,128)} fusion(bf16[1,3,128,128]{3,2,1,0:T(8,128)(2,1)S(1)} %bitcast.68, bf16[1,3,128,128]{3,2,1,0:T(8,128)(2,1)S(1)} %bitcast.62, pred[]{:T(512)S(6)} %eq.8), kind=kLoop, calls=%fused_computation.4 | loop fusion | flops 393216 | bytes 589825 | tf_op jit(solution)/shard_map/convert_element_type | solution.py:350
  72.4 0.5 collective-permute-done.5
  73.0 0.9 %convert.1 = f32[3,3,128,128]{3,2,1,0:T(8,128)} convert(bf16[3,3,128,128]{3,2,1,0:T(8,128)(2,1)S(1)} %bitcast.52) | non-fusion elementwise | flops 147456 | bytes 884736 | tf_op jit(solution)/shard_map/convert_element_type | solution.py:353
  (32 shorter events, 0.4 us)
Async XLA Ops:
  0.6 25.0 %copy-start.3 = (bf16[32,64,128]{2,1,0:T(8,128)(2,1)S(1)}, bf16[32,64,128]{2,1,0:T(8,128)(2,1)}, u32[]{:S(2)}) copy-start(bf16[32,64,128]{2,1,0:T(8,128)(2,1)} %param.11) | copy-start | bytes 1572868
  0.6 25.0 %copy-start.5 = (s32[2,3]{1,0:T(2,128)S(1)}, s32[2,3]{1,0:T(2,128)}, u32[]{:S(2)}) copy-start(s32[2,3]{1,0:T(2,128)} %off_ref.3) | copy-start | bytes 76
  0.7 25.0 %copy-start.4 = (bf16[2,3,128,128]{3,2,1,0:T(8,128)(2,1)S(1)}, bf16[2,3,128,128]{3,2,1,0:T(8,128)(2,1)}, u32[]{:S(2)}) copy-start(bf16[2,3,128,128]{3,2,1,0:T(8,128)(2,1)} %w_ref.1) | copy-start | bytes 589828
  0.7 25.0 %copy-start.6 = (s32[2]{0:T(128)S(1)}, s32[2]{0:T(128)}, u32[]{:S(2)}) copy-start(s32[2]{0:T(128)} %dil_ref.3) | copy-start | bytes 28
  30.1 18.6 %all-to-all-start.1 = ((bf16[16,128,128]{2,1,0:T(8,128)(2,1)}), bf16[16,128,128]{2,1,0:T(8,128)(2,1)S(1)}, u32[]{:S(2)}, u32[]{:S(2)}) async-start(bf16[16,128,128]{2,1,0:T(8,128)(2,1)} %bitcast.59), calls=%async_computation.1 | async-start | bytes 1048576 | tf_op jit(solution)/shard_map/all_to_all | solution.py:332
  34.2 1.2 %copy-start.1 = (bf16[2,2048,128]{2,1,0:T(8,128)(2,1)S(1)}, bf16[2,2048,128]{2,1,0:T(8,128)(2,1)}, u32[]{:S(2)}) copy-start(bf16[2,2048,128]{2,1,0:T(8,128)(2,1)} %get-tuple-element.14.dz_ref) | copy-start | bytes 3145732
  35.4 1.0 %copy-start.2 = (bf16[1,2048,128]{2,1,0:T(8,128)(2,1)S(1)}, bf16[1,2048,128]{2,1,0:T(8,128)(2,1)}, u32[]{:S(2)}) copy-start(bf16[1,2048,128]{2,1,0:T(8,128)(2,1)} %get-tuple-element.13.mid_ref) | copy-start | bytes 1572868
  38.1 0.8 %copy-start = (f32[2,3,128,128]{3,2,1,0:T(8,128)}, f32[2,3,128,128]{3,2,1,0:T(8,128)S(1)}, u32[]{:S(2)}) copy-start(f32[2,3,128,128]{3,2,1,0:T(8,128)S(1)} %temporal_outer.1) | copy-start | bytes 1179652
  38.8 1.4 %collective-permute-start.6 = (bf16[384,128]{1,0:T(8,128)(2,1)S(1)}, bf16[384,128]{1,0:T(8,128)(2,1)S(1)}, u32[]{:S(2)}, u32[]{:S(2)}) collective-permute-start(bf16[384,128]{1,0:T(8,128)(2,1)S(1)} %fusion.3), channel_id=1, source_target_pairs={{0,1},{1,0},{2,3},{3,2},{4,5},{5,4},{6,7},{7,6},{8,9},{9,8},{10,11... | collective-permute-start | bytes 294920 | tf_op jit(solution)/shard_map/ppermute | solution.py:300
  41.2 8.7 %collective-permute-start.7 = (bf16[192,128]{1,0:T(8,128)(2,1)S(1)}, bf16[192,128]{1,0:T(8,128)(2,1)S(1)}, u32[]{:S(2)}, u32[]{:S(2)}) collective-permute-start(bf16[192,128]{1,0:T(8,128)(2,1)S(1)} %fusion.6), channel_id=1, source_target_pairs={{0,2},{1,3},{2,0},{3,1},{4,6},{5,7},{6,4},{7,5},{8,10},{9,11},{10,... | collective-permute-start | bytes 147464 | tf_op jit(solution)/shard_map/ppermute | solution.py:300
  49.8 1.9 %collective-permute-start = (bf16[576,128]{1,0:T(8,128)(2,1)S(1)}, bf16[576,128]{1,0:T(8,128)(2,1)S(1)}, u32[]{:S(2)}, u32[]{:S(2)}) collective-permute-start(bf16[576,128]{1,0:T(8,128)(2,1)S(1)} %fusion.1), channel_id=1, source_target_pairs={{0,1},{1,0},{2,3},{3,2},{4,5},{5,4},{6,7},{7,6},{8,9},{9,8},{10,11... | collective-permute-start | bytes 442376 | tf_op jit(solution)/shard_map/ppermute | solution.py:300
  49.9 4.2 %collective-permute-start.8 = (bf16[192,128]{1,0:T(8,128)(2,1)S(1)}, bf16[192,128]{1,0:T(8,128)(2,1)S(1)}, u32[]{:S(2)}, u32[]{:S(2)}) collective-permute-start(bf16[192,128]{1,0:T(8,128)(2,1)S(1)} %fusion.4), channel_id=1, source_target_pairs={{0,4},{1,5},{2,6},{3,7},{4,0},{5,1},{6,2},{7,3},{8,12},{9,13},{10,... | collective-permute-start | bytes 147464 | tf_op jit(solution)/shard_map/ppermute | solution.py:300
  51.8 4.7 %collective-permute-start.1 = (bf16[288,128]{1,0:T(8,128)(2,1)S(1)}, bf16[288,128]{1,0:T(8,128)(2,1)S(1)}, u32[]{:S(2)}, u32[]{:S(2)}) collective-permute-start(bf16[288,128]{1,0:T(8,128)(2,1)S(1)} %fusion.5), channel_id=1, source_target_pairs={{0,2},{1,3},{2,0},{3,1},{4,6},{5,7},{6,4},{7,5},{8,10},{9,11},{10,... | collective-permute-start | bytes 221192 | tf_op jit(solution)/shard_map/ppermute | solution.py:300
  54.2 5.2 %collective-permute-start.9 = (bf16[192,128]{1,0:T(8,128)(2,1)S(1)}, bf16[192,128]{1,0:T(8,128)(2,1)S(1)}, u32[]{:S(2)}, u32[]{:S(2)}) collective-permute-start(bf16[192,128]{1,0:T(8,128)(2,1)S(1)} %add_convert_fusion.3), channel_id=1, source_target_pairs={{0,8},{1,9},{2,10},{3,11},{4,12},{5,13},{6,14},{7,15},{8,0},{9,1},... | collective-permute-start | bytes 147464 | tf_op jit(solution)/shard_map/ppermute | solution.py:300
  56.5 4.4 %collective-permute-start.2 = (bf16[288,128]{1,0:T(8,128)(2,1)S(1)}, bf16[288,128]{1,0:T(8,128)(2,1)S(1)}, u32[]{:S(2)}, u32[]{:S(2)}) collective-permute-start(bf16[288,128]{1,0:T(8,128)(2,1)S(1)} %fusion.2), channel_id=1, source_target_pairs={{0,4},{1,5},{2,6},{3,7},{4,0},{5,1},{6,2},{7,3},{8,12},{9,13},{10,... | collective-permute-start | bytes 221192 | tf_op jit(solution)/shard_map/ppermute | solution.py:300
  59.3 4.2 %collective-permute-start.10 = (bf16[192,128]{1,0:T(8,128)(2,1)S(1)}, bf16[192,128]{1,0:T(8,128)(2,1)S(1)}, u32[]{:S(2)}, u32[]{:S(2)}) collective-permute-start(bf16[192,128]{1,0:T(8,128)(2,1)S(1)} %add_convert_fusion.2), channel_id=1, source_target_pairs={{0,2},{1,3},{2,0},{3,1},{4,6},{5,7},{6,4},{7,5},{8,10},{9,11},{10,... | collective-permute-start | bytes 147464 | tf_op jit(solution)/shard_map/ppermute | solution.py:300
  60.9 6.1 %collective-permute-start.3 = (bf16[288,128]{1,0:T(8,128)(2,1)S(1)}, bf16[288,128]{1,0:T(8,128)(2,1)S(1)}, u32[]{:S(2)}, u32[]{:S(2)}) collective-permute-start(bf16[288,128]{1,0:T(8,128)(2,1)S(1)} %add_convert_fusion.1), channel_id=1, source_target_pairs={{0,8},{1,9},{2,10},{3,11},{4,12},{5,13},{6,14},{7,15},{8,0},{9,1},... | collective-permute-start | bytes 221192 | tf_op jit(solution)/shard_map/ppermute | solution.py:300
  63.5 8.1 %collective-permute-start.11 = (bf16[2,192,128]{2,1,0:T(8,128)(2,1)S(1)}, bf16[2,192,128]{2,1,0:T(8,128)(2,1)S(1)}, u32[]{:S(2)}, u32[]{:S(2)}) collective-permute-start(bf16[2,192,128]{2,1,0:T(8,128)(2,1)S(1)} %maximum_select_fusion.5), channel_id=1, source_target_pairs={{0,1},{1,0},{2,3},{3,2},{4,5},{5,4},{6,7},{7,6},{8,9},{9,8},{10,11... | collective-permute-start | bytes 294920 | tf_op jit(solution)/shard_map/ppermute | solution.py:300
  67.1 4.4 %collective-permute-start.4 = (bf16[288,128]{1,0:T(8,128)(2,1)S(1)}, bf16[288,128]{1,0:T(8,128)(2,1)S(1)}, u32[]{:S(2)}, u32[]{:S(2)}) collective-permute-start(bf16[288,128]{1,0:T(8,128)(2,1)S(1)} %add_convert_fusion), channel_id=1, source_target_pairs={{0,2},{1,3},{2,0},{3,1},{4,6},{5,7},{6,4},{7,5},{8,10},{9,11},{10,... | collective-permute-start | bytes 221192 | tf_op jit(solution)/shard_map/ppermute | solution.py:300
  71.5 1.4 %collective-permute-start.5 = (bf16[2,288,128]{2,1,0:T(8,128)(2,1)S(1)}, bf16[2,288,128]{2,1,0:T(8,128)(2,1)S(1)}, u32[]{:S(2)}, u32[]{:S(2)}) collective-permute-start(bf16[2,288,128]{2,1,0:T(8,128)(2,1)S(1)} %maximum_select_fusion.3), channel_id=1, source_target_pairs={{0,1},{1,0},{2,3},{3,2},{4,5},{5,4},{6,7},{7,6},{8,9},{9,8},{10,11... | collective-permute-start | bytes 442376 | tf_op jit(solution)/shard_map/ppermute | solution.py:300

commit v4 on v3

--- a/solution.py
+++ b/solution.py
@@ -232,41 +232,70 @@
     )(dilations, offsets, on_chip(start), on_chip(cotangent), on_chip(w_temporal))
 
 
-def temporal_outer_kernel(length, dil_ref, off_ref, start_ref, mid_ref, dz_ref, out_ref, state):
-    layers, taps, channels = out_ref.shape[:3]
-    rows = start_ref.shape[0]
+def deal(core_ref, whole, own_ref, other_ref):
+    half = own_ref.shape[0]
+    core = core_ref[0]
+    own_ref[...] = whole[pl.ds(pl.multiple_of(core * half, half), half), :]
+    other_ref[...] = whole[pl.ds(pl.multiple_of((1 - core) * half, half), half), :].astype(BF16)
+
+
+def temporal_outer_kernel(
+    length, core_ref, dil_ref, off_ref, start_ref, mid_hbm, dz_hbm, own_ref, other_ref, state, dz, whole, sems
+):
+    layers, taps = off_ref.shape
+    rows, channels = start_ref.shape
     pixels = rows // length
     size = min(1024, rows)
+    copies = []
+    for layer in range(layers):
+        copies.append([pltpu.make_async_copy(dz_hbm.at[layer], dz.at[layer], sems.at[2 * layer])])
+        if layer > 0:
+            target = state.at[layer, pl.ds(rows, rows)]
+            copies[-1].append(
+                pltpu.make_async_copy(mid_hbm.at[layer - 1], target, sems.at[2 * layer + 1])
+            )
+        for copy in copies[-1]:
+            copy.start()
     shifts = row_shifts(dil_ref, off_ref, length, pixels)
     blank = jnp.zeros((rows, channels), BF16)
     for layer in range(layers):
         state[layer, pl.ds(0, rows), :] = blank
-        held = start_ref[...] if layer == 0 else mid_ref[layer - 1]
-        state[layer, pl.ds(rows, rows), :] = held
+        if layer == 0:
+            state[layer, pl.ds(rows, rows), :] = start_ref[...]
+        for copy in copies[layer]:
+            copy.wait()
         total = jnp.zeros((channels, taps * channels), F32)
         for at in range(0, rows, size):
             moved = moved_rows(state, layer, rows + at, [-s for s in shifts[layer]], size, pixels)
-            values = dz_ref[layer, pl.ds(at, size), :]
+            values = dz[layer, pl.ds(at, size), :]
             total += lax.dot_general(values, moved, ROWS, preferred_element_type=F32)
         for tap in range(taps):
-            out_ref[layer, tap] = total[:, tap * channels : (tap + 1) * channels].T
-
-
-def temporal_outer(start, mid, dz, dilations, offsets, length):
+            place = pl.ds((layer * taps + tap) * channels, channels)
+            whole[place, :] = total[:, tap * channels : (tap + 1) * channels].T
+    deal(core_ref, whole, own_ref, other_ref)
+
+
+def temporal_outer(start, mid, dz, dilations, offsets, length, core):
     rows, channels = start.shape
     layers, taps = offsets.shape
+    half = layers * taps * channels // 2
     return pl.pallas_call(
         functools.partial(temporal_outer_kernel, length),
-        in_specs=[SMEM, SMEM, VMEM, VMEM, VMEM],
-        out_specs=VMEM,
-        out_shape=pltpu.VMEM((layers, taps, channels, channels), F32),
-        scratch_shapes=[pltpu.VMEM((layers, 2 * rows, channels), BF16)],
+        in_specs=[SMEM, SMEM, SMEM, VMEM, HBM, HBM],
+        out_specs=[VMEM, VMEM],
+        out_shape=[pltpu.VMEM((half, channels), F32), pltpu.VMEM((half, channels), BF16)],
+        scratch_shapes=[
+            pltpu.VMEM((layers, 2 * rows, channels), BF16),
+            pltpu.VMEM((layers, rows, channels), BF16),
+            pltpu.VMEM((2 * half, channels), F32),
+            pltpu.SemaphoreType.DMA((2 * layers,)),
+        ],
         compiler_params=pltpu.CompilerParams(vmem_limit_bytes=VMEM_LIMIT),
         name="temporal_outer",
-    )(dilations, offsets, on_chip(start), mid, dz)
-
-
-def spatial_outer_kernel(planes, back_ref, out_ref):
+    )(core, dilations, offsets, on_chip(start), in_hbm(mid), in_hbm(dz))
+
+
+def spatial_outer_kernel(core_ref, planes, back_ref, own_ref, other_ref, whole):
     count, height, out_cols, channels = planes.shape
     channels //= 2
     out_rows = (height - 1) // 2
@@ -279,53 +308,83 @@
             moved = jnp.concatenate([planes[frame, 2 * i + a] for i in range(out_rows)], 0)
             totals[a] += dot(both, moved)
     for a in range(3):
-        out_ref[a, 1] = totals[a][:channels, :channels].T
-        out_ref[a, 2] = totals[a][:channels, channels:].T
-        out_ref[a, 0] = totals[a][channels:, channels:].T
-
-
-def spatial_outer(planes, back):
+        products = (
+            totals[a][channels:, channels:],
+            totals[a][:channels, :channels],
+            totals[a][:channels, channels:],
+        )
+        for b, product in enumerate(products):
+            whole[pl.ds((3 * a + b) * channels, channels), :] = product.T
+    deal(core_ref, whole, own_ref, other_ref)
+
+
+def spatial_outer(planes, back, core):
     channels = planes.shape[-1] // 2
+    half = 9 * channels // 2
     return pl.pallas_call(
         spatial_outer_kernel,
-        in_specs=[VMEM, VMEM],
-        out_specs=VMEM,
-        out_shape=pltpu.VMEM((3, 3, channels, channels), F32),
+        in_specs=[SMEM, VMEM, VMEM],
+        out_specs=[VMEM, VMEM],
+        out_shape=[pltpu.VMEM((half, channels), F32), pltpu.VMEM((half, channels), BF16)],
+        scratch_shapes=[pltpu.VMEM((2 * half, channels), F32)],
         compiler_params=pltpu.CompilerParams(vmem_limit_bytes=VMEM_LIMIT),
         name="spatial_outer",
-    )(on_chip(planes), on_chip(back))
-
-
-def swap(x, n, bit):
-    return lax.ppermute(x, "seq", [(i, i ^ (1 << bit)) for i in range(n)])
-
-
-def sum_halves(values, n, halved):
-    me = lax.axis_index("seq")
-    for bit in range(halved):
-        half = values.shape[0] // 2
-        upper = (me >> bit) & 1
-        pieces = values.reshape(2, half, -1)
-        mine = lax.dynamic_index_in_dim(pieces, upper, 0, keepdims=False)
-        other = lax.dynamic_index_in_dim(pieces, 1 - upper, 0, keepdims=False)
-        values = mine + swap(other.astype(BF16), n, bit).astype(F32)
-    return values
+    )(core, on_chip(planes), on_chip(back))
+
+
+def swap(x, n, mask):
+    return lax.ppermute(x, "seq", [(i, i ^ mask) for i in range(n)])
+
+
+def sum_parts(values, n, low, count):
+    me = lax.rem(lax.axis_index("seq") >> low, 1 << count)
+    parts = values.reshape(1 << count, values.shape[0] >> count, -1)
+    total = lax.dynamic_index_in_dim(parts, me, 0, keepdims=False)
+    for peer in range(1, 1 << count):
+        theirs = lax.dynamic_index_in_dim(parts, me ^ peer, 0, keepdims=False)
+        total = total + swap(theirs.astype(BF16), n, peer << low).astype(F32)
+    return total
 
 
 def sum_whole(values, n, bits):
     for bit in bits:
         sent = values.astype(BF16)
-        values = sent.astype(F32) + swap(sent, n, bit).astype(F32)
+        values = sent.astype(F32) + swap(sent, n, 1 << bit).astype(F32)
     return values
 
 
-def gather_halves(values, n, halved):
-    me = lax.axis_index("seq")
-    for bit in reversed(range(halved)):
-        got = swap(values, n, bit)
+def gather_parts(values, n, low, count):
+    me = lax.axis_index("seq") >> low
+    held = [values] + [swap(values, n, peer << low) for peer in range(1, 1 << count)]
+    for bit in range(count):
         upper = (me >> bit) & 1
-        values = jnp.where(upper == 0, jnp.stack([values, got]), jnp.stack([got, values]))
-    return values
+        step = 1 << bit
+        held = [jnp.where(upper == 0, held[q], held[q ^ step]) for q in range(1 << count)]
+    return jnp.concatenate(held, 0)
+
+
+def widen_kernel(core_ref, own_ref, got_ref, spatial_ref, temporal_ref):
+    cut = spatial_ref.shape[2]
+    core = core_ref[0]
+    for place, ref in ((core, own_ref), (1 - core, got_ref)):
+        spatial_ref[place] = ref[:, :cut].astype(F32)
+        temporal_ref[place] = ref[:, cut:].astype(F32)
+
+
+def widen(own, n, core, spatial_rows, temporal_rows):
+    own = own.reshape(-1, spatial_rows + temporal_rows, own.shape[-1])
+    parts, channels = own.shape[0], own.shape[-1]
+    return pl.pallas_call(
+        widen_kernel,
+        in_specs=[SMEM, VMEM, VMEM],
+        out_specs=[VMEM, VMEM],
+        out_shape=[
+            jax.ShapeDtypeStruct((2, parts, spatial_rows, channels), F32),
+            jax.ShapeDtypeStruct((2, parts, temporal_rows, channels), F32),
+        ],
+        compiler_params=pltpu.CompilerParams(vmem_limit_bytes=VMEM_LIMIT),
+        name="widen",
+    )(core, on_chip(own), on_chip(swap(own, n, 1)))
 
 
 def exchange(x):
@@ -336,25 +395,35 @@
     count, height, width, channels = frames.shape
     length, pixels = cotangent.shape[:2]
     bits = n.bit_length() - 1
-    halved = min(2, bits)
     maps, planes = conv(frames, w_spatial, n)
     start = exchange(maps.reshape(n, count * pixels, channels)).reshape(length * pixels, channels)
     features, grad_maps, mid, dz = temporal(
         start, cotangent.reshape(length * pixels, channels), w_temporal, dilations, offsets, length
     )
     back = exchange(grad_maps.reshape(n, count * pixels, channels))
-    grad_temporal = temporal_outer(start, mid, dz, dilations, offsets, length)
-    of_temporal = sum_halves(grad_temporal.reshape(-1, channels), n, halved)
-    grad_spatial = spatial_outer(planes, back.reshape(n, count, pixels, channels))
-    of_temporal = sum_whole(of_temporal, n, range(halved, bits))
-    of_temporal = gather_halves(of_temporal.astype(BF16), n, halved).astype(F32)
-    of_spatial = sum_halves(grad_spatial.reshape(-1, channels), n, halved)
-    of_spatial = sum_whole(of_spatial, n, range(halved, bits))
-    of_spatial = gather_halves(of_spatial.astype(BF16), n, halved).astype(F32)
+    core = lax.rem(lax.axis_index("seq"), 2).astype(jnp.int32).reshape(1)
+    size = min(2, bits - 1)
+    one = min(1, bits - 1)
+
+    def add_cores(own, other):
+        return own + swap(other, n, 1).astype(F32)
+
+    of_temporal = sum_parts(add_cores(*temporal_outer(start, mid, dz, dilations, offsets, length, core)), n, 1, one)
+    of_temporal = sum_whole(of_temporal, n, range(1 + one, min(2 + one, bits)))
+    own, other = spatial_outer(planes, back.reshape(n, count, pixels, channels), core)
+    of_spatial = add_cores(own, other)
+    of_spatial, of_temporal = lax.optimization_barrier((of_spatial, of_temporal))
+    of_spatial = sum_parts(of_spatial, n, 1, size)
+    of_temporal = sum_whole(of_temporal, n, range(min(2 + one, bits), bits)).astype(BF16)
+    of_temporal = gather_parts(gather_parts(of_temporal, n, 1, one), n, 0, 1)
+    of_temporal = of_temporal.astype(F32).reshape(w_temporal.shape)
+    of_spatial = sum_whole(of_spatial, n, range(1 + size, bits)).astype(BF16)
+    of_spatial = gather_parts(gather_parts(of_spatial, n, 1, size), n, 0, 1)
+    of_spatial = of_spatial.astype(F32).reshape(w_spatial.shape)
     return (
         features.reshape(length, pixels, channels),
-        of_spatial.reshape(grad_spatial.shape),
-        of_temporal.reshape(grad_temporal.shape),
+        of_spatial.reshape(w_spatial.shape),
+        of_temporal.reshape(w_temporal.shape),
     )
 
 

time: 74.3 us -> 72.6 us (0.977)
  starting transfers between devices: 15.4 us -> 19.4 us
  local copies, waits for them, and re-layouts: 3.09 us -> 0.06 us
  waiting for transfers between devices: 19.6 us -> 16.6 us
  Pallas kernels: 10.5 us -> 11.8 us
  other arithmetic: 2.82 us -> 1.97 us
    ppermute x12 -> x15, starting transfers between devices: 11.3 us -> 15.3 us  [swap(): return lax.ppermute(x, 'seq', [(i, i ^ mask) for i in range(n)])]
    unnamed x14 -> x8, local copies, waits for them, and re-layouts: 3.02 us -> 0.02 us
    ppermute x12 -> x15, waiting for transfers between devices: 14.1 us -> 12.4 us  [swap(): return lax.ppermute(x, 'seq', [(i, i ^ mask) for i in range(n)])]
    all_to_all x1, waiting for transfers between devices: 5.5 us -> 4.16 us  [exchange(): return lax.all_to_all(x, 'seq', split_axis=0, concat_axis=0, tiled=True)]
    pallas_call x1, Pallas kernels: 1.59 us -> 2.86 us  [temporal_outer(): pl.pallas_call(functools.partial(temporal_outer_kernel, length), in_specs...]
    add x2 -> x3, other arithmetic: 0.97 us -> 0.06 us  [the longest x2 0.05 us: add_cores(): return own + swap(other, n, 1).astype(F32)]
  transfers between devices with their start and end apart: 13 -> 16, of which waited for: 9 -> 10; matrix products, arithmetic and copies ran while one was open for 3% -> 1% of each run, Pallas kernels for 4% -> 6%
where the time goes in v4:
time: 72.6 us; the launch traced here: 72.3 us
  blocking collectives  21.6 us (30%)
  starting transfers between devices  19.4 us (27%)
  waiting for transfers between devices  16.6 us (23%)
  Pallas kernels  11.8 us (16%)
  other arithmetic  1.97 us (3%)
  between operations  0.87 us (1%)
    all_to_all x1, blocking collectives, exchange(): return lax.all_to_all(x, 'seq', split_axis=0, concat_axis=0, tiled=True)  21.6 us
    ppermute x15, starting transfers between devices, swap(): return lax.ppermute(x, 'seq', [(i, i ^ mask) for i in range(n)])  15.3 us
    ppermute x15, waiting for transfers between devices, swap(): return lax.ppermute(x, 'seq', [(i, i ^ mask) for i in range(n)])  12.4 us
    pallas_call x1, Pallas kernels, temporal(): pl.pallas_call(functools.partial(temporal_kernel, length), in_specs=[SMEM...  4.37 us
    all_to_all x1, waiting for transfers between devices, exchange(): return lax.all_to_all(x, 'seq', split_axis=0, concat_axis=0, tiled=True)  4.16 us
    all_to_all x1, starting transfers between devices, exchange(): return lax.all_to_all(x, 'seq', split_axis=0, concat_axis=0, tiled=True)  4.11 us
    pallas_call x1, Pallas kernels, conv(): pl.pallas_call(functools.partial(conv_kernel, bands=bands), in_specs=[HBM...  3.37 us
    pallas_call x1, Pallas kernels, temporal_outer(): pl.pallas_call(functools.partial(temporal_outer_kernel, length), in_specs...  2.86 us
  transfers between devices with their start and end apart: 16, of which 10 were waited for; matrix products, arithmetic and copies ran while one was open for 1% of the time, Pallas kernels for 6%

profile of v4, /device:TPU:0, one launch (start us, length us, event | category | flops | bytes accessed | tf_op | source)
XLA Modules:
  0.0 72.3 jit_solution(9536903047664205101)
XLA Ops:
  0.7 3.4 %conv.1 = (bf16[16,2,64,128]{3,2,1,0:T(8,128)(2,1)S(1)}, bf16[2,33,64,256]{3,2,1,0:T(8,128)(2,1)S(1)}) custom-call(bf16[2,32,128,128]{3,2,1,0:T(8,128)(2,1)} %x_hbm.1, bf16[3,3,128,128]{3,2,1,0:T(8,128)(2,1)} %w_hbm.1), custom_call_target="tpu_custom_call" | custom-call | tf_op jit(solution)/shard_map/conv/pallas_call | solution.py:103
  4.0 21.6 %all_to_all.10 = bf16[16,128,128]{2,1,0:T(8,128)(2,1)S(1)} all-to-all(bf16[16,128,128]{2,1,0:T(8,128)(2,1)S(1)} %bitcast.36), channel_id=1, replica_groups=mesh['groups'=2,'seq'=16] {'seq'}, dimensions={0} | all-to-all | bytes 1048576 | tf_op jit(solution)/shard_map/all_to_all | solution.py:391
  25.7 4.4 %temporal.1 = (bf16[2048,128]{1,0:T(8,128)(2,1)}, bf16[2048,128]{1,0:T(8,128)(2,1)}, bf16[1,2048,128]{2,1,0:T(8,128)(2,1)}, bf16[2,2048,128]{2,1,0:T(8,128)(2,1)}) custom-call(s32[2]{0:T(128)S(1)} %copy-done.3, s32[2,3]{1,0:T(2,128)S(1)} %copy-done.2, bf16[2048,128]{1,0:T(8,128)(2,1)S(1)} %bitcast.33, bf16[2048,128]{1,0:T(8,128)(2,1)S(1)} %bitcast.37, ...), custom_call_target="tpu_custom_call" | custom-call | tf_op jit(solution)/shard_map/temporal/pallas_call | solution.py:211
  30.1 4.1 %all-to-all-start.1 = ((bf16[16,128,128]{2,1,0:T(8,128)(2,1)}), bf16[16,128,128]{2,1,0:T(8,128)(2,1)S(1)}, u32[]{:S(2)}, u32[]{:S(2)}) async-start(bf16[16,128,128]{2,1,0:T(8,128)(2,1)} %bitcast.44), calls=%async_computation.1 | async-start | bytes 1048576 | tf_op jit(solution)/shard_map/all_to_all | solution.py:391
  34.2 2.9 %temporal_outer.1 = (f32[384,128]{1,0:T(8,128)S(1)}, bf16[384,128]{1,0:T(8,128)(2,1)S(1)}) custom-call(s32[1]{0:T(128)} %bitcast.4.core_ref, s32[2]{0:T(128)S(1)} %copy-done.3, s32[2,3]{1,0:T(2,128)S(1)} %copy-done.2, bf16[2048,128]{1,0:T(8,128)(2,1)S(1)} %bitcast.34, bf16[1,2048,128]{2,1,0:T(8,128)(2,1)} %get-tuple-element.21.mid_hbm, ...), custom_call_target="tpu_custom_call" | custom-call | tf_op jit(solution)/shard_map/temporal_outer/pallas_call | solution.py:282
  37.1 0.5 collective-permute-start.1
  37.5 0.9 %collective-permute-done.1 = bf16[384,128]{1,0:T(8,128)(2,1)S(1)} collective-permute-done((bf16[384,128]{1,0:T(8,128)(2,1)S(1)}, bf16[384,128]{1,0:T(8,128)(2,1)S(1)}, u32[]{:S(2)}, u32[]{:S(2)}) %collective-permute-start.1) | collective-permute-done | bytes 98336 | tf_op jit(solution)/shard_map/ppermute | solution.py:336
  38.5 1.9 %collective-permute-start.2 = (bf16[192,128]{1,0:T(8,128)(2,1)S(1)}, bf16[192,128]{1,0:T(8,128)(2,1)S(1)}, u32[]{:S(2)}, u32[]{:S(2)}) collective-permute-start(bf16[192,128]{1,0:T(8,128)(2,1)S(1)} %fusion.4), channel_id=1, source_target_pairs={{0,2},{1,3},{2,0},{3,1},{4,6},{5,7},{6,4},{7,5},{8,10},{9,11},{10,... | collective-permute-start | bytes 147464 | tf_op jit(solution)/shard_map/ppermute | solution.py:336
  40.5 2.6 %collective-permute-done.2 = bf16[192,128]{1,0:T(8,128)(2,1)S(1)} collective-permute-done((bf16[192,128]{1,0:T(8,128)(2,1)S(1)}, bf16[192,128]{1,0:T(8,128)(2,1)S(1)}, u32[]{:S(2)}, u32[]{:S(2)}) %collective-permute-start.2) | collective-permute-done | bytes 49184 | tf_op jit(solution)/shard_map/ppermute | solution.py:336
  43.1 1.8 %collective-permute-start.3 = (bf16[192,128]{1,0:T(8,128)(2,1)S(1)}, bf16[192,128]{1,0:T(8,128)(2,1)S(1)}, u32[]{:S(2)}, u32[]{:S(2)}) collective-permute-start(bf16[192,128]{1,0:T(8,128)(2,1)S(1)} %fusion), channel_id=1, source_target_pairs={{0,4},{1,5},{2,6},{3,7},{4,0},{5,1},{6,2},{7,3},{8,12},{9,13},{10,... | collective-permute-start | bytes 147464 | tf_op jit(solution)/shard_map/ppermute | solution.py:336
  44.9 4.2 %all-to-all-done.1 = bf16[16,128,128]{2,1,0:T(8,128)(2,1)S(1)} async-done(((bf16[16,128,128]{2,1,0:T(8,128)(2,1)}), bf16[16,128,128]{2,1,0:T(8,128)(2,1)S(1)}, u32[]{:S(2)}, u32[]{:S(2)}) %all-to-all-start.1) | async-done | bytes 524320 | tf_op jit(solution)/shard_map/all_to_all | solution.py:391
  49.0 1.2 %spatial_outer.1 = (f32[576,128]{1,0:T(8,128)S(1)}, bf16[576,128]{1,0:T(8,128)(2,1)S(1)}) custom-call(s32[1]{0:T(128)} %bitcast.4.core_ref, bf16[2,33,64,256]{3,2,1,0:T(8,128)(2,1)S(1)} %get-tuple-element.17.planes, bf16[16,2,64,128]{3,2,1,0:T(8,128)(2,1)S(1)} %bitcast.35), custom_call_target="tpu_custom_call" | custom-call | tf_op jit(solution)/shard_map/spatial_outer/pallas_call | solution.py:324
  50.2 0.1 collective-permute-start
  50.3 1.3 %collective-permute-done = bf16[576,128]{1,0:T(8,128)(2,1)S(1)} collective-permute-done((bf16[576,128]{1,0:T(8,128)(2,1)S(1)}, bf16[576,128]{1,0:T(8,128)(2,1)S(1)}, u32[]{:S(2)}, u32[]{:S(2)}) %collective-permute-start) | collective-permute-done | bytes 147488 | tf_op jit(solution)/shard_map/ppermute | solution.py:336
  51.7 0.5 collective-permute-start.4
  52.2 1.6 %collective-permute-start.5 = (bf16[144,128]{1,0:T(8,128)(2,1)S(1)}, bf16[144,128]{1,0:T(8,128)(2,1)S(1)}, u32[]{:S(2)}, u32[]{:S(2)}) collective-permute-start(bf16[144,128]{1,0:T(8,128)(2,1)S(1)} %get-tuple-element.31), channel_id=1, source_target_pairs={{0,4},{1,5},{2,6},{3,7},{4,0},{5,1},{6,2},{7,3},{8,12},{9,13},{10,... | collective-permute-start | bytes 110600 | tf_op jit(solution)/shard_map/ppermute | solution.py:336
  53.8 1.5 %collective-permute-start.6 = (bf16[144,128]{1,0:T(8,128)(2,1)S(1)}, bf16[144,128]{1,0:T(8,128)(2,1)S(1)}, u32[]{:S(2)}, u32[]{:S(2)}) collective-permute-start(bf16[144,128]{1,0:T(8,128)(2,1)S(1)} %get-tuple-element.30), channel_id=1, source_target_pairs={{0,6},{1,7},{2,4},{3,5},{4,2},{5,3},{6,0},{7,1},{8,14},{9,15},{10,... | collective-permute-start | bytes 110600 | tf_op jit(solution)/shard_map/ppermute | solution.py:336
  55.3 1.9 %collective-permute-start.12 = (bf16[192,128]{1,0:T(8,128)(2,1)S(1)}, bf16[192,128]{1,0:T(8,128)(2,1)S(1)}, u32[]{:S(2)}, u32[]{:S(2)}) collective-permute-start(bf16[192,128]{1,0:T(8,128)(2,1)S(1)} %convert_add_fusion.2), channel_id=1, source_target_pairs={{0,8},{1,9},{2,10},{3,11},{4,12},{5,13},{6,14},{7,15},{8,0},{9,1},... | collective-permute-start | bytes 147464 | tf_op jit(solution)/shard_map/ppermute | solution.py:336
  57.1 1.9 %collective-permute-done.6 = bf16[144,128]{1,0:T(8,128)(2,1)S(1)} collective-permute-done((bf16[144,128]{1,0:T(8,128)(2,1)S(1)}, bf16[144,128]{1,0:T(8,128)(2,1)S(1)}, u32[]{:S(2)}, u32[]{:S(2)}) %collective-permute-start.6) | collective-permute-done | bytes 36896 | tf_op jit(solution)/shard_map/ppermute | solution.py:336
  59.1 1.6 %collective-permute-start.7 = (bf16[144,128]{1,0:T(8,128)(2,1)S(1)}, bf16[144,128]{1,0:T(8,128)(2,1)S(1)}, u32[]{:S(2)}, u32[]{:S(2)}) collective-permute-start(bf16[144,128]{1,0:T(8,128)(2,1)S(1)} %fusion.3), channel_id=1, source_target_pairs={{0,8},{1,9},{2,10},{3,11},{4,12},{5,13},{6,14},{7,15},{8,0},{9,1},... | collective-permute-start | bytes 110600 | tf_op jit(solution)/shard_map/ppermute | solution.py:336
  60.7 0.3 collective-permute-start.13
  61.0 3.2 %collective-permute-done.7 = bf16[144,128]{1,0:T(8,128)(2,1)S(1)} collective-permute-done((bf16[144,128]{1,0:T(8,128)(2,1)S(1)}, bf16[144,128]{1,0:T(8,128)(2,1)S(1)}, u32[]{:S(2)}, u32[]{:S(2)}) %collective-permute-start.7) | collective-permute-done | bytes 36896 | tf_op jit(solution)/shard_map/ppermute | solution.py:336
  64.2 1.3 %collective-permute-start.10 = (bf16[144,128]{1,0:T(8,128)(2,1)S(1)}, bf16[144,128]{1,0:T(8,128)(2,1)S(1)}, u32[]{:S(2)}, u32[]{:S(2)}) collective-permute-start(bf16[144,128]{1,0:T(8,128)(2,1)S(1)} %add_convert_fusion.1), channel_id=1, source_target_pairs={{0,6},{1,7},{2,4},{3,5},{4,2},{5,3},{6,0},{7,1},{8,14},{9,15},{10,... | collective-permute-start | bytes 110600 | tf_op jit(solution)/shard_map/ppermute | solution.py:336
  65.4 0.4 collective-permute-start.8
  65.9 1.8 %collective-permute-start.9 = (bf16[144,128]{1,0:T(8,128)(2,1)S(1)}, bf16[144,128]{1,0:T(8,128)(2,1)S(1)}, u32[]{:S(2)}, u32[]{:S(2)}) collective-permute-start(bf16[144,128]{1,0:T(8,128)(2,1)S(1)} %add_convert_fusion.1), channel_id=1, source_target_pairs={{0,4},{1,5},{2,6},{3,7},{4,0},{5,1},{6,2},{7,3},{8,12},{9,13},{10,... | collective-permute-start | bytes 110600 | tf_op jit(solution)/shard_map/ppermute | solution.py:336
  67.8 1.3 %collective-permute-done.10 = bf16[144,128]{1,0:T(8,128)(2,1)S(1)} collective-permute-done((bf16[144,128]{1,0:T(8,128)(2,1)S(1)}, bf16[144,128]{1,0:T(8,128)(2,1)S(1)}, u32[]{:S(2)}, u32[]{:S(2)}) %collective-permute-start.10) | collective-permute-done | bytes 36896 | tf_op jit(solution)/shard_map/ppermute | solution.py:336
  69.1 0.4 collective-permute-done.8
  69.5 0.3 collective-permute-done.9
  70.0 0.8 %convert.3 = f32[2,3,128,128]{3,2,1,0:T(8,128)} convert(bf16[2,3,128,128]{3,2,1,0:T(8,128)(2,1)S(1)} %bitcast.39) | non-fusion elementwise | flops 98304 | bytes 589824 | tf_op jit(solution)/shard_map/convert_element_type | solution.py:419
  70.8 0.5 collective-permute-done.11
  71.3 0.1 broadcast_select_fusion.1
  71.4 0.9 %convert.2 = f32[3,3,128,128]{3,2,1,0:T(8,128)} convert(bf16[3,3,128,128]{3,2,1,0:T(8,128)(2,1)S(1)} %bitcast.38) | non-fusion elementwise | flops 147456 | bytes 884736 | tf_op jit(solution)/shard_map/convert_element_type | solution.py:422
  (32 shorter events, 0.5 us)
Async XLA Ops:
  0.6 25.0 %copy-start = (bf16[32,64,128]{2,1,0:T(8,128)(2,1)S(1)}, bf16[32,64,128]{2,1,0:T(8,128)(2,1)}, u32[]{:S(2)}) copy-start(bf16[32,64,128]{2,1,0:T(8,128)(2,1)} %param.11) | copy-start | bytes 1572868
  0.6 25.0 %copy-start.2 = (s32[2,3]{1,0:T(2,128)S(1)}, s32[2,3]{1,0:T(2,128)}, u32[]{:S(2)}) copy-start(s32[2,3]{1,0:T(2,128)} %off_ref.3) | copy-start | bytes 76
  0.7 25.0 %copy-start.1 = (bf16[2,3,128,128]{3,2,1,0:T(8,128)(2,1)S(1)}, bf16[2,3,128,128]{3,2,1,0:T(8,128)(2,1)}, u32[]{:S(2)}) copy-start(bf16[2,3,128,128]{3,2,1,0:T(8,128)(2,1)} %w_ref.1) | copy-start | bytes 589828
  0.7 25.0 %copy-start.3 = (s32[2]{0:T(128)S(1)}, s32[2]{0:T(128)}, u32[]{:S(2)}) copy-start(s32[2]{0:T(128)} %dil_ref.3) | copy-start | bytes 28
  30.1 19.0 %all-to-all-start.1 = ((bf16[16,128,128]{2,1,0:T(8,128)(2,1)}), bf16[16,128,128]{2,1,0:T(8,128)(2,1)S(1)}, u32[]{:S(2)}, u32[]{:S(2)}) async-start(bf16[16,128,128]{2,1,0:T(8,128)(2,1)} %bitcast.44), calls=%async_computation.1 | async-start | bytes 1048576 | tf_op jit(solution)/shard_map/all_to_all | solution.py:391
  37.1 1.4 %collective-permute-start.1 = (bf16[384,128]{1,0:T(8,128)(2,1)S(1)}, bf16[384,128]{1,0:T(8,128)(2,1)S(1)}, u32[]{:S(2)}, u32[]{:S(2)}) collective-permute-start(bf16[384,128]{1,0:T(8,128)(2,1)S(1)} %get-tuple-element.24), channel_id=1, source_target_pairs={{0,1},{1,0},{2,3},{3,2},{4,5},{5,4},{6,7},{7,6},{8,9},{9,8},{10,11... | collective-permute-start | bytes 294920 | tf_op jit(solution)/shard_map/ppermute | solution.py:336
  38.5 4.5 %collective-permute-start.2 = (bf16[192,128]{1,0:T(8,128)(2,1)S(1)}, bf16[192,128]{1,0:T(8,128)(2,1)S(1)}, u32[]{:S(2)}, u32[]{:S(2)}) collective-permute-start(bf16[192,128]{1,0:T(8,128)(2,1)S(1)} %fusion.4), channel_id=1, source_target_pairs={{0,2},{1,3},{2,0},{3,1},{4,6},{5,7},{6,4},{7,5},{8,10},{9,11},{10,... | collective-permute-start | bytes 147464 | tf_op jit(solution)/shard_map/ppermute | solution.py:336
  43.1 7.2 %collective-permute-start.3 = (bf16[192,128]{1,0:T(8,128)(2,1)S(1)}, bf16[192,128]{1,0:T(8,128)(2,1)S(1)}, u32[]{:S(2)}, u32[]{:S(2)}) collective-permute-start(bf16[192,128]{1,0:T(8,128)(2,1)S(1)} %fusion), channel_id=1, source_target_pairs={{0,4},{1,5},{2,6},{3,7},{4,0},{5,1},{6,2},{7,3},{8,12},{9,13},{10,... | collective-permute-start | bytes 147464 | tf_op jit(solution)/shard_map/ppermute | solution.py:336
  50.2 1.4 %collective-permute-start = (bf16[576,128]{1,0:T(8,128)(2,1)S(1)}, bf16[576,128]{1,0:T(8,128)(2,1)S(1)}, u32[]{:S(2)}, u32[]{:S(2)}) collective-permute-start(bf16[576,128]{1,0:T(8,128)(2,1)S(1)} %get-tuple-element.20), channel_id=1, source_target_pairs={{0,1},{1,0},{2,3},{3,2},{4,5},{5,4},{6,7},{7,6},{8,9},{9,8},{10,11... | collective-permute-start | bytes 442376 | tf_op jit(solution)/shard_map/ppermute | solution.py:336
  51.7 5.4 %collective-permute-start.4 = (bf16[144,128]{1,0:T(8,128)(2,1)S(1)}, bf16[144,128]{1,0:T(8,128)(2,1)S(1)}, u32[]{:S(2)}, u32[]{:S(2)}) collective-permute-start(bf16[144,128]{1,0:T(8,128)(2,1)S(1)} %get-tuple-element.29), channel_id=1, source_target_pairs={{0,2},{1,3},{2,0},{3,1},{4,6},{5,7},{6,4},{7,5},{8,10},{9,11},{10,... | collective-permute-start | bytes 110600 | tf_op jit(solution)/shard_map/ppermute | solution.py:336
  52.2 4.9 %collective-permute-start.5 = (bf16[144,128]{1,0:T(8,128)(2,1)S(1)}, bf16[144,128]{1,0:T(8,128)(2,1)S(1)}, u32[]{:S(2)}, u32[]{:S(2)}) collective-permute-start(bf16[144,128]{1,0:T(8,128)(2,1)S(1)} %get-tuple-element.31), channel_id=1, source_target_pairs={{0,4},{1,5},{2,6},{3,7},{4,0},{5,1},{6,2},{7,3},{8,12},{9,13},{10,... | collective-permute-start | bytes 110600 | tf_op jit(solution)/shard_map/ppermute | solution.py:336
  53.8 5.3 %collective-permute-start.6 = (bf16[144,128]{1,0:T(8,128)(2,1)S(1)}, bf16[144,128]{1,0:T(8,128)(2,1)S(1)}, u32[]{:S(2)}, u32[]{:S(2)}) collective-permute-start(bf16[144,128]{1,0:T(8,128)(2,1)S(1)} %get-tuple-element.30), channel_id=1, source_target_pairs={{0,6},{1,7},{2,4},{3,5},{4,2},{5,3},{6,0},{7,1},{8,14},{9,15},{10,... | collective-permute-start | bytes 110600 | tf_op jit(solution)/shard_map/ppermute | solution.py:336
  55.3 5.4 %collective-permute-start.12 = (bf16[192,128]{1,0:T(8,128)(2,1)S(1)}, bf16[192,128]{1,0:T(8,128)(2,1)S(1)}, u32[]{:S(2)}, u32[]{:S(2)}) collective-permute-start(bf16[192,128]{1,0:T(8,128)(2,1)S(1)} %convert_add_fusion.2), channel_id=1, source_target_pairs={{0,8},{1,9},{2,10},{3,11},{4,12},{5,13},{6,14},{7,15},{8,0},{9,1},... | collective-permute-start | bytes 147464 | tf_op jit(solution)/shard_map/ppermute | solution.py:336
  59.1 5.0 %collective-permute-start.7 = (bf16[144,128]{1,0:T(8,128)(2,1)S(1)}, bf16[144,128]{1,0:T(8,128)(2,1)S(1)}, u32[]{:S(2)}, u32[]{:S(2)}) collective-permute-start(bf16[144,128]{1,0:T(8,128)(2,1)S(1)} %fusion.3), channel_id=1, source_target_pairs={{0,8},{1,9},{2,10},{3,11},{4,12},{5,13},{6,14},{7,15},{8,0},{9,1},... | collective-permute-start | bytes 110600 | tf_op jit(solution)/shard_map/ppermute | solution.py:336
  60.7 7.0 %collective-permute-start.13 = (bf16[192,128]{1,0:T(8,128)(2,1)S(1)}, bf16[192,128]{1,0:T(8,128)(2,1)S(1)}, u32[]{:S(2)}, u32[]{:S(2)}) collective-permute-start(bf16[192,128]{1,0:T(8,128)(2,1)S(1)} %add_convert_fusion), channel_id=1, source_target_pairs={{0,2},{1,3},{2,0},{3,1},{4,6},{5,7},{6,4},{7,5},{8,10},{9,11},{10,... | collective-permute-start | bytes 147464 | tf_op jit(solution)/shard_map/ppermute | solution.py:336
  64.2 4.9 %collective-permute-start.10 = (bf16[144,128]{1,0:T(8,128)(2,1)S(1)}, bf16[144,128]{1,0:T(8,128)(2,1)S(1)}, u32[]{:S(2)}, u32[]{:S(2)}) collective-permute-start(bf16[144,128]{1,0:T(8,128)(2,1)S(1)} %add_convert_fusion.1), channel_id=1, source_target_pairs={{0,6},{1,7},{2,4},{3,5},{4,2},{5,3},{6,0},{7,1},{8,14},{9,15},{10,... | collective-permute-start | bytes 110600 | tf_op jit(solution)/shard_map/ppermute | solution.py:336
  65.4 4.1 %collective-permute-start.8 = (bf16[144,128]{1,0:T(8,128)(2,1)S(1)}, bf16[144,128]{1,0:T(8,128)(2,1)S(1)}, u32[]{:S(2)}, u32[]{:S(2)}) collective-permute-start(bf16[144,128]{1,0:T(8,128)(2,1)S(1)} %add_convert_fusion.1), channel_id=1, source_target_pairs={{0,2},{1,3},{2,0},{3,1},{4,6},{5,7},{6,4},{7,5},{8,10},{9,11},{10,... | collective-permute-start | bytes 110600 | tf_op jit(solution)/shard_map/ppermute | solution.py:336
  65.9 4.0 %collective-permute-start.9 = (bf16[144,128]{1,0:T(8,128)(2,1)S(1)}, bf16[144,128]{1,0:T(8,128)(2,1)S(1)}, u32[]{:S(2)}, u32[]{:S(2)}) collective-permute-start(bf16[144,128]{1,0:T(8,128)(2,1)S(1)} %add_convert_fusion.1), channel_id=1, source_target_pairs={{0,4},{1,5},{2,6},{3,7},{4,0},{5,1},{6,2},{7,3},{8,12},{9,13},{10,... | collective-permute-start | bytes 110600 | tf_op jit(solution)/shard_map/ppermute | solution.py:336
  67.7 2.2 %collective-permute-start.14 = (bf16[384,128]{1,0:T(8,128)(2,1)S(1)}, bf16[384,128]{1,0:T(8,128)(2,1)S(1)}, u32[]{:S(2)}, u32[]{:S(2)}) collective-permute-start(bf16[384,128]{1,0:T(8,128)(2,1)S(1)} %pad_maximum_fusion.3), channel_id=1, source_target_pairs={{0,1},{1,0},{2,3},{3,2},{4,5},{5,4},{6,7},{7,6},{8,9},{9,8},{10,11... | collective-permute-start | bytes 294920 | tf_op jit(solution)/shard_map/ppermute | solution.py:336
  69.9 1.4 %collective-permute-start.11 = (bf16[576,128]{1,0:T(8,128)(2,1)S(1)}, bf16[576,128]{1,0:T(8,128)(2,1)S(1)}, u32[]{:S(2)}, u32[]{:S(2)}) collective-permute-start(bf16[576,128]{1,0:T(8,128)(2,1)S(1)} %pad_maximum_fusion.2), channel_id=1, source_target_pairs={{0,1},{1,0},{2,3},{3,2},{4,5},{5,4},{6,7},{7,6},{8,9},{9,8},{10,11... | collective-permute-start | bytes 442376 | tf_op jit(solution)/shard_map/ppermute | solution.py:336

commit v5 on v4

--- a/solution.py
+++ b/solution.py
@@ -133,16 +133,18 @@
     ]
 
 
-def moved_rows(ref, layer, at, shifts, size, pixels):
+def moved_rows(ref, at, shifts, size, pixels):
     return jnp.concatenate(
-        [ref[layer, pl.ds(pl.multiple_of(at + s, pixels), size), :] for s in shifts], 1
+        [ref[pl.ds(pl.multiple_of(at + s, pixels), size), :] for s in shifts], 1
     )
 
 
 def temporal_kernel(
-    length, dil_ref, off_ref, start_ref, cot_ref, w_ref, feat_hbm, back_hbm, mid_hbm, dz_hbm, state, dz, act, grad, feat, back, sems
+    length, dil_ref, off_ref, start_ref, cot_ref, w_ref, feat_hbm, back_hbm, mid_hbm, dz_hbm, *scratch
 ):
     layers, taps, channels = w_ref.shape[:3]
+    state, dz = scratch[:layers], scratch[layers : 2 * layers]
+    act, grad, feat, back, sems = scratch[2 * layers :]
     rows = start_ref.shape[0]
     pixels = rows // length
     size = min(1024, rows)
@@ -156,9 +158,9 @@
 
     blank = jnp.zeros((rows, channels), BF16)
     for layer in range(layers):
-        state[layer, pl.ds(0, rows), :] = blank
-        dz[layer, pl.ds(rows, rows), :] = blank
-    state[0, pl.ds(rows, rows), :] = start_ref[...]
+        state[layer][pl.ds(0, rows), :] = blank
+        dz[layer][pl.ds(rows, rows), :] = blank
+    state[0][pl.ds(rows, rows), :] = start_ref[...]
     down = [w_ref[layer].reshape(taps * channels, channels) for layer in range(layers)]
     up = [
         jnp.concatenate([w_ref[layer, tap].T for tap in range(taps)], 0)
@@ -168,22 +170,22 @@
         last = layer == layers - 1
         for at in starts:
             here = pl.ds(at, size)
-            moved = moved_rows(state, layer, rows + at, [-s for s in shifts[layer]], size, pixels)
+            moved = moved_rows(state[layer], rows + at, [-s for s in shifts[layer]], size, pixels)
             activ = jnp.tanh(dot(moved, down[layer]))
-            held = state[layer, pl.ds(rows + at, size), :].astype(F32)
+            held = state[layer][pl.ds(rows + at, size), :].astype(F32)
             following = (held + activ).astype(BF16)
             slope = 1.0 - activ * activ
             if last:
                 feat[here, :] = following
-                dz[layer, here, :] = (cot_ref[here, :].astype(F32) * slope).astype(BF16)
+                dz[layer][here, :] = (cot_ref[here, :].astype(F32) * slope).astype(BF16)
             else:
-                state[layer + 1, pl.ds(rows + at, size), :] = following
+                state[layer + 1][pl.ds(rows + at, size), :] = following
                 act[layer, here, :] = slope
         if last:
             send(feat, feat_hbm)
-            send(dz.at[layer, pl.ds(0, rows)], dz_hbm.at[layer])
+            send(dz[layer].at[pl.ds(0, rows)], dz_hbm.at[layer])
         else:
-            send(state.at[layer + 1, pl.ds(rows, rows)], mid_hbm.at[layer])
+            send(state[layer + 1].at[pl.ds(rows, rows)], mid_hbm.at[layer])
     for layer in reversed(range(layers)):
         for at in starts:
             here = pl.ds(at, size)
@@ -191,15 +193,15 @@
                 before = cot_ref[here, :].astype(F32)
             else:
                 before = grad[here, :]
-            after = before + dot(moved_rows(dz, layer, at, shifts[layer], size, pixels), up[layer])
+            after = before + dot(moved_rows(dz[layer], at, shifts[layer], size, pixels), up[layer])
             if layer > 0:
                 grad[here, :] = after
-                dz[layer - 1, here, :] = (after * act[layer - 1, here, :]).astype(BF16)
+                dz[layer - 1][here, :] = (after * act[layer - 1, here, :]).astype(BF16)
             else:
                 back[here, :] = after.astype(BF16)
                 send(back.at[here], back_hbm.at[here])
         if layer > 0:
-            send(dz.at[layer - 1, pl.ds(0, rows)], dz_hbm.at[layer - 1])
+            send(dz[layer - 1].at[pl.ds(0, rows)], dz_hbm.at[layer - 1])
     for copy in sent:
         copy.wait()
 
@@ -218,9 +220,8 @@
             pltpu.HBM((max(layers - 1, 1), rows, channels), BF16),
             pltpu.HBM((layers, rows, channels), BF16),
         ],
-        scratch_shapes=[
-            pltpu.VMEM((layers, 2 * rows, channels), BF16),
-            pltpu.VMEM((layers, 2 * rows, channels), BF16),
+        scratch_shapes=[pltpu.VMEM((2 * rows, channels), BF16)] * (2 * layers)
+        + [
             pltpu.VMEM((max(layers - 1, 1), rows, channels), F32),
             pltpu.VMEM((rows, channels), F32),
             pltpu.VMEM((rows, channels), BF16),
@@ -266,7 +267,7 @@
             copy.wait()
         total = jnp.zeros((channels, taps * channels), F32)
         for at in range(0, rows, size):
-            moved = moved_rows(state, layer, rows + at, [-s for s in shifts[layer]], size, pixels)
+            moved = moved_rows(state.at[layer], rows + at, [-s for s in shifts[layer]], size, pixels)
             values = dz[layer, pl.ds(at, size), :]
             total += lax.dot_general(values, moved, ROWS, preferred_element_type=F32)
         for tap in range(taps):

time: 72.6 us -> 72 us (level)
  no operation moved by 1% of the time
where the time goes in v5:
time: 72 us; the launch traced here: 71.7 us
  blocking collectives  21.6 us (30%)
  starting transfers between devices  19.4 us (27%)
  waiting for transfers between devices  16.6 us (23%)
  Pallas kernels  11.2 us (16%)
  other arithmetic  1.97 us (3%)
  between operations  0.87 us (1%)
    all_to_all x1, blocking collectives, exchange(): return lax.all_to_all(x, 'seq', split_axis=0, concat_axis=0, tiled=True)  21.6 us
    ppermute x15, starting transfers between devices, swap(): return lax.ppermute(x, 'seq', [(i, i ^ mask) for i in range(n)])  15.3 us
    ppermute x15, waiting for transfers between devices, swap(): return lax.ppermute(x, 'seq', [(i, i ^ mask) for i in range(n)])  12.4 us
    all_to_all x1, waiting for transfers between devices, exchange(): return lax.all_to_all(x, 'seq', split_axis=0, concat_axis=0, tiled=True)  4.15 us
    all_to_all x1, starting transfers between devices, exchange(): return lax.all_to_all(x, 'seq', split_axis=0, concat_axis=0, tiled=True)  4.11 us
    pallas_call x1, Pallas kernels, temporal(): pl.pallas_call(functools.partial(temporal_kernel, length), in_specs=[SMEM...  3.81 us
    pallas_call x1, Pallas kernels, conv(): pl.pallas_call(functools.partial(conv_kernel, bands=bands), in_specs=[HBM...  3.37 us
    pallas_call x1, Pallas kernels, temporal_outer(): pl.pallas_call(functools.partial(temporal_outer_kernel, length), in_specs...  2.86 us
  transfers between devices with their start and end apart: 16, of which 10 were waited for; matrix products, arithmetic and copies ran while one was open for 1% of the time, Pallas kernels for 6%

profile of v5, /device:TPU:0, one launch (start us, length us, event | category | flops | bytes accessed | tf_op | source)
XLA Modules:
  0.0 71.7 jit_solution(16035874923974235099)
XLA Ops:
  0.7 3.4 %conv.1 = (bf16[16,2,64,128]{3,2,1,0:T(8,128)(2,1)S(1)}, bf16[2,33,64,256]{3,2,1,0:T(8,128)(2,1)S(1)}) custom-call(bf16[2,32,128,128]{3,2,1,0:T(8,128)(2,1)} %x_hbm.1, bf16[3,3,128,128]{3,2,1,0:T(8,128)(2,1)} %w_hbm.1), custom_call_target="tpu_custom_call" | custom-call | tf_op jit(solution)/shard_map/conv/pallas_call | solution.py:103
  4.0 21.6 %all_to_all.10 = bf16[16,128,128]{2,1,0:T(8,128)(2,1)S(1)} all-to-all(bf16[16,128,128]{2,1,0:T(8,128)(2,1)S(1)} %bitcast.36), channel_id=1, replica_groups=mesh['groups'=2,'seq'=16] {'seq'}, dimensions={0} | all-to-all | bytes 1048576 | tf_op jit(solution)/shard_map/all_to_all | solution.py:392
  25.7 3.8 %temporal.1 = (bf16[2048,128]{1,0:T(8,128)(2,1)}, bf16[2048,128]{1,0:T(8,128)(2,1)}, bf16[1,2048,128]{2,1,0:T(8,128)(2,1)}, bf16[2,2048,128]{2,1,0:T(8,128)(2,1)}) custom-call(s32[2]{0:T(128)S(1)} %copy-done.3, s32[2,3]{1,0:T(2,128)S(1)} %copy-done.2, bf16[2048,128]{1,0:T(8,128)(2,1)S(1)} %bitcast.33, bf16[2048,128]{1,0:T(8,128)(2,1)S(1)} %bitcast.37, ...), custom_call_target="tpu_custom_call" | custom-call | tf_op jit(solution)/shard_map/temporal/pallas_call | solution.py:213
  29.5 4.1 %all-to-all-start.1 = ((bf16[16,128,128]{2,1,0:T(8,128)(2,1)}), bf16[16,128,128]{2,1,0:T(8,128)(2,1)S(1)}, u32[]{:S(2)}, u32[]{:S(2)}) async-start(bf16[16,128,128]{2,1,0:T(8,128)(2,1)} %bitcast.44), calls=%async_computation.1 | async-start | bytes 1048576 | tf_op jit(solution)/shard_map/all_to_all | solution.py:392
  33.6 2.9 %temporal_outer.1 = (f32[384,128]{1,0:T(8,128)S(1)}, bf16[384,128]{1,0:T(8,128)(2,1)S(1)}) custom-call(s32[1]{0:T(128)} %bitcast.4.core_ref, s32[2]{0:T(128)S(1)} %copy-done.3, s32[2,3]{1,0:T(2,128)S(1)} %copy-done.2, bf16[2048,128]{1,0:T(8,128)(2,1)S(1)} %bitcast.34, bf16[1,2048,128]{2,1,0:T(8,128)(2,1)} %get-tuple-element.21.mid_hbm, ...), custom_call_target="tpu_custom_call" | custom-call | tf_op jit(solution)/shard_map/temporal_outer/pallas_call | solution.py:283
  36.5 0.5 collective-permute-start.1
  37.0 0.9 %collective-permute-done.1 = bf16[384,128]{1,0:T(8,128)(2,1)S(1)} collective-permute-done((bf16[384,128]{1,0:T(8,128)(2,1)S(1)}, bf16[384,128]{1,0:T(8,128)(2,1)S(1)}, u32[]{:S(2)}, u32[]{:S(2)}) %collective-permute-start.1) | collective-permute-done | bytes 98336 | tf_op jit(solution)/shard_map/ppermute | solution.py:337
  38.0 1.9 %collective-permute-start.2 = (bf16[192,128]{1,0:T(8,128)(2,1)S(1)}, bf16[192,128]{1,0:T(8,128)(2,1)S(1)}, u32[]{:S(2)}, u32[]{:S(2)}) collective-permute-start(bf16[192,128]{1,0:T(8,128)(2,1)S(1)} %fusion.4), channel_id=1, source_target_pairs={{0,2},{1,3},{2,0},{3,1},{4,6},{5,7},{6,4},{7,5},{8,10},{9,11},{10,... | collective-permute-start | bytes 147464 | tf_op jit(solution)/shard_map/ppermute | solution.py:337
  39.9 2.6 %collective-permute-done.2 = bf16[192,128]{1,0:T(8,128)(2,1)S(1)} collective-permute-done((bf16[192,128]{1,0:T(8,128)(2,1)S(1)}, bf16[192,128]{1,0:T(8,128)(2,1)S(1)}, u32[]{:S(2)}, u32[]{:S(2)}) %collective-permute-start.2) | collective-permute-done | bytes 49184 | tf_op jit(solution)/shard_map/ppermute | solution.py:337
  42.5 1.8 %collective-permute-start.3 = (bf16[192,128]{1,0:T(8,128)(2,1)S(1)}, bf16[192,128]{1,0:T(8,128)(2,1)S(1)}, u32[]{:S(2)}, u32[]{:S(2)}) collective-permute-start(bf16[192,128]{1,0:T(8,128)(2,1)S(1)} %fusion), channel_id=1, source_target_pairs={{0,4},{1,5},{2,6},{3,7},{4,0},{5,1},{6,2},{7,3},{8,12},{9,13},{10,... | collective-permute-start | bytes 147464 | tf_op jit(solution)/shard_map/ppermute | solution.py:337
  44.3 4.2 %all-to-all-done.1 = bf16[16,128,128]{2,1,0:T(8,128)(2,1)S(1)} async-done(((bf16[16,128,128]{2,1,0:T(8,128)(2,1)}), bf16[16,128,128]{2,1,0:T(8,128)(2,1)S(1)}, u32[]{:S(2)}, u32[]{:S(2)}) %all-to-all-start.1) | async-done | bytes 524320 | tf_op jit(solution)/shard_map/all_to_all | solution.py:392
  48.5 1.2 %spatial_outer.1 = (f32[576,128]{1,0:T(8,128)S(1)}, bf16[576,128]{1,0:T(8,128)(2,1)S(1)}) custom-call(s32[1]{0:T(128)} %bitcast.4.core_ref, bf16[2,33,64,256]{3,2,1,0:T(8,128)(2,1)S(1)} %get-tuple-element.17.planes, bf16[16,2,64,128]{3,2,1,0:T(8,128)(2,1)S(1)} %bitcast.35), custom_call_target="tpu_custom_call" | custom-call | tf_op jit(solution)/shard_map/spatial_outer/pallas_call | solution.py:325
  49.6 0.1 collective-permute-start
  49.8 1.3 %collective-permute-done = bf16[576,128]{1,0:T(8,128)(2,1)S(1)} collective-permute-done((bf16[576,128]{1,0:T(8,128)(2,1)S(1)}, bf16[576,128]{1,0:T(8,128)(2,1)S(1)}, u32[]{:S(2)}, u32[]{:S(2)}) %collective-permute-start) | collective-permute-done | bytes 147488 | tf_op jit(solution)/shard_map/ppermute | solution.py:337
  51.1 0.5 collective-permute-start.4
  51.6 1.6 %collective-permute-start.5 = (bf16[144,128]{1,0:T(8,128)(2,1)S(1)}, bf16[144,128]{1,0:T(8,128)(2,1)S(1)}, u32[]{:S(2)}, u32[]{:S(2)}) collective-permute-start(bf16[144,128]{1,0:T(8,128)(2,1)S(1)} %get-tuple-element.31), channel_id=1, source_target_pairs={{0,4},{1,5},{2,6},{3,7},{4,0},{5,1},{6,2},{7,3},{8,12},{9,13},{10,... | collective-permute-start | bytes 110600 | tf_op jit(solution)/shard_map/ppermute | solution.py:337
  53.2 1.5 %collective-permute-start.6 = (bf16[144,128]{1,0:T(8,128)(2,1)S(1)}, bf16[144,128]{1,0:T(8,128)(2,1)S(1)}, u32[]{:S(2)}, u32[]{:S(2)}) collective-permute-start(bf16[144,128]{1,0:T(8,128)(2,1)S(1)} %get-tuple-element.30), channel_id=1, source_target_pairs={{0,6},{1,7},{2,4},{3,5},{4,2},{5,3},{6,0},{7,1},{8,14},{9,15},{10,... | collective-permute-start | bytes 110600 | tf_op jit(solution)/shard_map/ppermute | solution.py:337
  54.7 1.9 %collective-permute-start.12 = (bf16[192,128]{1,0:T(8,128)(2,1)S(1)}, bf16[192,128]{1,0:T(8,128)(2,1)S(1)}, u32[]{:S(2)}, u32[]{:S(2)}) collective-permute-start(bf16[192,128]{1,0:T(8,128)(2,1)S(1)} %convert_add_fusion.2), channel_id=1, source_target_pairs={{0,8},{1,9},{2,10},{3,11},{4,12},{5,13},{6,14},{7,15},{8,0},{9,1},... | collective-permute-start | bytes 147464 | tf_op jit(solution)/shard_map/ppermute | solution.py:337
  56.6 1.9 %collective-permute-done.6 = bf16[144,128]{1,0:T(8,128)(2,1)S(1)} collective-permute-done((bf16[144,128]{1,0:T(8,128)(2,1)S(1)}, bf16[144,128]{1,0:T(8,128)(2,1)S(1)}, u32[]{:S(2)}, u32[]{:S(2)}) %collective-permute-start.6) | collective-permute-done | bytes 36896 | tf_op jit(solution)/shard_map/ppermute | solution.py:337
  58.5 1.6 %collective-permute-start.7 = (bf16[144,128]{1,0:T(8,128)(2,1)S(1)}, bf16[144,128]{1,0:T(8,128)(2,1)S(1)}, u32[]{:S(2)}, u32[]{:S(2)}) collective-permute-start(bf16[144,128]{1,0:T(8,128)(2,1)S(1)} %fusion.3), channel_id=1, source_target_pairs={{0,8},{1,9},{2,10},{3,11},{4,12},{5,13},{6,14},{7,15},{8,0},{9,1},... | collective-permute-start | bytes 110600 | tf_op jit(solution)/shard_map/ppermute | solution.py:337
  60.1 0.3 collective-permute-start.13
  60.4 3.2 %collective-permute-done.7 = bf16[144,128]{1,0:T(8,128)(2,1)S(1)} collective-permute-done((bf16[144,128]{1,0:T(8,128)(2,1)S(1)}, bf16[144,128]{1,0:T(8,128)(2,1)S(1)}, u32[]{:S(2)}, u32[]{:S(2)}) %collective-permute-start.7) | collective-permute-done | bytes 36896 | tf_op jit(solution)/shard_map/ppermute | solution.py:337
  63.6 1.3 %collective-permute-start.10 = (bf16[144,128]{1,0:T(8,128)(2,1)S(1)}, bf16[144,128]{1,0:T(8,128)(2,1)S(1)}, u32[]{:S(2)}, u32[]{:S(2)}) collective-permute-start(bf16[144,128]{1,0:T(8,128)(2,1)S(1)} %add_convert_fusion.1), channel_id=1, source_target_pairs={{0,6},{1,7},{2,4},{3,5},{4,2},{5,3},{6,0},{7,1},{8,14},{9,15},{10,... | collective-permute-start | bytes 110600 | tf_op jit(solution)/shard_map/ppermute | solution.py:337
  64.8 0.4 collective-permute-start.8
  65.3 1.8 %collective-permute-start.9 = (bf16[144,128]{1,0:T(8,128)(2,1)S(1)}, bf16[144,128]{1,0:T(8,128)(2,1)S(1)}, u32[]{:S(2)}, u32[]{:S(2)}) collective-permute-start(bf16[144,128]{1,0:T(8,128)(2,1)S(1)} %add_convert_fusion.1), channel_id=1, source_target_pairs={{0,4},{1,5},{2,6},{3,7},{4,0},{5,1},{6,2},{7,3},{8,12},{9,13},{10,... | collective-permute-start | bytes 110600 | tf_op jit(solution)/shard_map/ppermute | solution.py:337
  67.3 1.3 %collective-permute-done.10 = bf16[144,128]{1,0:T(8,128)(2,1)S(1)} collective-permute-done((bf16[144,128]{1,0:T(8,128)(2,1)S(1)}, bf16[144,128]{1,0:T(8,128)(2,1)S(1)}, u32[]{:S(2)}, u32[]{:S(2)}) %collective-permute-start.10) | collective-permute-done | bytes 36896 | tf_op jit(solution)/shard_map/ppermute | solution.py:337
  68.5 0.4 collective-permute-done.8
  68.9 0.3 collective-permute-done.9
  69.5 0.8 %convert.3 = f32[2,3,128,128]{3,2,1,0:T(8,128)} convert(bf16[2,3,128,128]{3,2,1,0:T(8,128)(2,1)S(1)} %bitcast.39) | non-fusion elementwise | flops 98304 | bytes 589824 | tf_op jit(solution)/shard_map/convert_element_type | solution.py:420
  70.2 0.5 collective-permute-done.11
  70.7 0.1 broadcast_select_fusion.1
  70.8 0.9 %convert.2 = f32[3,3,128,128]{3,2,1,0:T(8,128)} convert(bf16[3,3,128,128]{3,2,1,0:T(8,128)(2,1)S(1)} %bitcast.38) | non-fusion elementwise | flops 147456 | bytes 884736 | tf_op jit(solution)/shard_map/convert_element_type | solution.py:423
  (32 shorter events, 0.5 us)
Async XLA Ops:
  0.6 25.0 %copy-start = (bf16[32,64,128]{2,1,0:T(8,128)(2,1)S(1)}, bf16[32,64,128]{2,1,0:T(8,128)(2,1)}, u32[]{:S(2)}) copy-start(bf16[32,64,128]{2,1,0:T(8,128)(2,1)} %param.11) | copy-start | bytes 1572868
  0.6 25.0 %copy-start.2 = (s32[2,3]{1,0:T(2,128)S(1)}, s32[2,3]{1,0:T(2,128)}, u32[]{:S(2)}) copy-start(s32[2,3]{1,0:T(2,128)} %off_ref.3) | copy-start | bytes 76
  0.7 25.0 %copy-start.1 = (bf16[2,3,128,128]{3,2,1,0:T(8,128)(2,1)S(1)}, bf16[2,3,128,128]{3,2,1,0:T(8,128)(2,1)}, u32[]{:S(2)}) copy-start(bf16[2,3,128,128]{3,2,1,0:T(8,128)(2,1)} %w_ref.1) | copy-start | bytes 589828
  0.7 25.0 %copy-start.3 = (s32[2]{0:T(128)S(1)}, s32[2]{0:T(128)}, u32[]{:S(2)}) copy-start(s32[2]{0:T(128)} %dil_ref.3) | copy-start | bytes 28
  29.5 19.0 %all-to-all-start.1 = ((bf16[16,128,128]{2,1,0:T(8,128)(2,1)}), bf16[16,128,128]{2,1,0:T(8,128)(2,1)S(1)}, u32[]{:S(2)}, u32[]{:S(2)}) async-start(bf16[16,128,128]{2,1,0:T(8,128)(2,1)} %bitcast.44), calls=%async_computation.1 | async-start | bytes 1048576 | tf_op jit(solution)/shard_map/all_to_all | solution.py:392
  36.5 1.4 %collective-permute-start.1 = (bf16[384,128]{1,0:T(8,128)(2,1)S(1)}, bf16[384,128]{1,0:T(8,128)(2,1)S(1)}, u32[]{:S(2)}, u32[]{:S(2)}) collective-permute-start(bf16[384,128]{1,0:T(8,128)(2,1)S(1)} %get-tuple-element.24), channel_id=1, source_target_pairs={{0,1},{1,0},{2,3},{3,2},{4,5},{5,4},{6,7},{7,6},{8,9},{9,8},{10,11... | collective-permute-start | bytes 294920 | tf_op jit(solution)/shard_map/ppermute | solution.py:337
  38.0 4.5 %collective-permute-start.2 = (bf16[192,128]{1,0:T(8,128)(2,1)S(1)}, bf16[192,128]{1,0:T(8,128)(2,1)S(1)}, u32[]{:S(2)}, u32[]{:S(2)}) collective-permute-start(bf16[192,128]{1,0:T(8,128)(2,1)S(1)} %fusion.4), channel_id=1, source_target_pairs={{0,2},{1,3},{2,0},{3,1},{4,6},{5,7},{6,4},{7,5},{8,10},{9,11},{10,... | collective-permute-start | bytes 147464 | tf_op jit(solution)/shard_map/ppermute | solution.py:337
  42.5 7.2 %collective-permute-start.3 = (bf16[192,128]{1,0:T(8,128)(2,1)S(1)}, bf16[192,128]{1,0:T(8,128)(2,1)S(1)}, u32[]{:S(2)}, u32[]{:S(2)}) collective-permute-start(bf16[192,128]{1,0:T(8,128)(2,1)S(1)} %fusion), channel_id=1, source_target_pairs={{0,4},{1,5},{2,6},{3,7},{4,0},{5,1},{6,2},{7,3},{8,12},{9,13},{10,... | collective-permute-start | bytes 147464 | tf_op jit(solution)/shard_map/ppermute | solution.py:337
  49.6 1.4 %collective-permute-start = (bf16[576,128]{1,0:T(8,128)(2,1)S(1)}, bf16[576,128]{1,0:T(8,128)(2,1)S(1)}, u32[]{:S(2)}, u32[]{:S(2)}) collective-permute-start(bf16[576,128]{1,0:T(8,128)(2,1)S(1)} %get-tuple-element.20), channel_id=1, source_target_pairs={{0,1},{1,0},{2,3},{3,2},{4,5},{5,4},{6,7},{7,6},{8,9},{9,8},{10,11... | collective-permute-start | bytes 442376 | tf_op jit(solution)/shard_map/ppermute | solution.py:337
  51.1 5.4 %collective-permute-start.4 = (bf16[144,128]{1,0:T(8,128)(2,1)S(1)}, bf16[144,128]{1,0:T(8,128)(2,1)S(1)}, u32[]{:S(2)}, u32[]{:S(2)}) collective-permute-start(bf16[144,128]{1,0:T(8,128)(2,1)S(1)} %get-tuple-element.29), channel_id=1, source_target_pairs={{0,2},{1,3},{2,0},{3,1},{4,6},{5,7},{6,4},{7,5},{8,10},{9,11},{10,... | collective-permute-start | bytes 110600 | tf_op jit(solution)/shard_map/ppermute | solution.py:337
  51.6 4.9 %collective-permute-start.5 = (bf16[144,128]{1,0:T(8,128)(2,1)S(1)}, bf16[144,128]{1,0:T(8,128)(2,1)S(1)}, u32[]{:S(2)}, u32[]{:S(2)}) collective-permute-start(bf16[144,128]{1,0:T(8,128)(2,1)S(1)} %get-tuple-element.31), channel_id=1, source_target_pairs={{0,4},{1,5},{2,6},{3,7},{4,0},{5,1},{6,2},{7,3},{8,12},{9,13},{10,... | collective-permute-start | bytes 110600 | tf_op jit(solution)/shard_map/ppermute | solution.py:337
  53.2 5.3 %collective-permute-start.6 = (bf16[144,128]{1,0:T(8,128)(2,1)S(1)}, bf16[144,128]{1,0:T(8,128)(2,1)S(1)}, u32[]{:S(2)}, u32[]{:S(2)}) collective-permute-start(bf16[144,128]{1,0:T(8,128)(2,1)S(1)} %get-tuple-element.30), channel_id=1, source_target_pairs={{0,6},{1,7},{2,4},{3,5},{4,2},{5,3},{6,0},{7,1},{8,14},{9,15},{10,... | collective-permute-start | bytes 110600 | tf_op jit(solution)/shard_map/ppermute | solution.py:337
  54.7 5.4 %collective-permute-start.12 = (bf16[192,128]{1,0:T(8,128)(2,1)S(1)}, bf16[192,128]{1,0:T(8,128)(2,1)S(1)}, u32[]{:S(2)}, u32[]{:S(2)}) collective-permute-start(bf16[192,128]{1,0:T(8,128)(2,1)S(1)} %convert_add_fusion.2), channel_id=1, source_target_pairs={{0,8},{1,9},{2,10},{3,11},{4,12},{5,13},{6,14},{7,15},{8,0},{9,1},... | collective-permute-start | bytes 147464 | tf_op jit(solution)/shard_map/ppermute | solution.py:337
  58.5 5.0 %collective-permute-start.7 = (bf16[144,128]{1,0:T(8,128)(2,1)S(1)}, bf16[144,128]{1,0:T(8,128)(2,1)S(1)}, u32[]{:S(2)}, u32[]{:S(2)}) collective-permute-start(bf16[144,128]{1,0:T(8,128)(2,1)S(1)} %fusion.3), channel_id=1, source_target_pairs={{0,8},{1,9},{2,10},{3,11},{4,12},{5,13},{6,14},{7,15},{8,0},{9,1},... | collective-permute-start | bytes 110600 | tf_op jit(solution)/shard_map/ppermute | solution.py:337
  60.1 7.0 %collective-permute-start.13 = (bf16[192,128]{1,0:T(8,128)(2,1)S(1)}, bf16[192,128]{1,0:T(8,128)(2,1)S(1)}, u32[]{:S(2)}, u32[]{:S(2)}) collective-permute-start(bf16[192,128]{1,0:T(8,128)(2,1)S(1)} %add_convert_fusion), channel_id=1, source_target_pairs={{0,2},{1,3},{2,0},{3,1},{4,6},{5,7},{6,4},{7,5},{8,10},{9,11},{10,... | collective-permute-start | bytes 147464 | tf_op jit(solution)/shard_map/ppermute | solution.py:337
  63.6 4.9 %collective-permute-start.10 = (bf16[144,128]{1,0:T(8,128)(2,1)S(1)}, bf16[144,128]{1,0:T(8,128)(2,1)S(1)}, u32[]{:S(2)}, u32[]{:S(2)}) collective-permute-start(bf16[144,128]{1,0:T(8,128)(2,1)S(1)} %add_convert_fusion.1), channel_id=1, source_target_pairs={{0,6},{1,7},{2,4},{3,5},{4,2},{5,3},{6,0},{7,1},{8,14},{9,15},{10,... | collective-permute-start | bytes 110600 | tf_op jit(solution)/shard_map/ppermute | solution.py:337
  64.8 4.1 %collective-permute-start.8 = (bf16[144,128]{1,0:T(8,128)(2,1)S(1)}, bf16[144,128]{1,0:T(8,128)(2,1)S(1)}, u32[]{:S(2)}, u32[]{:S(2)}) collective-permute-start(bf16[144,128]{1,0:T(8,128)(2,1)S(1)} %add_convert_fusion.1), channel_id=1, source_target_pairs={{0,2},{1,3},{2,0},{3,1},{4,6},{5,7},{6,4},{7,5},{8,10},{9,11},{10,... | collective-permute-start | bytes 110600 | tf_op jit(solution)/shard_map/ppermute | solution.py:337
  65.3 4.0 %collective-permute-start.9 = (bf16[144,128]{1,0:T(8,128)(2,1)S(1)}, bf16[144,128]{1,0:T(8,128)(2,1)S(1)}, u32[]{:S(2)}, u32[]{:S(2)}) collective-permute-start(bf16[144,128]{1,0:T(8,128)(2,1)S(1)} %add_convert_fusion.1), channel_id=1, source_target_pairs={{0,4},{1,5},{2,6},{3,7},{4,0},{5,1},{6,2},{7,3},{8,12},{9,13},{10,... | collective-permute-start | bytes 110600 | tf_op jit(solution)/shard_map/ppermute | solution.py:337
  67.2 2.2 %collective-permute-start.14 = (bf16[384,128]{1,0:T(8,128)(2,1)S(1)}, bf16[384,128]{1,0:T(8,128)(2,1)S(1)}, u32[]{:S(2)}, u32[]{:S(2)}) collective-permute-start(bf16[384,128]{1,0:T(8,128)(2,1)S(1)} %pad_maximum_fusion.3), channel_id=1, source_target_pairs={{0,1},{1,0},{2,3},{3,2},{4,5},{5,4},{6,7},{7,6},{8,9},{9,8},{10,11... | collective-permute-start | bytes 294920 | tf_op jit(solution)/shard_map/ppermute | solution.py:337
  69.3 1.4 %collective-permute-start.11 = (bf16[576,128]{1,0:T(8,128)(2,1)S(1)}, bf16[576,128]{1,0:T(8,128)(2,1)S(1)}, u32[]{:S(2)}, u32[]{:S(2)}) collective-permute-start(bf16[576,128]{1,0:T(8,128)(2,1)S(1)} %pad_maximum_fusion.2), channel_id=1, source_target_pairs={{0,1},{1,0},{2,3},{3,2},{4,5},{5,4},{6,7},{7,6},{8,9},{9,8},{10,11... | collective-permute-start | bytes 442376 | tf_op jit(solution)/shard_map/ppermute | solution.py:337

commit v6 on v5

--- a/solution.py
+++ b/solution.py
@@ -39,7 +39,8 @@
     return pltpu.with_memory_space_constraint(x, pltpu.HBM)
 
 
-def conv_kernel(x_hbm, w_hbm, out_ref, planes, buf, weights, wide, sems, w_sem, *, bands):
+def conv_kernel(x_hbm, w_hbm, out_ref, planes, buf, weights, *rest, bands):
+    *wide, sems, w_sem = rest
     count, height, width, channels = x_hbm.shape
     out_cols = width // 2
     band = height // bands
@@ -61,45 +62,50 @@
     zero = jnp.zeros((out_cols, 2 * channels), BF16)
     chunk_pixels = out_ref.shape[2]
     owners = out_rows * out_cols // chunk_pixels
+
+    def split(frame, b):
+        copies[frame * bands + b].wait()
+        for row in range(b * band, (b + 1) * band):
+            slot = wide[row % len(wide)]
+            slot[...] = buf[frame, row].astype(F32)
+            even = slot[pl.ds(0, out_cols, stride=2), :]
+            odd = slot[pl.ds(1, out_cols, stride=2), :]
+            planes[frame, row + 1, :, :channels] = even.astype(BF16)
+            planes[frame, row + 1, :, channels:] = odd.astype(BF16)
+
+    def taps(lanes):
+        return jnp.concatenate(
+            [
+                jnp.concatenate(
+                    [planes[f, 2 * i + a, :, lanes] for f in range(count) for i in range(out_rows)], 0
+                )
+                for a in range(3)
+            ],
+            1,
+        )
+
     for frame in range(count):
         planes[frame, 0] = zero
+    for frame in range(count):
         for b in range(bands):
-            copies[frame * bands + b].wait()
-            for row in range(b * band, (b + 1) * band):
-                slot = row % wide.shape[0]
-                wide[slot] = buf[frame, row].astype(F32)
-                even = wide[slot, pl.ds(0, out_cols, stride=2), :]
-                odd = wide[slot, pl.ds(1, out_cols, stride=2), :]
-                planes[frame, row + 1, :, :channels] = even.astype(BF16)
-                planes[frame, row + 1, :, channels:] = odd.astype(BF16)
-        if frame == 0:
-            w_copy.wait()
-            w_even = jnp.concatenate([weights[a, 1] for a in range(3)], 0)
-            w_odd = jnp.concatenate(
-                [jnp.concatenate([weights[a, 2], weights[a, 0]], 1) for a in range(3)], 0
-            )
-
-        def taps(lanes):
-            return jnp.concatenate(
-                [
-                    jnp.concatenate(
-                        [planes[frame, 2 * i + a, :, lanes] for i in range(out_rows)], 0
-                    )
-                    for a in range(3)
-                ],
-                1,
-            )
-
-        odds = dot(taps(slice(channels, 2 * channels)), w_odd)
-        total = dot(taps(slice(0, channels)), w_even) + odds[:, :channels]
-        total = (total + moved_down(odds[:, channels:], out_cols)).astype(BF16)
-        out_ref[:, frame] = total.reshape(owners, chunk_pixels, channels)
+            split(frame, b)
+    w_copy.wait()
+    w_even = jnp.concatenate([weights[a, 1] for a in range(3)], 0)
+    w_odd = jnp.concatenate(
+        [jnp.concatenate([weights[a, 2], weights[a, 0]], 1) for a in range(3)], 0
+    )
+    odds = dot(taps(slice(channels, 2 * channels)), w_odd)
+    total = dot(taps(slice(0, channels)), w_even) + odds[:, :channels]
+    total = (total + moved_down(odds[:, channels:], out_cols)).astype(BF16)
+    total = total.reshape(count, owners, chunk_pixels, channels)
+    for frame in range(count):
+        out_ref[:, frame] = total[frame]
 
 
 def conv(frames, w_spatial, n):
     count, height, width, channels = frames.shape
     out_cols = width // 2
-    bands = 4
+    bands = 2
     return pl.pallas_call(
         functools.partial(conv_kernel, bands=bands),
         in_specs=[HBM, HBM],
@@ -111,7 +117,7 @@
         scratch_shapes=[
             pltpu.VMEM((count, height, width, channels), BF16),
             pltpu.VMEM(w_spatial.shape, BF16),
-            pltpu.VMEM((4, width, channels), F32),
+            *[pltpu.VMEM((width, channels), F32)] * 4,
             pltpu.SemaphoreType.DMA((count * bands,)),
             pltpu.SemaphoreType.DMA,
         ],

time: 72 us -> 71.6 us (level)
  no operation moved by 1% of the time
where the time goes in v6:
time: 71.6 us; the launch traced here: 71.3 us
  blocking collectives  21.6 us (30%)
  starting transfers between devices  19.4 us (27%)
  waiting for transfers between devices  16.6 us (23%)
  Pallas kernels  10.8 us (15%)
  other arithmetic  1.97 us (3%)
  between operations  0.87 us (1%)
    all_to_all x1, blocking collectives, exchange(): return lax.all_to_all(x, 'seq', split_axis=0, concat_axis=0, tiled=True)  21.6 us
    ppermute x15, starting transfers between devices, swap(): return lax.ppermute(x, 'seq', [(i, i ^ mask) for i in range(n)])  15.3 us
    ppermute x15, waiting for transfers between devices, swap(): return lax.ppermute(x, 'seq', [(i, i ^ mask) for i in range(n)])  12.4 us
    all_to_all x1, waiting for transfers between devices, exchange(): return lax.all_to_all(x, 'seq', split_axis=0, concat_axis=0, tiled=True)  4.16 us
    all_to_all x1, starting transfers between devices, exchange(): return lax.all_to_all(x, 'seq', split_axis=0, concat_axis=0, tiled=True)  4.11 us
    pallas_call x1, Pallas kernels, temporal(): pl.pallas_call(functools.partial(temporal_kernel, length), in_specs=[SMEM...  3.81 us
    pallas_call x1, Pallas kernels, conv(): pl.pallas_call(functools.partial(conv_kernel, bands=bands), in_specs=[HBM...  3 us
    pallas_call x1, Pallas kernels, temporal_outer(): pl.pallas_call(functools.partial(temporal_outer_kernel, length), in_specs...  2.88 us
  transfers between devices with their start and end apart: 16, of which 10 were waited for; matrix products, arithmetic and copies ran while one was open for 1% of the time, Pallas kernels for 6%

profile of v6, /device:TPU:0, one launch (start us, length us, event | category | flops | bytes accessed | tf_op | source)
XLA Modules:
  0.0 71.3 jit_solution(12900067051306806121)
XLA Ops:
  0.7 3.0 %conv.1 = (bf16[16,2,64,128]{3,2,1,0:T(8,128)(2,1)S(1)}, bf16[2,33,64,256]{3,2,1,0:T(8,128)(2,1)S(1)}) custom-call(bf16[2,32,128,128]{3,2,1,0:T(8,128)(2,1)} %x_hbm.1, bf16[3,3,128,128]{3,2,1,0:T(8,128)(2,1)} %w_hbm.1), custom_call_target="tpu_custom_call" | custom-call | tf_op jit(solution)/shard_map/conv/pallas_call | solution.py:109
  3.7 21.6 %all_to_all.10 = bf16[16,128,128]{2,1,0:T(8,128)(2,1)S(1)} all-to-all(bf16[16,128,128]{2,1,0:T(8,128)(2,1)S(1)} %bitcast.36), channel_id=1, replica_groups=mesh['groups'=2,'seq'=16] {'seq'}, dimensions={0} | all-to-all | bytes 1048576 | tf_op jit(solution)/shard_map/all_to_all | solution.py:398
  25.3 3.8 %temporal.1 = (bf16[2048,128]{1,0:T(8,128)(2,1)}, bf16[2048,128]{1,0:T(8,128)(2,1)}, bf16[1,2048,128]{2,1,0:T(8,128)(2,1)}, bf16[2,2048,128]{2,1,0:T(8,128)(2,1)}) custom-call(s32[2]{0:T(128)S(1)} %copy-done.3, s32[2,3]{1,0:T(2,128)S(1)} %copy-done.2, bf16[2048,128]{1,0:T(8,128)(2,1)S(1)} %bitcast.33, bf16[2048,128]{1,0:T(8,128)(2,1)S(1)} %bitcast.37, ...), custom_call_target="tpu_custom_call" | custom-call | tf_op jit(solution)/shard_map/temporal/pallas_call | solution.py:219
  29.1 4.1 %all-to-all-start.1 = ((bf16[16,128,128]{2,1,0:T(8,128)(2,1)}), bf16[16,128,128]{2,1,0:T(8,128)(2,1)S(1)}, u32[]{:S(2)}, u32[]{:S(2)}) async-start(bf16[16,128,128]{2,1,0:T(8,128)(2,1)} %bitcast.44), calls=%async_computation.1 | async-start | bytes 1048576 | tf_op jit(solution)/shard_map/all_to_all | solution.py:398
  33.3 2.9 %temporal_outer.1 = (f32[384,128]{1,0:T(8,128)S(1)}, bf16[384,128]{1,0:T(8,128)(2,1)S(1)}) custom-call(s32[1]{0:T(128)} %bitcast.4.core_ref, s32[2]{0:T(128)S(1)} %copy-done.3, s32[2,3]{1,0:T(2,128)S(1)} %copy-done.2, bf16[2048,128]{1,0:T(8,128)(2,1)S(1)} %bitcast.34, bf16[1,2048,128]{2,1,0:T(8,128)(2,1)} %get-tuple-element.21.mid_hbm, ...), custom_call_target="tpu_custom_call" | custom-call | tf_op jit(solution)/shard_map/temporal_outer/pallas_call | solution.py:289
  36.1 0.5 collective-permute-start.1
  36.6 0.9 %collective-permute-done.1 = bf16[384,128]{1,0:T(8,128)(2,1)S(1)} collective-permute-done((bf16[384,128]{1,0:T(8,128)(2,1)S(1)}, bf16[384,128]{1,0:T(8,128)(2,1)S(1)}, u32[]{:S(2)}, u32[]{:S(2)}) %collective-permute-start.1) | collective-permute-done | bytes 98336 | tf_op jit(solution)/shard_map/ppermute | solution.py:343
  37.6 1.9 %collective-permute-start.2 = (bf16[192,128]{1,0:T(8,128)(2,1)S(1)}, bf16[192,128]{1,0:T(8,128)(2,1)S(1)}, u32[]{:S(2)}, u32[]{:S(2)}) collective-permute-start(bf16[192,128]{1,0:T(8,128)(2,1)S(1)} %fusion.4), channel_id=1, source_target_pairs={{0,2},{1,3},{2,0},{3,1},{4,6},{5,7},{6,4},{7,5},{8,10},{9,11},{10,... | collective-permute-start | bytes 147464 | tf_op jit(solution)/shard_map/ppermute | solution.py:343
  39.5 2.6 %collective-permute-done.2 = bf16[192,128]{1,0:T(8,128)(2,1)S(1)} collective-permute-done((bf16[192,128]{1,0:T(8,128)(2,1)S(1)}, bf16[192,128]{1,0:T(8,128)(2,1)S(1)}, u32[]{:S(2)}, u32[]{:S(2)}) %collective-permute-start.2) | collective-permute-done | bytes 49184 | tf_op jit(solution)/shard_map/ppermute | solution.py:343
  42.1 1.8 %collective-permute-start.3 = (bf16[192,128]{1,0:T(8,128)(2,1)S(1)}, bf16[192,128]{1,0:T(8,128)(2,1)S(1)}, u32[]{:S(2)}, u32[]{:S(2)}) collective-permute-start(bf16[192,128]{1,0:T(8,128)(2,1)S(1)} %fusion), channel_id=1, source_target_pairs={{0,4},{1,5},{2,6},{3,7},{4,0},{5,1},{6,2},{7,3},{8,12},{9,13},{10,... | collective-permute-start | bytes 147464 | tf_op jit(solution)/shard_map/ppermute | solution.py:343
  43.9 4.2 %all-to-all-done.1 = bf16[16,128,128]{2,1,0:T(8,128)(2,1)S(1)} async-done(((bf16[16,128,128]{2,1,0:T(8,128)(2,1)}), bf16[16,128,128]{2,1,0:T(8,128)(2,1)S(1)}, u32[]{:S(2)}, u32[]{:S(2)}) %all-to-all-start.1) | async-done | bytes 524320 | tf_op jit(solution)/shard_map/all_to_all | solution.py:398
  48.1 1.2 %spatial_outer.1 = (f32[576,128]{1,0:T(8,128)S(1)}, bf16[576,128]{1,0:T(8,128)(2,1)S(1)}) custom-call(s32[1]{0:T(128)} %bitcast.4.core_ref, bf16[2,33,64,256]{3,2,1,0:T(8,128)(2,1)S(1)} %get-tuple-element.17.planes, bf16[16,2,64,128]{3,2,1,0:T(8,128)(2,1)S(1)} %bitcast.35), custom_call_target="tpu_custom_call" | custom-call | tf_op jit(solution)/shard_map/spatial_outer/pallas_call | solution.py:331
  49.4 1.3 %collective-permute-done = bf16[576,128]{1,0:T(8,128)(2,1)S(1)} collective-permute-done((bf16[576,128]{1,0:T(8,128)(2,1)S(1)}, bf16[576,128]{1,0:T(8,128)(2,1)S(1)}, u32[]{:S(2)}, u32[]{:S(2)}) %collective-permute-start) | collective-permute-done | bytes 147488 | tf_op jit(solution)/shard_map/ppermute | solution.py:343
  50.8 0.5 collective-permute-start.4
  51.3 1.5 %collective-permute-start.5 = (bf16[144,128]{1,0:T(8,128)(2,1)S(1)}, bf16[144,128]{1,0:T(8,128)(2,1)S(1)}, u32[]{:S(2)}, u32[]{:S(2)}) collective-permute-start(bf16[144,128]{1,0:T(8,128)(2,1)S(1)} %get-tuple-element.31), channel_id=1, source_target_pairs={{0,4},{1,5},{2,6},{3,7},{4,0},{5,1},{6,2},{7,3},{8,12},{9,13},{10,... | collective-permute-start | bytes 110600 | tf_op jit(solution)/shard_map/ppermute | solution.py:343
  52.8 1.5 %collective-permute-start.6 = (bf16[144,128]{1,0:T(8,128)(2,1)S(1)}, bf16[144,128]{1,0:T(8,128)(2,1)S(1)}, u32[]{:S(2)}, u32[]{:S(2)}) collective-permute-start(bf16[144,128]{1,0:T(8,128)(2,1)S(1)} %get-tuple-element.30), channel_id=1, source_target_pairs={{0,6},{1,7},{2,4},{3,5},{4,2},{5,3},{6,0},{7,1},{8,14},{9,15},{10,... | collective-permute-start | bytes 110600 | tf_op jit(solution)/shard_map/ppermute | solution.py:343
  54.3 1.9 %collective-permute-start.12 = (bf16[192,128]{1,0:T(8,128)(2,1)S(1)}, bf16[192,128]{1,0:T(8,128)(2,1)S(1)}, u32[]{:S(2)}, u32[]{:S(2)}) collective-permute-start(bf16[192,128]{1,0:T(8,128)(2,1)S(1)} %convert_add_fusion.2), channel_id=1, source_target_pairs={{0,8},{1,9},{2,10},{3,11},{4,12},{5,13},{6,14},{7,15},{8,0},{9,1},... | collective-permute-start | bytes 147464 | tf_op jit(solution)/shard_map/ppermute | solution.py:343
  56.2 1.9 %collective-permute-done.6 = bf16[144,128]{1,0:T(8,128)(2,1)S(1)} collective-permute-done((bf16[144,128]{1,0:T(8,128)(2,1)S(1)}, bf16[144,128]{1,0:T(8,128)(2,1)S(1)}, u32[]{:S(2)}, u32[]{:S(2)}) %collective-permute-start.6) | collective-permute-done | bytes 36896 | tf_op jit(solution)/shard_map/ppermute | solution.py:343
  58.2 1.6 %collective-permute-start.7 = (bf16[144,128]{1,0:T(8,128)(2,1)S(1)}, bf16[144,128]{1,0:T(8,128)(2,1)S(1)}, u32[]{:S(2)}, u32[]{:S(2)}) collective-permute-start(bf16[144,128]{1,0:T(8,128)(2,1)S(1)} %fusion.3), channel_id=1, source_target_pairs={{0,8},{1,9},{2,10},{3,11},{4,12},{5,13},{6,14},{7,15},{8,0},{9,1},... | collective-permute-start | bytes 110600 | tf_op jit(solution)/shard_map/ppermute | solution.py:343
  59.7 0.3 collective-permute-start.13
  60.0 3.2 %collective-permute-done.7 = bf16[144,128]{1,0:T(8,128)(2,1)S(1)} collective-permute-done((bf16[144,128]{1,0:T(8,128)(2,1)S(1)}, bf16[144,128]{1,0:T(8,128)(2,1)S(1)}, u32[]{:S(2)}, u32[]{:S(2)}) %collective-permute-start.7) | collective-permute-done | bytes 36896 | tf_op jit(solution)/shard_map/ppermute | solution.py:343
  63.2 1.3 %collective-permute-start.10 = (bf16[144,128]{1,0:T(8,128)(2,1)S(1)}, bf16[144,128]{1,0:T(8,128)(2,1)S(1)}, u32[]{:S(2)}, u32[]{:S(2)}) collective-permute-start(bf16[144,128]{1,0:T(8,128)(2,1)S(1)} %add_convert_fusion.1), channel_id=1, source_target_pairs={{0,6},{1,7},{2,4},{3,5},{4,2},{5,3},{6,0},{7,1},{8,14},{9,15},{10,... | collective-permute-start | bytes 110600 | tf_op jit(solution)/shard_map/ppermute | solution.py:343
  64.5 0.4 collective-permute-start.8
  64.9 1.8 %collective-permute-start.9 = (bf16[144,128]{1,0:T(8,128)(2,1)S(1)}, bf16[144,128]{1,0:T(8,128)(2,1)S(1)}, u32[]{:S(2)}, u32[]{:S(2)}) collective-permute-start(bf16[144,128]{1,0:T(8,128)(2,1)S(1)} %add_convert_fusion.1), channel_id=1, source_target_pairs={{0,4},{1,5},{2,6},{3,7},{4,0},{5,1},{6,2},{7,3},{8,12},{9,13},{10,... | collective-permute-start | bytes 110600 | tf_op jit(solution)/shard_map/ppermute | solution.py:343
  66.8 0.1 collective-permute-start.14
  66.9 1.3 %collective-permute-done.10 = bf16[144,128]{1,0:T(8,128)(2,1)S(1)} collective-permute-done((bf16[144,128]{1,0:T(8,128)(2,1)S(1)}, bf16[144,128]{1,0:T(8,128)(2,1)S(1)}, u32[]{:S(2)}, u32[]{:S(2)}) %collective-permute-start.10) | collective-permute-done | bytes 36896 | tf_op jit(solution)/shard_map/ppermute | solution.py:343
  68.1 0.4 collective-permute-done.8
  68.5 0.3 collective-permute-done.9
  69.1 0.8 %convert.3 = f32[2,3,128,128]{3,2,1,0:T(8,128)} convert(bf16[2,3,128,128]{3,2,1,0:T(8,128)(2,1)S(1)} %bitcast.39) | non-fusion elementwise | flops 98304 | bytes 589824 | tf_op jit(solution)/shard_map/convert_element_type | solution.py:426
  69.9 0.5 collective-permute-done.11
  70.4 0.1 broadcast_select_fusion.1
  70.5 0.9 %convert.2 = f32[3,3,128,128]{3,2,1,0:T(8,128)} convert(bf16[3,3,128,128]{3,2,1,0:T(8,128)(2,1)S(1)} %bitcast.38) | non-fusion elementwise | flops 147456 | bytes 884736 | tf_op jit(solution)/shard_map/convert_element_type | solution.py:429
  (32 shorter events, 0.5 us)
Async XLA Ops:
  0.6 24.7 %copy-start = (bf16[32,64,128]{2,1,0:T(8,128)(2,1)S(1)}, bf16[32,64,128]{2,1,0:T(8,128)(2,1)}, u32[]{:S(2)}) copy-start(bf16[32,64,128]{2,1,0:T(8,128)(2,1)} %param.11) | copy-start | bytes 1572868
  0.6 24.7 %copy-start.2 = (s32[2,3]{1,0:T(2,128)S(1)}, s32[2,3]{1,0:T(2,128)}, u32[]{:S(2)}) copy-start(s32[2,3]{1,0:T(2,128)} %off_ref.3) | copy-start | bytes 76
  0.7 24.7 %copy-start.1 = (bf16[2,3,128,128]{3,2,1,0:T(8,128)(2,1)S(1)}, bf16[2,3,128,128]{3,2,1,0:T(8,128)(2,1)}, u32[]{:S(2)}) copy-start(bf16[2,3,128,128]{3,2,1,0:T(8,128)(2,1)} %w_ref.1) | copy-start | bytes 589828
  0.7 24.7 %copy-start.3 = (s32[2]{0:T(128)S(1)}, s32[2]{0:T(128)}, u32[]{:S(2)}) copy-start(s32[2]{0:T(128)} %dil_ref.3) | copy-start | bytes 28
  29.1 19.0 %all-to-all-start.1 = ((bf16[16,128,128]{2,1,0:T(8,128)(2,1)}), bf16[16,128,128]{2,1,0:T(8,128)(2,1)S(1)}, u32[]{:S(2)}, u32[]{:S(2)}) async-start(bf16[16,128,128]{2,1,0:T(8,128)(2,1)} %bitcast.44), calls=%async_computation.1 | async-start | bytes 1048576 | tf_op jit(solution)/shard_map/all_to_all | solution.py:398
  36.1 1.4 %collective-permute-start.1 = (bf16[384,128]{1,0:T(8,128)(2,1)S(1)}, bf16[384,128]{1,0:T(8,128)(2,1)S(1)}, u32[]{:S(2)}, u32[]{:S(2)}) collective-permute-start(bf16[384,128]{1,0:T(8,128)(2,1)S(1)} %get-tuple-element.24), channel_id=1, source_target_pairs={{0,1},{1,0},{2,3},{3,2},{4,5},{5,4},{6,7},{7,6},{8,9},{9,8},{10,11... | collective-permute-start | bytes 294920 | tf_op jit(solution)/shard_map/ppermute | solution.py:343
  37.6 4.5 %collective-permute-start.2 = (bf16[192,128]{1,0:T(8,128)(2,1)S(1)}, bf16[192,128]{1,0:T(8,128)(2,1)S(1)}, u32[]{:S(2)}, u32[]{:S(2)}) collective-permute-start(bf16[192,128]{1,0:T(8,128)(2,1)S(1)} %fusion.4), channel_id=1, source_target_pairs={{0,2},{1,3},{2,0},{3,1},{4,6},{5,7},{6,4},{7,5},{8,10},{9,11},{10,... | collective-permute-start | bytes 147464 | tf_op jit(solution)/shard_map/ppermute | solution.py:343
  42.1 7.2 %collective-permute-start.3 = (bf16[192,128]{1,0:T(8,128)(2,1)S(1)}, bf16[192,128]{1,0:T(8,128)(2,1)S(1)}, u32[]{:S(2)}, u32[]{:S(2)}) collective-permute-start(bf16[192,128]{1,0:T(8,128)(2,1)S(1)} %fusion), channel_id=1, source_target_pairs={{0,4},{1,5},{2,6},{3,7},{4,0},{5,1},{6,2},{7,3},{8,12},{9,13},{10,... | collective-permute-start | bytes 147464 | tf_op jit(solution)/shard_map/ppermute | solution.py:343
  49.3 1.4 %collective-permute-start = (bf16[576,128]{1,0:T(8,128)(2,1)S(1)}, bf16[576,128]{1,0:T(8,128)(2,1)S(1)}, u32[]{:S(2)}, u32[]{:S(2)}) collective-permute-start(bf16[576,128]{1,0:T(8,128)(2,1)S(1)} %get-tuple-element.20), channel_id=1, source_target_pairs={{0,1},{1,0},{2,3},{3,2},{4,5},{5,4},{6,7},{7,6},{8,9},{9,8},{10,11... | collective-permute-start | bytes 442376 | tf_op jit(solution)/shard_map/ppermute | solution.py:343
  50.8 5.4 %collective-permute-start.4 = (bf16[144,128]{1,0:T(8,128)(2,1)S(1)}, bf16[144,128]{1,0:T(8,128)(2,1)S(1)}, u32[]{:S(2)}, u32[]{:S(2)}) collective-permute-start(bf16[144,128]{1,0:T(8,128)(2,1)S(1)} %get-tuple-element.29), channel_id=1, source_target_pairs={{0,2},{1,3},{2,0},{3,1},{4,6},{5,7},{6,4},{7,5},{8,10},{9,11},{10,... | collective-permute-start | bytes 110600 | tf_op jit(solution)/shard_map/ppermute | solution.py:343
  51.3 4.9 %collective-permute-start.5 = (bf16[144,128]{1,0:T(8,128)(2,1)S(1)}, bf16[144,128]{1,0:T(8,128)(2,1)S(1)}, u32[]{:S(2)}, u32[]{:S(2)}) collective-permute-start(bf16[144,128]{1,0:T(8,128)(2,1)S(1)} %get-tuple-element.31), channel_id=1, source_target_pairs={{0,4},{1,5},{2,6},{3,7},{4,0},{5,1},{6,2},{7,3},{8,12},{9,13},{10,... | collective-permute-start | bytes 110600 | tf_op jit(solution)/shard_map/ppermute | solution.py:343
  52.8 5.3 %collective-permute-start.6 = (bf16[144,128]{1,0:T(8,128)(2,1)S(1)}, bf16[144,128]{1,0:T(8,128)(2,1)S(1)}, u32[]{:S(2)}, u32[]{:S(2)}) collective-permute-start(bf16[144,128]{1,0:T(8,128)(2,1)S(1)} %get-tuple-element.30), channel_id=1, source_target_pairs={{0,6},{1,7},{2,4},{3,5},{4,2},{5,3},{6,0},{7,1},{8,14},{9,15},{10,... | collective-permute-start | bytes 110600 | tf_op jit(solution)/shard_map/ppermute | solution.py:343
  54.3 5.4 %collective-permute-start.12 = (bf16[192,128]{1,0:T(8,128)(2,1)S(1)}, bf16[192,128]{1,0:T(8,128)(2,1)S(1)}, u32[]{:S(2)}, u32[]{:S(2)}) collective-permute-start(bf16[192,128]{1,0:T(8,128)(2,1)S(1)} %convert_add_fusion.2), channel_id=1, source_target_pairs={{0,8},{1,9},{2,10},{3,11},{4,12},{5,13},{6,14},{7,15},{8,0},{9,1},... | collective-permute-start | bytes 147464 | tf_op jit(solution)/shard_map/ppermute | solution.py:343
  58.2 5.0 %collective-permute-start.7 = (bf16[144,128]{1,0:T(8,128)(2,1)S(1)}, bf16[144,128]{1,0:T(8,128)(2,1)S(1)}, u32[]{:S(2)}, u32[]{:S(2)}) collective-permute-start(bf16[144,128]{1,0:T(8,128)(2,1)S(1)} %fusion.3), channel_id=1, source_target_pairs={{0,8},{1,9},{2,10},{3,11},{4,12},{5,13},{6,14},{7,15},{8,0},{9,1},... | collective-permute-start | bytes 110600 | tf_op jit(solution)/shard_map/ppermute | solution.py:343
  59.7 7.0 %collective-permute-start.13 = (bf16[192,128]{1,0:T(8,128)(2,1)S(1)}, bf16[192,128]{1,0:T(8,128)(2,1)S(1)}, u32[]{:S(2)}, u32[]{:S(2)}) collective-permute-start(bf16[192,128]{1,0:T(8,128)(2,1)S(1)} %add_convert_fusion), channel_id=1, source_target_pairs={{0,2},{1,3},{2,0},{3,1},{4,6},{5,7},{6,4},{7,5},{8,10},{9,11},{10,... | collective-permute-start | bytes 147464 | tf_op jit(solution)/shard_map/ppermute | solution.py:343
  63.2 4.9 %collective-permute-start.10 = (bf16[144,128]{1,0:T(8,128)(2,1)S(1)}, bf16[144,128]{1,0:T(8,128)(2,1)S(1)}, u32[]{:S(2)}, u32[]{:S(2)}) collective-permute-start(bf16[144,128]{1,0:T(8,128)(2,1)S(1)} %add_convert_fusion.1), channel_id=1, source_target_pairs={{0,6},{1,7},{2,4},{3,5},{4,2},{5,3},{6,0},{7,1},{8,14},{9,15},{10,... | collective-permute-start | bytes 110600 | tf_op jit(solution)/shard_map/ppermute | solution.py:343
  64.5 4.1 %collective-permute-start.8 = (bf16[144,128]{1,0:T(8,128)(2,1)S(1)}, bf16[144,128]{1,0:T(8,128)(2,1)S(1)}, u32[]{:S(2)}, u32[]{:S(2)}) collective-permute-start(bf16[144,128]{1,0:T(8,128)(2,1)S(1)} %add_convert_fusion.1), channel_id=1, source_target_pairs={{0,2},{1,3},{2,0},{3,1},{4,6},{5,7},{6,4},{7,5},{8,10},{9,11},{10,... | collective-permute-start | bytes 110600 | tf_op jit(solution)/shard_map/ppermute | solution.py:343
  64.9 4.0 %collective-permute-start.9 = (bf16[144,128]{1,0:T(8,128)(2,1)S(1)}, bf16[144,128]{1,0:T(8,128)(2,1)S(1)}, u32[]{:S(2)}, u32[]{:S(2)}) collective-permute-start(bf16[144,128]{1,0:T(8,128)(2,1)S(1)} %add_convert_fusion.1), channel_id=1, source_target_pairs={{0,4},{1,5},{2,6},{3,7},{4,0},{5,1},{6,2},{7,3},{8,12},{9,13},{10,... | collective-permute-start | bytes 110600 | tf_op jit(solution)/shard_map/ppermute | solution.py:343
  66.8 2.2 %collective-permute-start.14 = (bf16[384,128]{1,0:T(8,128)(2,1)S(1)}, bf16[384,128]{1,0:T(8,128)(2,1)S(1)}, u32[]{:S(2)}, u32[]{:S(2)}) collective-permute-start(bf16[384,128]{1,0:T(8,128)(2,1)S(1)} %pad_maximum_fusion.3), channel_id=1, source_target_pairs={{0,1},{1,0},{2,3},{3,2},{4,5},{5,4},{6,7},{7,6},{8,9},{9,8},{10,11... | collective-permute-start | bytes 294920 | tf_op jit(solution)/shard_map/ppermute | solution.py:343
  68.9 1.4 %collective-permute-start.11 = (bf16[576,128]{1,0:T(8,128)(2,1)S(1)}, bf16[576,128]{1,0:T(8,128)(2,1)S(1)}, u32[]{:S(2)}, u32[]{:S(2)}) collective-permute-start(bf16[576,128]{1,0:T(8,128)(2,1)S(1)} %pad_maximum_fusion.2), channel_id=1, source_target_pairs={{0,1},{1,0},{2,3},{3,2},{4,5},{5,4},{6,7},{7,6},{8,9},{9,8},{10,11... | collective-permute-start | bytes 442376 | tf_op jit(solution)/shard_map/ppermute | solution.py:343

commit v7 on v6

--- a/solution.py
+++ b/solution.py
@@ -149,9 +149,11 @@
     length, dil_ref, off_ref, start_ref, cot_ref, w_ref, feat_hbm, back_hbm, mid_hbm, dz_hbm, *scratch
 ):
     layers, taps, channels = w_ref.shape[:3]
-    state, dz = scratch[:layers], scratch[layers : 2 * layers]
-    act, grad, feat, back, sems = scratch[2 * layers :]
     rows = start_ref.shape[0]
+    held_in = scratch[:layers]
+    act, grad, feat, back, sems = scratch[layers:]
+    state = [ref.at[pl.ds(rows, 2 * rows)] for ref in held_in]
+    dz = [ref.at[pl.ds(0, 2 * rows)] for ref in reversed(held_in)]
     pixels = rows // length
     size = min(1024, rows)
     starts = range(0, rows, size)
@@ -164,8 +166,7 @@
 
     blank = jnp.zeros((rows, channels), BF16)
     for layer in range(layers):
-        state[layer][pl.ds(0, rows), :] = blank
-        dz[layer][pl.ds(rows, rows), :] = blank
+        held_in[layer][pl.ds(rows, rows), :] = blank
     state[0][pl.ds(rows, rows), :] = start_ref[...]
     down = [w_ref[layer].reshape(taps * channels, channels) for layer in range(layers)]
     up = [
@@ -226,7 +227,7 @@
             pltpu.HBM((max(layers - 1, 1), rows, channels), BF16),
             pltpu.HBM((layers, rows, channels), BF16),
         ],
-        scratch_shapes=[pltpu.VMEM((2 * rows, channels), BF16)] * (2 * layers)
+        scratch_shapes=[pltpu.VMEM((3 * rows, channels), BF16)] * layers
         + [
             pltpu.VMEM((max(layers - 1, 1), rows, channels), F32),
             pltpu.VMEM((rows, channels), F32),
@@ -347,7 +348,7 @@
     me = lax.rem(lax.axis_index("seq") >> low, 1 << count)
     parts = values.reshape(1 << count, values.shape[0] >> count, -1)
     total = lax.dynamic_index_in_dim(parts, me, 0, keepdims=False)
-    for peer in range(1, 1 << count):
+    for peer in reversed(range(1, 1 << count)):
         theirs = lax.dynamic_index_in_dim(parts, me ^ peer, 0, keepdims=False)
         total = total + swap(theirs.astype(BF16), n, peer << low).astype(F32)
     return total

time: 71.6 us -> 71.3 us (level)
  waiting for transfers between devices: 16.6 us -> 15.8 us
    ppermute x15, waiting for transfers between devices: 12.4 us -> 11.6 us  [swap(): return lax.ppermute(x, 'seq', [(i, i ^ mask) for i in range(n)])]
  transfers between devices with their start and end apart: 16 -> 16, of which waited for: 10 -> 11; matrix products, arithmetic and copies ran while one was open for 1% -> 1% of each run, Pallas kernels for 6% -> 6%
where the time goes in v7:
time: 71.3 us; the launch traced here: 71 us
  blocking collectives  21.6 us (30%)
  starting transfers between devices  20 us (28%)
  waiting for transfers between devices  15.8 us (22%)
  Pallas kernels  10.7 us (15%)
  other arithmetic  1.97 us (3%)
  between operations  0.87 us (1%)
    all_to_all x1, blocking collectives, exchange(): return lax.all_to_all(x, 'seq', split_axis=0, concat_axis=0, tiled=True)  21.6 us
    ppermute x15, starting transfers between devices, swap(): return lax.ppermute(x, 'seq', [(i, i ^ mask) for i in range(n)])  15.9 us
    ppermute x15, waiting for transfers between devices, swap(): return lax.ppermute(x, 'seq', [(i, i ^ mask) for i in range(n)])  11.6 us
    all_to_all x1, waiting for transfers between devices, exchange(): return lax.all_to_all(x, 'seq', split_axis=0, concat_axis=0, tiled=True)  4.16 us
    all_to_all x1, starting transfers between devices, exchange(): return lax.all_to_all(x, 'seq', split_axis=0, concat_axis=0, tiled=True)  4.11 us
    pallas_call x1, Pallas kernels, temporal(): pl.pallas_call(functools.partial(temporal_kernel, length), in_specs=[SMEM...  3.68 us
    pallas_call x1, Pallas kernels, conv(): pl.pallas_call(functools.partial(conv_kernel, bands=bands), in_specs=[HBM...  3 us
    pallas_call x1, Pallas kernels, temporal_outer(): pl.pallas_call(functools.partial(temporal_outer_kernel, length), in_specs...  2.87 us
  transfers between devices with their start and end apart: 16, of which 11 were waited for; matrix products, arithmetic and copies ran while one was open for 1% of the time, Pallas kernels for 6%

profile of v7, /device:TPU:0, one launch (start us, length us, event | category | flops | bytes accessed | tf_op | source)
XLA Modules:
  0.0 71.0 jit_solution(7065903373713948736)
XLA Ops:
  0.7 3.0 %conv.1 = (bf16[16,2,64,128]{3,2,1,0:T(8,128)(2,1)S(1)}, bf16[2,33,64,256]{3,2,1,0:T(8,128)(2,1)S(1)}) custom-call(bf16[2,32,128,128]{3,2,1,0:T(8,128)(2,1)} %x_hbm.1, bf16[3,3,128,128]{3,2,1,0:T(8,128)(2,1)} %w_hbm.1), custom_call_target="tpu_custom_call" | custom-call | tf_op jit(solution)/shard_map/conv/pallas_call | solution.py:109
  3.7 21.6 %all_to_all.10 = bf16[16,128,128]{2,1,0:T(8,128)(2,1)S(1)} all-to-all(bf16[16,128,128]{2,1,0:T(8,128)(2,1)S(1)} %bitcast.36), channel_id=1, replica_groups=mesh['groups'=2,'seq'=16] {'seq'}, dimensions={0} | all-to-all | bytes 1048576 | tf_op jit(solution)/shard_map/all_to_all | solution.py:399
  25.3 3.7 %temporal.1 = (bf16[2048,128]{1,0:T(8,128)(2,1)}, bf16[2048,128]{1,0:T(8,128)(2,1)}, bf16[1,2048,128]{2,1,0:T(8,128)(2,1)}, bf16[2,2048,128]{2,1,0:T(8,128)(2,1)}) custom-call(s32[2]{0:T(128)S(1)} %copy-done.3, s32[2,3]{1,0:T(2,128)S(1)} %copy-done.2, bf16[2048,128]{1,0:T(8,128)(2,1)S(1)} %bitcast.33, bf16[2048,128]{1,0:T(8,128)(2,1)S(1)} %bitcast.37, ...), custom_call_target="tpu_custom_call" | custom-call | tf_op jit(solution)/shard_map/temporal/pallas_call | solution.py:220
  29.0 4.1 %all-to-all-start.1 = ((bf16[16,128,128]{2,1,0:T(8,128)(2,1)}), bf16[16,128,128]{2,1,0:T(8,128)(2,1)S(1)}, u32[]{:S(2)}, u32[]{:S(2)}) async-start(bf16[16,128,128]{2,1,0:T(8,128)(2,1)} %bitcast.44), calls=%async_computation.1 | async-start | bytes 1048576 | tf_op jit(solution)/shard_map/all_to_all | solution.py:399
  33.1 2.9 %temporal_outer.1 = (f32[384,128]{1,0:T(8,128)S(1)}, bf16[384,128]{1,0:T(8,128)(2,1)S(1)}) custom-call(s32[1]{0:T(128)} %bitcast.4.core_ref, s32[2]{0:T(128)S(1)} %copy-done.3, s32[2,3]{1,0:T(2,128)S(1)} %copy-done.2, bf16[2048,128]{1,0:T(8,128)(2,1)S(1)} %bitcast.34, bf16[1,2048,128]{2,1,0:T(8,128)(2,1)} %get-tuple-element.21.mid_hbm, ...), custom_call_target="tpu_custom_call" | custom-call | tf_op jit(solution)/shard_map/temporal_outer/pallas_call | solution.py:290
  36.0 0.5 collective-permute-start.1
  36.5 0.9 %collective-permute-done.1 = bf16[384,128]{1,0:T(8,128)(2,1)S(1)} collective-permute-done((bf16[384,128]{1,0:T(8,128)(2,1)S(1)}, bf16[384,128]{1,0:T(8,128)(2,1)S(1)}, u32[]{:S(2)}, u32[]{:S(2)}) %collective-permute-start.1) | collective-permute-done | bytes 98336 | tf_op jit(solution)/shard_map/ppermute | solution.py:344
  37.5 1.9 %collective-permute-start.2 = (bf16[192,128]{1,0:T(8,128)(2,1)S(1)}, bf16[192,128]{1,0:T(8,128)(2,1)S(1)}, u32[]{:S(2)}, u32[]{:S(2)}) collective-permute-start(bf16[192,128]{1,0:T(8,128)(2,1)S(1)} %fusion.4), channel_id=1, source_target_pairs={{0,2},{1,3},{2,0},{3,1},{4,6},{5,7},{6,4},{7,5},{8,10},{9,11},{10,... | collective-permute-start | bytes 147464 | tf_op jit(solution)/shard_map/ppermute | solution.py:344
  39.4 2.6 %collective-permute-done.2 = bf16[192,128]{1,0:T(8,128)(2,1)S(1)} collective-permute-done((bf16[192,128]{1,0:T(8,128)(2,1)S(1)}, bf16[192,128]{1,0:T(8,128)(2,1)S(1)}, u32[]{:S(2)}, u32[]{:S(2)}) %collective-permute-start.2) | collective-permute-done | bytes 49184 | tf_op jit(solution)/shard_map/ppermute | solution.py:344
  42.0 1.8 %collective-permute-start.3 = (bf16[192,128]{1,0:T(8,128)(2,1)S(1)}, bf16[192,128]{1,0:T(8,128)(2,1)S(1)}, u32[]{:S(2)}, u32[]{:S(2)}) collective-permute-start(bf16[192,128]{1,0:T(8,128)(2,1)S(1)} %fusion), channel_id=1, source_target_pairs={{0,4},{1,5},{2,6},{3,7},{4,0},{5,1},{6,2},{7,3},{8,12},{9,13},{10,... | collective-permute-start | bytes 147464 | tf_op jit(solution)/shard_map/ppermute | solution.py:344
  43.8 4.2 %all-to-all-done.1 = bf16[16,128,128]{2,1,0:T(8,128)(2,1)S(1)} async-done(((bf16[16,128,128]{2,1,0:T(8,128)(2,1)}), bf16[16,128,128]{2,1,0:T(8,128)(2,1)S(1)}, u32[]{:S(2)}, u32[]{:S(2)}) %all-to-all-start.1) | async-done | bytes 524320 | tf_op jit(solution)/shard_map/all_to_all | solution.py:399
  48.0 1.2 %spatial_outer.1 = (f32[576,128]{1,0:T(8,128)S(1)}, bf16[576,128]{1,0:T(8,128)(2,1)S(1)}) custom-call(s32[1]{0:T(128)} %bitcast.4.core_ref, bf16[2,33,64,256]{3,2,1,0:T(8,128)(2,1)S(1)} %get-tuple-element.17.planes, bf16[16,2,64,128]{3,2,1,0:T(8,128)(2,1)S(1)} %bitcast.35), custom_call_target="tpu_custom_call" | custom-call | tf_op jit(solution)/shard_map/spatial_outer/pallas_call | solution.py:332
  49.2 1.3 %collective-permute-done = bf16[576,128]{1,0:T(8,128)(2,1)S(1)} collective-permute-done((bf16[576,128]{1,0:T(8,128)(2,1)S(1)}, bf16[576,128]{1,0:T(8,128)(2,1)S(1)}, u32[]{:S(2)}, u32[]{:S(2)}) %collective-permute-start) | collective-permute-done | bytes 147488 | tf_op jit(solution)/shard_map/ppermute | solution.py:344
  50.6 1.5 %collective-permute-start.4 = (bf16[144,128]{1,0:T(8,128)(2,1)S(1)}, bf16[144,128]{1,0:T(8,128)(2,1)S(1)}, u32[]{:S(2)}, u32[]{:S(2)}) collective-permute-start(bf16[144,128]{1,0:T(8,128)(2,1)S(1)} %get-tuple-element.29), channel_id=1, source_target_pairs={{0,6},{1,7},{2,4},{3,5},{4,2},{5,3},{6,0},{7,1},{8,14},{9,15},{10,... | collective-permute-start | bytes 110600 | tf_op jit(solution)/shard_map/ppermute | solution.py:344
  52.1 0.5 collective-permute-start.5
  52.6 1.6 %collective-permute-start.6 = (bf16[144,128]{1,0:T(8,128)(2,1)S(1)}, bf16[144,128]{1,0:T(8,128)(2,1)S(1)}, u32[]{:S(2)}, u32[]{:S(2)}) collective-permute-start(bf16[144,128]{1,0:T(8,128)(2,1)S(1)} %get-tuple-element.30), channel_id=1, source_target_pairs={{0,2},{1,3},{2,0},{3,1},{4,6},{5,7},{6,4},{7,5},{8,10},{9,11},{10,... | collective-permute-start | bytes 110600 | tf_op jit(solution)/shard_map/ppermute | solution.py:344
  54.2 1.9 %collective-permute-start.12 = (bf16[192,128]{1,0:T(8,128)(2,1)S(1)}, bf16[192,128]{1,0:T(8,128)(2,1)S(1)}, u32[]{:S(2)}, u32[]{:S(2)}) collective-permute-start(bf16[192,128]{1,0:T(8,128)(2,1)S(1)} %convert_add_fusion.2), channel_id=1, source_target_pairs={{0,8},{1,9},{2,10},{3,11},{4,12},{5,13},{6,14},{7,15},{8,0},{9,1},... | collective-permute-start | bytes 147464 | tf_op jit(solution)/shard_map/ppermute | solution.py:344
  56.1 0.5 collective-permute-done.6
  56.6 1.5 %collective-permute-start.7 = (bf16[144,128]{1,0:T(8,128)(2,1)S(1)}, bf16[144,128]{1,0:T(8,128)(2,1)S(1)}, u32[]{:S(2)}, u32[]{:S(2)}) collective-permute-start(bf16[144,128]{1,0:T(8,128)(2,1)S(1)} %fusion.3), channel_id=1, source_target_pairs={{0,8},{1,9},{2,10},{3,11},{4,12},{5,13},{6,14},{7,15},{8,0},{9,1},... | collective-permute-start | bytes 110600 | tf_op jit(solution)/shard_map/ppermute | solution.py:344
  58.1 1.1 %collective-permute-done.12 = bf16[192,128]{1,0:T(8,128)(2,1)S(1)} collective-permute-done((bf16[192,128]{1,0:T(8,128)(2,1)S(1)}, bf16[192,128]{1,0:T(8,128)(2,1)S(1)}, u32[]{:S(2)}, u32[]{:S(2)}) %collective-permute-start.12) | collective-permute-done | bytes 49184 | tf_op jit(solution)/shard_map/ppermute | solution.py:344
  59.2 1.0 %collective-permute-start.13 = (bf16[192,128]{1,0:T(8,128)(2,1)S(1)}, bf16[192,128]{1,0:T(8,128)(2,1)S(1)}, u32[]{:S(2)}, u32[]{:S(2)}) collective-permute-start(bf16[192,128]{1,0:T(8,128)(2,1)S(1)} %add_convert_fusion), channel_id=1, source_target_pairs={{0,2},{1,3},{2,0},{3,1},{4,6},{5,7},{6,4},{7,5},{8,10},{9,11},{10,... | collective-permute-start | bytes 147464 | tf_op jit(solution)/shard_map/ppermute | solution.py:344
  60.2 1.3 %collective-permute-done.7 = bf16[144,128]{1,0:T(8,128)(2,1)S(1)} collective-permute-done((bf16[144,128]{1,0:T(8,128)(2,1)S(1)}, bf16[144,128]{1,0:T(8,128)(2,1)S(1)}, u32[]{:S(2)}, u32[]{:S(2)}) %collective-permute-start.7) | collective-permute-done | bytes 36896 | tf_op jit(solution)/shard_map/ppermute | solution.py:344
  61.5 2.1 %collective-permute-start.10 = (bf16[144,128]{1,0:T(8,128)(2,1)S(1)}, bf16[144,128]{1,0:T(8,128)(2,1)S(1)}, u32[]{:S(2)}, u32[]{:S(2)}) collective-permute-start(bf16[144,128]{1,0:T(8,128)(2,1)S(1)} %add_convert_fusion.1), channel_id=1, source_target_pairs={{0,6},{1,7},{2,4},{3,5},{4,2},{5,3},{6,0},{7,1},{8,14},{9,15},{10,... | collective-permute-start | bytes 110600 | tf_op jit(solution)/shard_map/ppermute | solution.py:344
  63.6 1.0 %collective-permute-start.8 = (bf16[144,128]{1,0:T(8,128)(2,1)S(1)}, bf16[144,128]{1,0:T(8,128)(2,1)S(1)}, u32[]{:S(2)}, u32[]{:S(2)}) collective-permute-start(bf16[144,128]{1,0:T(8,128)(2,1)S(1)} %add_convert_fusion.1), channel_id=1, source_target_pairs={{0,2},{1,3},{2,0},{3,1},{4,6},{5,7},{6,4},{7,5},{8,10},{9,11},{10,... | collective-permute-start | bytes 110600 | tf_op jit(solution)/shard_map/ppermute | solution.py:344
  64.6 0.5 collective-permute-start.9
  65.2 1.3 %collective-permute-done.10 = bf16[144,128]{1,0:T(8,128)(2,1)S(1)} collective-permute-done((bf16[144,128]{1,0:T(8,128)(2,1)S(1)}, bf16[144,128]{1,0:T(8,128)(2,1)S(1)}, u32[]{:S(2)}, u32[]{:S(2)}) %collective-permute-start.10) | collective-permute-done | bytes 36896 | tf_op jit(solution)/shard_map/ppermute | solution.py:344
  66.5 1.1 %collective-permute-done.8 = bf16[144,128]{1,0:T(8,128)(2,1)S(1)} collective-permute-done((bf16[144,128]{1,0:T(8,128)(2,1)S(1)}, bf16[144,128]{1,0:T(8,128)(2,1)S(1)}, u32[]{:S(2)}, u32[]{:S(2)}) %collective-permute-start.8) | collective-permute-done | bytes 36896 | tf_op jit(solution)/shard_map/ppermute | solution.py:344
  67.6 1.0 %collective-permute-done.9 = bf16[144,128]{1,0:T(8,128)(2,1)S(1)} collective-permute-done((bf16[144,128]{1,0:T(8,128)(2,1)S(1)}, bf16[144,128]{1,0:T(8,128)(2,1)S(1)}, u32[]{:S(2)}, u32[]{:S(2)}) %collective-permute-start.9) | collective-permute-done | bytes 36896 | tf_op jit(solution)/shard_map/ppermute | solution.py:344
  68.8 0.8 %convert.3 = f32[2,3,128,128]{3,2,1,0:T(8,128)} convert(bf16[2,3,128,128]{3,2,1,0:T(8,128)(2,1)S(1)} %bitcast.39) | non-fusion elementwise | flops 98304 | bytes 589824 | tf_op jit(solution)/shard_map/convert_element_type | solution.py:427
  69.6 0.5 collective-permute-done.11
  70.1 0.1 broadcast_select_fusion.1
  70.2 0.9 %convert.2 = f32[3,3,128,128]{3,2,1,0:T(8,128)} convert(bf16[3,3,128,128]{3,2,1,0:T(8,128)(2,1)S(1)} %bitcast.38) | non-fusion elementwise | flops 147456 | bytes 884736 | tf_op jit(solution)/shard_map/convert_element_type | solution.py:430
  (32 shorter events, 0.6 us)
Async XLA Ops:
  0.6 24.7 %copy-start = (bf16[32,64,128]{2,1,0:T(8,128)(2,1)S(1)}, bf16[32,64,128]{2,1,0:T(8,128)(2,1)}, u32[]{:S(2)}) copy-start(bf16[32,64,128]{2,1,0:T(8,128)(2,1)} %param.11) | copy-start | bytes 1572868
  0.6 24.7 %copy-start.2 = (s32[2,3]{1,0:T(2,128)S(1)}, s32[2,3]{1,0:T(2,128)}, u32[]{:S(2)}) copy-start(s32[2,3]{1,0:T(2,128)} %off_ref.3) | copy-start | bytes 76
  0.7 24.7 %copy-start.1 = (bf16[2,3,128,128]{3,2,1,0:T(8,128)(2,1)S(1)}, bf16[2,3,128,128]{3,2,1,0:T(8,128)(2,1)}, u32[]{:S(2)}) copy-start(bf16[2,3,128,128]{3,2,1,0:T(8,128)(2,1)} %w_ref.1) | copy-start | bytes 589828
  0.7 24.7 %copy-start.3 = (s32[2]{0:T(128)S(1)}, s32[2]{0:T(128)}, u32[]{:S(2)}) copy-start(s32[2]{0:T(128)} %dil_ref.3) | copy-start | bytes 28
  29.0 19.0 %all-to-all-start.1 = ((bf16[16,128,128]{2,1,0:T(8,128)(2,1)}), bf16[16,128,128]{2,1,0:T(8,128)(2,1)S(1)}, u32[]{:S(2)}, u32[]{:S(2)}) async-start(bf16[16,128,128]{2,1,0:T(8,128)(2,1)} %bitcast.44), calls=%async_computation.1 | async-start | bytes 1048576 | tf_op jit(solution)/shard_map/all_to_all | solution.py:399
  36.0 1.4 %collective-permute-start.1 = (bf16[384,128]{1,0:T(8,128)(2,1)S(1)}, bf16[384,128]{1,0:T(8,128)(2,1)S(1)}, u32[]{:S(2)}, u32[]{:S(2)}) collective-permute-start(bf16[384,128]{1,0:T(8,128)(2,1)S(1)} %get-tuple-element.24), channel_id=1, source_target_pairs={{0,1},{1,0},{2,3},{3,2},{4,5},{5,4},{6,7},{7,6},{8,9},{9,8},{10,11... | collective-permute-start | bytes 294920 | tf_op jit(solution)/shard_map/ppermute | solution.py:344
  37.5 4.5 %collective-permute-start.2 = (bf16[192,128]{1,0:T(8,128)(2,1)S(1)}, bf16[192,128]{1,0:T(8,128)(2,1)S(1)}, u32[]{:S(2)}, u32[]{:S(2)}) collective-permute-start(bf16[192,128]{1,0:T(8,128)(2,1)S(1)} %fusion.4), channel_id=1, source_target_pairs={{0,2},{1,3},{2,0},{3,1},{4,6},{5,7},{6,4},{7,5},{8,10},{9,11},{10,... | collective-permute-start | bytes 147464 | tf_op jit(solution)/shard_map/ppermute | solution.py:344
  42.0 7.2 %collective-permute-start.3 = (bf16[192,128]{1,0:T(8,128)(2,1)S(1)}, bf16[192,128]{1,0:T(8,128)(2,1)S(1)}, u32[]{:S(2)}, u32[]{:S(2)}) collective-permute-start(bf16[192,128]{1,0:T(8,128)(2,1)S(1)} %fusion), channel_id=1, source_target_pairs={{0,4},{1,5},{2,6},{3,7},{4,0},{5,1},{6,2},{7,3},{8,12},{9,13},{10,... | collective-permute-start | bytes 147464 | tf_op jit(solution)/shard_map/ppermute | solution.py:344
  49.1 1.4 %collective-permute-start = (bf16[576,128]{1,0:T(8,128)(2,1)S(1)}, bf16[576,128]{1,0:T(8,128)(2,1)S(1)}, u32[]{:S(2)}, u32[]{:S(2)}) collective-permute-start(bf16[576,128]{1,0:T(8,128)(2,1)S(1)} %get-tuple-element.20), channel_id=1, source_target_pairs={{0,1},{1,0},{2,3},{3,2},{4,5},{5,4},{6,7},{7,6},{8,9},{9,8},{10,11... | collective-permute-start | bytes 442376 | tf_op jit(solution)/shard_map/ppermute | solution.py:344
  50.6 5.4 %collective-permute-start.4 = (bf16[144,128]{1,0:T(8,128)(2,1)S(1)}, bf16[144,128]{1,0:T(8,128)(2,1)S(1)}, u32[]{:S(2)}, u32[]{:S(2)}) collective-permute-start(bf16[144,128]{1,0:T(8,128)(2,1)S(1)} %get-tuple-element.29), channel_id=1, source_target_pairs={{0,6},{1,7},{2,4},{3,5},{4,2},{5,3},{6,0},{7,1},{8,14},{9,15},{10,... | collective-permute-start | bytes 110600 | tf_op jit(solution)/shard_map/ppermute | solution.py:344
  52.1 4.0 %collective-permute-start.5 = (bf16[144,128]{1,0:T(8,128)(2,1)S(1)}, bf16[144,128]{1,0:T(8,128)(2,1)S(1)}, u32[]{:S(2)}, u32[]{:S(2)}) collective-permute-start(bf16[144,128]{1,0:T(8,128)(2,1)S(1)} %get-tuple-element.31), channel_id=1, source_target_pairs={{0,4},{1,5},{2,6},{3,7},{4,0},{5,1},{6,2},{7,3},{8,12},{9,13},{10,... | collective-permute-start | bytes 110600 | tf_op jit(solution)/shard_map/ppermute | solution.py:344
  52.6 4.0 %collective-permute-start.6 = (bf16[144,128]{1,0:T(8,128)(2,1)S(1)}, bf16[144,128]{1,0:T(8,128)(2,1)S(1)}, u32[]{:S(2)}, u32[]{:S(2)}) collective-permute-start(bf16[144,128]{1,0:T(8,128)(2,1)S(1)} %get-tuple-element.30), channel_id=1, source_target_pairs={{0,2},{1,3},{2,0},{3,1},{4,6},{5,7},{6,4},{7,5},{8,10},{9,11},{10,... | collective-permute-start | bytes 110600 | tf_op jit(solution)/shard_map/ppermute | solution.py:344
  54.2 5.0 %collective-permute-start.12 = (bf16[192,128]{1,0:T(8,128)(2,1)S(1)}, bf16[192,128]{1,0:T(8,128)(2,1)S(1)}, u32[]{:S(2)}, u32[]{:S(2)}) collective-permute-start(bf16[192,128]{1,0:T(8,128)(2,1)S(1)} %convert_add_fusion.2), channel_id=1, source_target_pairs={{0,8},{1,9},{2,10},{3,11},{4,12},{5,13},{6,14},{7,15},{8,0},{9,1},... | collective-permute-start | bytes 147464 | tf_op jit(solution)/shard_map/ppermute | solution.py:344
  56.6 4.9 %collective-permute-start.7 = (bf16[144,128]{1,0:T(8,128)(2,1)S(1)}, bf16[144,128]{1,0:T(8,128)(2,1)S(1)}, u32[]{:S(2)}, u32[]{:S(2)}) collective-permute-start(bf16[144,128]{1,0:T(8,128)(2,1)S(1)} %fusion.3), channel_id=1, source_target_pairs={{0,8},{1,9},{2,10},{3,11},{4,12},{5,13},{6,14},{7,15},{8,0},{9,1},... | collective-permute-start | bytes 110600 | tf_op jit(solution)/shard_map/ppermute | solution.py:344
  59.2 5.9 %collective-permute-start.13 = (bf16[192,128]{1,0:T(8,128)(2,1)S(1)}, bf16[192,128]{1,0:T(8,128)(2,1)S(1)}, u32[]{:S(2)}, u32[]{:S(2)}) collective-permute-start(bf16[192,128]{1,0:T(8,128)(2,1)S(1)} %add_convert_fusion), channel_id=1, source_target_pairs={{0,2},{1,3},{2,0},{3,1},{4,6},{5,7},{6,4},{7,5},{8,10},{9,11},{10,... | collective-permute-start | bytes 147464 | tf_op jit(solution)/shard_map/ppermute | solution.py:344
  61.5 4.9 %collective-permute-start.10 = (bf16[144,128]{1,0:T(8,128)(2,1)S(1)}, bf16[144,128]{1,0:T(8,128)(2,1)S(1)}, u32[]{:S(2)}, u32[]{:S(2)}) collective-permute-start(bf16[144,128]{1,0:T(8,128)(2,1)S(1)} %add_convert_fusion.1), channel_id=1, source_target_pairs={{0,6},{1,7},{2,4},{3,5},{4,2},{5,3},{6,0},{7,1},{8,14},{9,15},{10,... | collective-permute-start | bytes 110600 | tf_op jit(solution)/shard_map/ppermute | solution.py:344
  63.6 4.0 %collective-permute-start.8 = (bf16[144,128]{1,0:T(8,128)(2,1)S(1)}, bf16[144,128]{1,0:T(8,128)(2,1)S(1)}, u32[]{:S(2)}, u32[]{:S(2)}) collective-permute-start(bf16[144,128]{1,0:T(8,128)(2,1)S(1)} %add_convert_fusion.1), channel_id=1, source_target_pairs={{0,2},{1,3},{2,0},{3,1},{4,6},{5,7},{6,4},{7,5},{8,10},{9,11},{10,... | collective-permute-start | bytes 110600 | tf_op jit(solution)/shard_map/ppermute | solution.py:344
  64.6 4.0 %collective-permute-start.9 = (bf16[144,128]{1,0:T(8,128)(2,1)S(1)}, bf16[144,128]{1,0:T(8,128)(2,1)S(1)}, u32[]{:S(2)}, u32[]{:S(2)}) collective-permute-start(bf16[144,128]{1,0:T(8,128)(2,1)S(1)} %add_convert_fusion.1), channel_id=1, source_target_pairs={{0,4},{1,5},{2,6},{3,7},{4,0},{5,1},{6,2},{7,3},{8,12},{9,13},{10,... | collective-permute-start | bytes 110600 | tf_op jit(solution)/shard_map/ppermute | solution.py:344
  65.1 3.6 %collective-permute-start.14 = (bf16[384,128]{1,0:T(8,128)(2,1)S(1)}, bf16[384,128]{1,0:T(8,128)(2,1)S(1)}, u32[]{:S(2)}, u32[]{:S(2)}) collective-permute-start(bf16[384,128]{1,0:T(8,128)(2,1)S(1)} %pad_maximum_fusion.3), channel_id=1, source_target_pairs={{0,1},{1,0},{2,3},{3,2},{4,5},{5,4},{6,7},{7,6},{8,9},{9,8},{10,11... | collective-permute-start | bytes 294920 | tf_op jit(solution)/shard_map/ppermute | solution.py:344
  68.6 1.4 %collective-permute-start.11 = (bf16[576,128]{1,0:T(8,128)(2,1)S(1)}, bf16[576,128]{1,0:T(8,128)(2,1)S(1)}, u32[]{:S(2)}, u32[]{:S(2)}) collective-permute-start(bf16[576,128]{1,0:T(8,128)(2,1)S(1)} %pad_maximum_fusion.2), channel_id=1, source_target_pairs={{0,1},{1,0},{2,3},{3,2},{4,5},{5,4},{6,7},{7,6},{8,9},{9,8},{10,11... | collective-permute-start | bytes 442376 | tf_op jit(solution)/shard_map/ppermute | solution.py:344
